TPU v7x, 512 devices: a whole 4x8x8 slice. The times are simulated.
512 devices in a mesh: req: 128 (over z_hi, x, y), tp: 4 (over z_lo, core).
Axes of the slice: x: 4, y: 8, z: 8 (z_hi: 4, z_lo: 2; z = z_hi * 2 + z_lo), core: 2. Of those that a mesh axis runs over, the one named last changes fastest.
Arguments:
- queries: bfloat16 [2, 1024, 2304], P(None, 'req', 'tp'), may hold values from -10 to 10
- new_keys: bfloat16 [2, 1024, 2304], P(None, 'req', 'tp'), may hold values from -4 to 4
- new_values: bfloat16 [2, 1024, 2304], P(None, 'req', 'tp'), may hold values from -4 to 4
- cache_keys: bfloat16 [32768, 2304], P('req', 'tp'), may hold values from -10 to 10
- cache_values: bfloat16 [32768, 2304], P('req', 'tp'), may hold values from -4 to 4
- lengths: int32 [128, 16], P('req'), may hold values from 1 to 128, 256 in all within a row
- hidden: bfloat16 [2, 1024, 2304], P(None, 'req'), may hold values from -6 to 6
- gain: float32 [2304], replicated, may hold values from 0.5 to 1.5
- expert_ids: int32 [2, 1024, 2], P(None, 'req'), may hold values from 0 to 7, all different within a row; in each aligned block of 8 rows (0 to 7, 8 to 15, ..., all dimensions but the last counted through in order) at most 3 rows name the same one
- route_weights: float32 [2, 1024, 2], P(None, 'req'), may hold values from 0.2 to 1
- old_place: int32 [128], replicated, may hold values from 0 to 63, as said below
- new_place: int32 [128], replicated, may hold values from 0 to 63, as said below
- old_weights: bfloat16 [128, 2304, 1728], P('req', None, 'tp'), as said below
Outputs:
- context: bfloat16 [2, 1024, 2304], P(None, 'req', 'tp')
- layer_out: bfloat16 [2, 1024, 2304], P(None, 'req', 'tp')
- new_weights: bfloat16 [128, 2304, 1728], P('req', None, 'tp')
Inputs may be any that keep to these rules, and one draw needn't show every extreme that they name: `old_place`: every one of the 64 shards is held by at least one device; the others hold duplicates. `new_place`: every one of the 64 shards is held by at least one device; the others hold duplicates. `old_weights`: devices with equal old_place hold equal weights. `expert_ids`: in a batch, the 8 tokens of one device name one expert at most 3 times, and each token names distinct experts. `lengths`: each row sums to 256.
All inputs are finite; a program needn't handle non-finite values.
Results may differ from a plain program's by a relative error of at most 0.009.
Values may be sent and summed in bfloat16 or wider, within the bound.
A program may use at most 64 MiB of HBM per device.

v0:
```python
import jax
import jax.numpy as jnp
from jax import lax
from jax.sharding import PartitionSpec as P

HEAD_SIZE = 64
EXPERTS = 8
CAP = 3


def attend(queries, new_keys, new_values, cache_keys, cache_values, lengths):
    batches, tok_rows, width = queries.shape
    heads = width // HEAD_SIZE
    pool = cache_keys.shape[0]
    scale = HEAD_SIZE ** (-0.5)
    req_lengths = lengths.reshape(-1)
    starts = jnp.cumsum(req_lengths) - req_lengths
    position = jnp.arange(pool, dtype=jnp.int32)
    owned = (position[None, :] >= starts[:, None]) & (
        position[None, :] < (starts + req_lengths)[:, None]
    )
    query_rows = queries.reshape(batches * tok_rows, heads, HEAD_SIZE)
    own_keys = new_keys.reshape(batches * tok_rows, heads, HEAD_SIZE)
    own_values = new_values.reshape(batches * tok_rows, heads, HEAD_SIZE)
    pool_keys = cache_keys.reshape(pool, heads, HEAD_SIZE)
    pool_values = cache_values.reshape(pool, heads, HEAD_SIZE)
    scores = (
        jnp.einsum("qhd,phd->hqp", query_rows, pool_keys, preferred_element_type=jnp.float32)
        * scale
    )
    scores = jnp.where(owned[None], scores, -jnp.inf)
    own_score = (
        jnp.einsum("qhd,qhd->hq", query_rows, own_keys, preferred_element_type=jnp.float32) * scale
    )
    highest = jnp.maximum(jnp.max(scores, axis=-1), own_score)
    exp_pool = jnp.exp(scores - highest[..., None])
    exp_own = jnp.exp(own_score - highest)
    denom = jnp.sum(exp_pool, axis=-1) + exp_own
    summed = jnp.einsum(
        "hqp,phd->qhd",
        exp_pool.astype(jnp.bfloat16),
        pool_values,
        preferred_element_type=jnp.float32,
    )
    prob_own = lax.optimization_barrier(exp_own.astype(jnp.bfloat16)).astype(jnp.float32)
    summed = summed + prob_own.T[:, :, None] * own_values.astype(jnp.float32)
    context = (summed / denom.T[:, :, None]).astype(jnp.bfloat16)
    return context.reshape(batches, tok_rows, width)


def choose_holders(place, me_index, nreq, shard_count):
    devices = jnp.arange(nreq, dtype=jnp.int32)
    holder = place[None, :] == jnp.arange(shard_count, dtype=jnp.int32)[:, None]
    before = (place[:, None] == place[None, :]) & (devices[:, None] < devices[None, :])
    rank_in = jnp.sum(before.astype(jnp.int32), axis=0)
    count = jnp.sum(holder.astype(jnp.int32), axis=1)
    wanted = me_index % count
    match = holder & (rank_in[None, :] == wanted[:, None])
    return jnp.sum(jnp.where(match, devices[None, :], 0), axis=1)


def expert_block(hidden_rows, chosen, weights_now, place, shard_weights, gain):
    nreq = lax.axis_size("req")
    me_index = lax.axis_index("req")
    split_count = max(1, nreq // 16)
    shard_count = EXPERTS * split_count
    tok_rows, width = hidden_rows.shape
    hid_dev = shard_weights.shape[1] // 3
    resid = hidden_rows.astype(jnp.float32)
    normed = (
        resid * gain / jnp.sqrt(jnp.mean(resid * resid, axis=-1, keepdims=True) + 1e-05)
    ).astype(jnp.bfloat16)
    flat_ids = chosen.reshape(-1)
    assigns = flat_ids.shape[0]
    shard_dest = choose_holders(place, me_index, nreq, shard_count)
    shard_list = flat_ids[:, None] * split_count + jnp.arange(split_count, dtype=jnp.int32)[None, :]
    pick = shard_list[:, :, None] == jnp.arange(shard_count, dtype=jnp.int32)[None, None, :]
    dest = jnp.sum(jnp.where(pick, shard_dest[None, None, :], 0), axis=-1)
    assign_index = jnp.arange(assigns, dtype=jnp.int32)
    earlier = (flat_ids[:, None] == flat_ids[None, :]) & (
        assign_index[None, :] < assign_index[:, None]
    )
    rank_in = jnp.sum(earlier.astype(jnp.int32), axis=1)
    slot = dest * CAP + rank_in[:, None]
    hits = jnp.any(
        slot[None, :, :] == jnp.arange(nreq * CAP, dtype=jnp.int32)[:, None, None], axis=-1
    )
    repeated = jnp.repeat(normed, assigns // tok_rows, axis=0)
    outgoing = jnp.dot(hits.astype(jnp.bfloat16), repeated, preferred_element_type=jnp.float32)
    outgoing = outgoing.astype(jnp.bfloat16).reshape(nreq, CAP, width)
    received = lax.all_to_all(outgoing, "req", split_axis=0, concat_axis=0, tiled=True)
    sources, items, feat = received.shape
    flat_rows = received.reshape(sources * items, feat)
    gate_up = jnp.dot(
        flat_rows, shard_weights[:, : 2 * hid_dev], preferred_element_type=jnp.float32
    )
    act = (jax.nn.silu(gate_up[:, :hid_dev]) * gate_up[:, hid_dev:]).astype(jnp.bfloat16)
    part = lax.dot_general(
        act,
        shard_weights[:, 2 * hid_dev :],
        (((1,), (1,)), ((), ())),
        preferred_element_type=jnp.float32,
    )
    part = part.astype(jnp.bfloat16).reshape(sources, items, feat)
    returned = lax.all_to_all(part, "req", split_axis=0, concat_axis=0, tiled=True)
    returned = returned.reshape(nreq * CAP, width)
    picked = (
        returned[slot.reshape(-1)]
        .astype(jnp.float32)
        .reshape(tok_rows, assigns // tok_rows, split_count, width)
    )
    partial_sum = jnp.einsum("rksd,rk->rd", picked, weights_now)
    tp_width = width // lax.axis_size("tp")
    tp_start = lax.axis_index("tp") * tp_width
    resid_share = lax.dynamic_slice_in_dim(resid, tp_start, tp_width, 1)
    whole = lax.psum(partial_sum.astype(jnp.bfloat16), "tp").astype(jnp.float32)
    share = lax.dynamic_slice_in_dim(whole, tp_start, tp_width, 1)
    return (resid_share + share).astype(jnp.bfloat16)


def migrate(old_weights, old_place, new_place):
    nreq = lax.axis_size("req")
    shard_count = EXPERTS * max(1, nreq // 16)
    _, width, columns = old_weights.shape
    piece = width // nreq
    pieces = old_weights.reshape(nreq, piece, columns)
    spread = lax.all_to_all(pieces, "req", split_axis=0, concat_axis=0, tiled=True)
    devices = jnp.arange(nreq, dtype=jnp.int32)
    shard_ids = jnp.arange(shard_count, dtype=jnp.int32)
    first_old = jnp.min(
        jnp.where(old_place[None, :] == shard_ids[:, None], devices[None, :], nreq), axis=1
    )
    needed = jnp.sum(
        jnp.where(new_place[:, None] == shard_ids[None, :], first_old[None, :], 0), axis=1
    )
    sending = spread[needed]
    collected = lax.all_to_all(sending, "req", split_axis=0, concat_axis=0, tiled=True)
    return collected.reshape(1, width, columns)


def on_device(
    queries,
    new_keys,
    new_values,
    cache_keys,
    cache_values,
    lengths,
    hidden,
    gain,
    expert_ids,
    route_weights,
    old_place,
    new_place,
    old_weights,
):
    context = attend(queries, new_keys, new_values, cache_keys, cache_values, lengths)
    moved = migrate(old_weights, old_place, new_place)
    first_out = expert_block(
        hidden[0], expert_ids[0], route_weights[0], old_place, old_weights[0], gain
    )
    second_out = expert_block(hidden[1], expert_ids[1], route_weights[1], new_place, moved[0], gain)
    layer_out = jnp.stack([first_out, second_out])
    return (context, layer_out, moved)


def solution(mesh):
    in_specs = (
        P(None, "req", "tp"),
        P(None, "req", "tp"),
        P(None, "req", "tp"),
        P("req", "tp"),
        P("req", "tp"),
        P("req", None),
        P(None, "req", None),
        P(),
        P(None, "req", None),
        P(None, "req", None),
        P(),
        P(),
        P("req", None, "tp"),
    )
    out_specs = (P(None, "req", "tp"), P(None, "req", "tp"), P("req", None, "tp"))
    return jax.shard_map(
        on_device, mesh=mesh, in_specs=in_specs, out_specs=out_specs, check_vma=False
    )
```

profile of v0, /device:TPU:1, one launch (start us, length us, event | category | flops | bytes accessed | tf_op | source)
XLA Modules:
  0.0 525.8 jit_solution(8682452073270853563)
XLA Ops:
  17.2 20.8 %all-to-all-start.2 = ((bf16[128,3,2304]{2,1,0:T(4,128)(2,1)}), bf16[128,3,2304]{2,1,0:T(4,128)(2,1)S(1)}, u32[]{:S(2)}, u32[]{:S(2)}) async-start(bf16[128,3,2304]{2,1,0:T(4,128)(2,1)} %reshape.378), calls=%async_computation.2 | async-start | bytes 4718592 | tf_op jit(solution)/shard_map/all_to_all | solution.py:91
  38.1 4.1 copy.34
  42.1 5.2 reshape.380
  47.4 49.8 %all-to-all-done.2 = bf16[128,3,2304]{2,1,0:T(4,128)(2,1)S(1)} async-done(((bf16[128,3,2304]{2,1,0:T(4,128)(2,1)}), bf16[128,3,2304]{2,1,0:T(4,128)(2,1)S(1)}, u32[]{:S(2)}, u32[]{:S(2)}) %all-to-all-start.2) | async-done | bytes 1769504 | tf_op jit(solution)/shard_map/all_to_all | solution.py:91
  98.6 7.6 %all-to-all-start.3 = ((bf16[128,18,432]{2,1,0:T(8,128)(2,1)}), bf16[128,18,432]{2,1,0:T(8,128)(2,1)S(1)}, u32[]{:S(2)}, u32[]{:S(2)}) async-start(bf16[128,18,432]{2,1,0:T(8,128)(2,1)} %reshape.380), calls=%async_computation.3 | async-start | bytes 6291456 | tf_op jit(solution)/shard_map/all_to_all | solution.py:127
  111.0 5.4 %reshape.373 = bf16[128,3,2304]{2,1,0:T(4,128)(2,1)} reshape(bf16[384,2304]{1,0:T(8,128)(2,1)} %convolution_convert_fusion.2) | data formatting | bytes 3538944 | tf_op jit(solution)/shard_map/reshape | solution.py:90
  116.4 64.4 %all-to-all-done.3 = bf16[128,18,432]{2,1,0:T(8,128)(2,1)S(1)} async-done(((bf16[128,18,432]{2,1,0:T(8,128)(2,1)}), bf16[128,18,432]{2,1,0:T(8,128)(2,1)S(1)}, u32[]{:S(2)}, u32[]{:S(2)}) %all-to-all-start.3) | async-done | bytes 1990688 | tf_op jit(solution)/shard_map/all_to_all | solution.py:127
  180.8 8.4 %all-to-all-start = ((bf16[128,3,2304]{2,1,0:T(4,128)(2,1)}), bf16[128,3,2304]{2,1,0:T(4,128)(2,1)}, u32[]{:S(2)}, u32[]{:S(2)}) async-start(bf16[128,3,2304]{2,1,0:T(4,128)(2,1)} %reshape.373), calls=%async_computation | async-start | bytes 4718592 | tf_op jit(solution)/shard_map/all_to_all | solution.py:91
  189.3 2.4 gather_fusion.1
  191.7 53.7 %all-to-all-done = bf16[128,3,2304]{2,1,0:T(4,128)(2,1)} async-done(((bf16[128,3,2304]{2,1,0:T(4,128)(2,1)}), bf16[128,3,2304]{2,1,0:T(4,128)(2,1)}, u32[]{:S(2)}, u32[]{:S(2)}) %all-to-all-start) | async-done | bytes 1769504 | tf_op jit(solution)/shard_map/all_to_all | solution.py:91
  245.4 7.3 %all-to-all-start.4 = ((bf16[128,18,432]{2,1,0:T(8,128)(2,1)}), bf16[128,18,432]{2,1,0:T(8,128)(2,1)S(1)}, u32[]{:S(2)}, u32[]{:S(2)}) async-start(bf16[128,18,432]{2,1,0:T(8,128)(2,1)} %gather_fusion.1), calls=%async_computation.4 | async-start | bytes 6291456 | tf_op jit(solution)/shard_map/all_to_all | solution.py:137
  252.7 5.2 reshape.374
  257.9 2.7 fusion.2
  260.6 3.0 convolution_convert_fusion.1
  263.6 5.3 %reshape.375 = bf16[128,3,2304]{2,1,0:T(4,128)(2,1)} reshape(bf16[384,2304]{1,0:T(8,128)(2,1)} %convolution_convert_fusion.1) | data formatting | bytes 3538944 | tf_op jit(solution)/shard_map/reshape | solution.py:104
  269.0 55.9 %all-to-all-done.4 = bf16[128,18,432]{2,1,0:T(8,128)(2,1)S(1)} async-done(((bf16[128,18,432]{2,1,0:T(8,128)(2,1)}), bf16[128,18,432]{2,1,0:T(8,128)(2,1)S(1)}, u32[]{:S(2)}, u32[]{:S(2)}) %all-to-all-start.4) | async-done | bytes 1990688 | tf_op jit(solution)/shard_map/all_to_all | solution.py:137
  324.9 8.0 %all-to-all-start.1 = ((bf16[128,3,2304]{2,1,0:T(4,128)(2,1)}), bf16[128,3,2304]{2,1,0:T(4,128)(2,1)}, u32[]{:S(2)}, u32[]{:S(2)}) async-start(bf16[128,3,2304]{2,1,0:T(4,128)(2,1)} %reshape.375), calls=%async_computation.1 | async-start | bytes 4718592 | tf_op jit(solution)/shard_map/all_to_all | solution.py:105
  334.1 5.2 reshape.379
  339.2 2.6 squeeze_reshape.3
  341.8 3.1 fusion
  344.9 2.3 convolution_convert_fusion.3
  347.2 5.3 %reshape.381 = bf16[128,3,2304]{2,1,0:T(4,128)(2,1)} reshape(bf16[384,2304]{1,0:T(8,128)(2,1)} %convolution_convert_fusion.3) | data formatting | bytes 3538944 | tf_op jit(solution)/shard_map/reshape | solution.py:104
  352.6 33.7 %all-to-all-done.1 = bf16[128,3,2304]{2,1,0:T(4,128)(2,1)} async-done(((bf16[128,3,2304]{2,1,0:T(4,128)(2,1)}), bf16[128,3,2304]{2,1,0:T(4,128)(2,1)}, u32[]{:S(2)}, u32[]{:S(2)}) %all-to-all-start.1) | async-done | bytes 1769504 | tf_op jit(solution)/shard_map/all_to_all | solution.py:105
  386.3 7.9 %all-to-all-start.5 = ((bf16[128,3,2304]{2,1,0:T(4,128)(2,1)}), bf16[128,3,2304]{2,1,0:T(4,128)(2,1)}, u32[]{:S(2)}, u32[]{:S(2)}) async-start(bf16[128,3,2304]{2,1,0:T(4,128)(2,1)} %reshape.381), calls=%async_computation.5 | async-start | bytes 4718592 | tf_op jit(solution)/shard_map/all_to_all | solution.py:105
  408.1 5.2 reshape.376
  413.3 4.2 gather_fusion
  419.9 26.4 %all-to-all-done.5 = bf16[128,3,2304]{2,1,0:T(4,128)(2,1)} async-done(((bf16[128,3,2304]{2,1,0:T(4,128)(2,1)}), bf16[128,3,2304]{2,1,0:T(4,128)(2,1)}, u32[]{:S(2)}, u32[]{:S(2)}) %all-to-all-start.5) | async-done | bytes 1769504 | tf_op jit(solution)/shard_map/all_to_all | solution.py:105
  446.3 5.2 reshape.382
  451.5 4.1 gather_fusion.2
  460.2 2.6 reshape.383
  462.8 4.1 copy.35
  466.9 49.8 %all-reduce.3.cloned.1.call-done = (bf16[8,2304]{1,0:T(8,128)(2,1)}, bf16[8,2304]{1,0:T(8,128)(2,1)}) async-done(((bf16[8,2304]{1,0:T(8,128)(2,1)}, bf16[8,2304]{1,0:T(8,128)(2,1)}), (bf16[8,2304]{1,0:T(8,128)(2,1)}, bf16[8,2304]{1,0:T(8,128)(2,1)})) %all-reduce.3.cloned.1.call-update) | async-done | bytes 73744 | tf_op jit(solution)/shard_map/psum | solution.py:116
  (102 shorter events, 40.5 us)
Async XLA Ops:
  7.2 392.9 %copy-start = (bf16[256,576]{0,1:T(8,128)(2,1)S(1)}, bf16[256,576]{0,1:T(8,128)(2,1)}, u32[]{:S(2)}) copy-start(bf16[256,576]{0,1:T(8,128)(2,1)} %param.16) | copy-start | bytes 884740
  17.2 79.9 %all-to-all-start.2 = ((bf16[128,3,2304]{2,1,0:T(4,128)(2,1)}), bf16[128,3,2304]{2,1,0:T(4,128)(2,1)S(1)}, u32[]{:S(2)}, u32[]{:S(2)}) async-start(bf16[128,3,2304]{2,1,0:T(4,128)(2,1)} %reshape.378), calls=%async_computation.2 | async-start | bytes 4718592 | tf_op jit(solution)/shard_map/all_to_all | solution.py:91
  47.4 60.8 %copy-start.9 = (s32[128]{0:T(128)S(1)}, s32[128]{0:T(128)}, u32[]{:S(2)}) copy-start(s32[128]{0:T(128)} %param.23) | copy-start | bytes 1540
  97.2 1.4 copy-start.1
  98.6 82.2 %all-to-all-start.3 = ((bf16[128,18,432]{2,1,0:T(8,128)(2,1)}), bf16[128,18,432]{2,1,0:T(8,128)(2,1)S(1)}, u32[]{:S(2)}, u32[]{:S(2)}) async-start(bf16[128,18,432]{2,1,0:T(8,128)(2,1)} %reshape.380), calls=%async_computation.3 | async-start | bytes 6291456 | tf_op jit(solution)/shard_map/all_to_all | solution.py:127
  116.4 72.8 %copy-start.12 = (s32[128]{0:T(128)S(1)}, s32[128]{0:T(128)}, u32[]{:S(2)}) copy-start(s32[128]{0:T(128)} %param.24) | copy-start | bytes 1540
  180.8 64.7 %all-to-all-start = ((bf16[128,3,2304]{2,1,0:T(4,128)(2,1)}), bf16[128,3,2304]{2,1,0:T(4,128)(2,1)}, u32[]{:S(2)}, u32[]{:S(2)}) async-start(bf16[128,3,2304]{2,1,0:T(4,128)(2,1)} %reshape.373), calls=%async_computation | async-start | bytes 4718592 | tf_op jit(solution)/shard_map/all_to_all | solution.py:91
  245.4 79.4 %all-to-all-start.4 = ((bf16[128,18,432]{2,1,0:T(8,128)(2,1)}), bf16[128,18,432]{2,1,0:T(8,128)(2,1)S(1)}, u32[]{:S(2)}, u32[]{:S(2)}) async-start(bf16[128,18,432]{2,1,0:T(8,128)(2,1)} %gather_fusion.1), calls=%async_computation.4 | async-start | bytes 6291456 | tf_op jit(solution)/shard_map/all_to_all | solution.py:137
  324.9 61.4 %all-to-all-start.1 = ((bf16[128,3,2304]{2,1,0:T(4,128)(2,1)}), bf16[128,3,2304]{2,1,0:T(4,128)(2,1)}, u32[]{:S(2)}, u32[]{:S(2)}) async-start(bf16[128,3,2304]{2,1,0:T(4,128)(2,1)} %reshape.375), calls=%async_computation.1 | async-start | bytes 4718592 | tf_op jit(solution)/shard_map/all_to_all | solution.py:105
  341.8 3.1 copy-start.2
  352.6 41.9 %copy-start.11 = (f32[2,8,2]{1,2,0:T(2,128)S(1)}, f32[2,8,2]{1,2,0:T(2,128)}, u32[]{:S(2)}) copy-start(f32[2,8,2]{1,2,0:T(2,128)} %param.22) | copy-start | bytes 388
  352.6 43.3 %copy-start.10 = (s32[1,16]{1,0:T(1,128)S(1)}, s32[1,16]{1,0:T(1,128)}, u32[]{:S(2)}) copy-start(s32[1,16]{1,0:T(1,128)} %param.18) | copy-start | bytes 196
  352.6 43.5 %copy-start.4 = (bf16[2,8,576]{2,1,0:T(8,128)(2,1)S(1)}, bf16[2,8,576]{2,1,0:T(8,128)(2,1)}, u32[]{:S(2)}) copy-start(bf16[2,8,576]{2,1,0:T(8,128)(2,1)} %param.13) | copy-start | bytes 55300
  352.6 54.9 %copy-start.3 = (bf16[2,8,2304]{2,1,0:T(8,128)(2,1)S(1)}, bf16[2,8,2304]{2,1,0:T(8,128)(2,1)}, u32[]{:S(2)}) copy-start(bf16[2,8,2304]{2,1,0:T(8,128)(2,1)} %param.19) | copy-start | bytes 221188
  386.3 60.0 %all-to-all-start.5 = ((bf16[128,3,2304]{2,1,0:T(4,128)(2,1)}), bf16[128,3,2304]{2,1,0:T(4,128)(2,1)}, u32[]{:S(2)}, u32[]{:S(2)}) async-start(bf16[128,3,2304]{2,1,0:T(4,128)(2,1)} %reshape.381), calls=%async_computation.5 | async-start | bytes 4718592 | tf_op jit(solution)/shard_map/all_to_all | solution.py:105
  394.2 122.5 %all-reduce.3.cloned.1.call-start = ((), (), s32[]{:S(2)}) async-start(), calls=%async_computation.6 | async-start | bytes 147456 | tf_op jit(solution)/shard_map/psum | solution.py:116
  413.3 5.7 %copy-start.8 = (bf16[8,2,1]{1,2,0:T(2,128)(2,1)S(1)}, bf16[8,2,1]{1,2,0:T(2,128)(2,1)}, u32[]{:S(2)}) copy-start(bf16[8,2,1]{1,2,0:T(2,128)(2,1)} %copy.43) | copy-start | bytes 100
  451.5 5.7 %copy-start.7 = (bf16[8,2,1]{1,2,0:T(2,128)(2,1)S(1)}, bf16[8,2,1]{1,2,0:T(2,128)(2,1)}, u32[]{:S(2)}) copy-start(bf16[8,2,1]{1,2,0:T(2,128)(2,1)} %copy.45) | copy-start | bytes 100
  451.5 6.5 %copy-start.5 = (f32[16,9]{0,1:T(8,128)S(1)}, f32[16,9]{0,1:T(8,128)}, u32[]{:S(2)}) copy-start(f32[16,9]{0,1:T(8,128)} %convert_bitcast_fusion) | copy-start | bytes 1732
  451.5 6.6 %copy-start.6 = (f32[16,9]{0,1:T(8,128)S(1)}, f32[16,9]{0,1:T(8,128)}, u32[]{:S(2)}) copy-start(f32[16,9]{0,1:T(8,128)} %fusion.40) | copy-start | bytes 1732
Sparse Core Ops, SparseCore 0:
  458.2 58.4 all-reduce.2
where the time goes:
time: 528 us; the launch traced here: 526 us
  waiting for transfers between devices  334 us (63%)
  local copies, waits for them, and re-layouts  81 us (15%)
  starting transfers between devices  60.2 us (11%)
  other arithmetic  19.5 us (4%)
  matrix products  17 us (3%)
  between operations  14.3 us (3%)
    all_to_all x2, waiting for transfers between devices, expert_block(): lax.all_to_all(outgoing, 'req', split_axis=0, concat_axis=0, tiled=True)  104 us
    all_to_all x1, waiting for transfers between devices, migrate(): lax.all_to_all(pieces, 'req', split_axis=0, concat_axis=0, tiled=True)  64.4 us
    all_to_all x2, waiting for transfers between devices, expert_block(): lax.all_to_all(part, 'req', split_axis=0, concat_axis=0, tiled=True)  60.1 us
    all_to_all x1, waiting for transfers between devices, migrate(): lax.all_to_all(sending, 'req', split_axis=0, concat_axis=0, tiled=True)  55.9 us
    psum x1, waiting for transfers between devices, expert_block(): whole = lax.psum(partial_sum.astype(jnp.bfloat16), 'tp').astype(jnp.float32)  49.8 us
    all_to_all x2, starting transfers between devices, expert_block(): lax.all_to_all(outgoing, 'req', split_axis=0, concat_axis=0, tiled=True)  29.2 us
    all_to_all x2, starting transfers between devices, expert_block(): lax.all_to_all(part, 'req', split_axis=0, concat_axis=0, tiled=True)  15.9 us
    reshape x2, local copies, waits for them, and re-layouts, expert_block(): part = part.astype(jnp.bfloat16).reshape(sources, items, feat)  10.7 us
  transfers between devices with their start and end apart: 7, of which 7 were waited for; matrix products, arithmetic and copies ran while one was open for 18% of the time, Pallas kernels for 0%

commit v1 on v0

--- a/solution.py
+++ b/solution.py
@@ -48,74 +48,53 @@
     return context.reshape(batches, tok_rows, width)
 
 
-def choose_holders(place, me_index, nreq, shard_count):
-    devices = jnp.arange(nreq, dtype=jnp.int32)
-    holder = place[None, :] == jnp.arange(shard_count, dtype=jnp.int32)[:, None]
-    before = (place[:, None] == place[None, :]) & (devices[:, None] < devices[None, :])
-    rank_in = jnp.sum(before.astype(jnp.int32), axis=0)
-    count = jnp.sum(holder.astype(jnp.int32), axis=1)
-    wanted = me_index % count
-    match = holder & (rank_in[None, :] == wanted[:, None])
-    return jnp.sum(jnp.where(match, devices[None, :], 0), axis=1)
-
-
-def expert_block(hidden_rows, chosen, weights_now, place, shard_weights, gain):
+def expert_all(hidden, chosen, route_weights, place, shard_weights, gain):
     nreq = lax.axis_size("req")
+    ntp = lax.axis_size("tp")
     me_index = lax.axis_index("req")
     split_count = max(1, nreq // 16)
     shard_count = EXPERTS * split_count
-    tok_rows, width = hidden_rows.shape
+    batches, tok_rows, width = hidden.shape
     hid_dev = shard_weights.shape[1] // 3
-    resid = hidden_rows.astype(jnp.float32)
+    resid = hidden.astype(jnp.float32)
     normed = (
         resid * gain / jnp.sqrt(jnp.mean(resid * resid, axis=-1, keepdims=True) + 1e-05)
     ).astype(jnp.bfloat16)
-    flat_ids = chosen.reshape(-1)
-    assigns = flat_ids.shape[0]
-    shard_dest = choose_holders(place, me_index, nreq, shard_count)
-    shard_list = flat_ids[:, None] * split_count + jnp.arange(split_count, dtype=jnp.int32)[None, :]
-    pick = shard_list[:, :, None] == jnp.arange(shard_count, dtype=jnp.int32)[None, None, :]
-    dest = jnp.sum(jnp.where(pick, shard_dest[None, None, :], 0), axis=-1)
-    assign_index = jnp.arange(assigns, dtype=jnp.int32)
-    earlier = (flat_ids[:, None] == flat_ids[None, :]) & (
-        assign_index[None, :] < assign_index[:, None]
+    experts = jnp.arange(EXPERTS, dtype=jnp.int32)
+    coef = jnp.sum(
+        jnp.where(chosen[..., None] == experts, route_weights[..., None], 0.0), axis=-2
     )
-    rank_in = jnp.sum(earlier.astype(jnp.int32), axis=1)
-    slot = dest * CAP + rank_in[:, None]
-    hits = jnp.any(
-        slot[None, :, :] == jnp.arange(nreq * CAP, dtype=jnp.int32)[:, None, None], axis=-1
+    all_normed = lax.all_gather(normed, "req", axis=0, tiled=False)
+    all_coef = lax.all_gather(coef, "req", axis=0, tiled=False)
+    devices = jnp.arange(nreq, dtype=jnp.int32)
+    shard_ids = jnp.arange(shard_count, dtype=jnp.int32)
+    first_old = jnp.min(
+        jnp.where(place[None, :] == shard_ids[:, None], devices[None, :], nreq), axis=1
     )
-    repeated = jnp.repeat(normed, assigns // tok_rows, axis=0)
-    outgoing = jnp.dot(hits.astype(jnp.bfloat16), repeated, preferred_element_type=jnp.float32)
-    outgoing = outgoing.astype(jnp.bfloat16).reshape(nreq, CAP, width)
-    received = lax.all_to_all(outgoing, "req", split_axis=0, concat_axis=0, tiled=True)
-    sources, items, feat = received.shape
-    flat_rows = received.reshape(sources * items, feat)
-    gate_up = jnp.dot(
-        flat_rows, shard_weights[:, : 2 * hid_dev], preferred_element_type=jnp.float32
-    )
+    my_shard = place[me_index]
+    my_expert = my_shard // split_count
+    designated = first_old[my_shard] == me_index
+    column = jnp.sum(jnp.where(experts == my_expert, all_coef, 0.0), axis=-1)
+    column = jnp.where(designated, column, 0.0).reshape(-1)
+    rows = all_normed.reshape(-1, width)
+    gate_up = jnp.dot(rows, shard_weights[:, : 2 * hid_dev], preferred_element_type=jnp.float32)
     act = (jax.nn.silu(gate_up[:, :hid_dev]) * gate_up[:, hid_dev:]).astype(jnp.bfloat16)
     part = lax.dot_general(
         act,
         shard_weights[:, 2 * hid_dev :],
         (((1,), (1,)), ((), ())),
         preferred_element_type=jnp.float32,
-    )
-    part = part.astype(jnp.bfloat16).reshape(sources, items, feat)
-    returned = lax.all_to_all(part, "req", split_axis=0, concat_axis=0, tiled=True)
-    returned = returned.reshape(nreq * CAP, width)
-    picked = (
-        returned[slot.reshape(-1)]
-        .astype(jnp.float32)
-        .reshape(tok_rows, assigns // tok_rows, split_count, width)
-    )
-    partial_sum = jnp.einsum("rksd,rk->rd", picked, weights_now)
-    tp_width = width // lax.axis_size("tp")
+    ).astype(jnp.bfloat16)
+    weighted = (part.astype(jnp.float32) * column[:, None]).astype(jnp.bfloat16)
+    weighted = weighted.reshape(nreq, batches * tok_rows, width)
+    mine = lax.psum_scatter(weighted, "req", scatter_dimension=0, tiled=True)
+    mine = mine.reshape(batches * tok_rows, ntp, width // ntp)
+    mine = lax.psum_scatter(mine, "tp", scatter_dimension=1, tiled=True)
+    mine = mine.reshape(batches, tok_rows, width // ntp).astype(jnp.float32)
+    tp_width = width // ntp
     tp_start = lax.axis_index("tp") * tp_width
-    resid_share = lax.dynamic_slice_in_dim(resid, tp_start, tp_width, 1)
-    whole = lax.psum(partial_sum.astype(jnp.bfloat16), "tp").astype(jnp.float32)
-    share = lax.dynamic_slice_in_dim(whole, tp_start, tp_width, 1)
-    return (resid_share + share).astype(jnp.bfloat16)
+    resid_share = lax.dynamic_slice_in_dim(resid, tp_start, tp_width, 2)
+    return (resid_share + mine).astype(jnp.bfloat16)
 
 
 def migrate(old_weights, old_place, new_place):
@@ -155,11 +134,7 @@
 ):
     context = attend(queries, new_keys, new_values, cache_keys, cache_values, lengths)
     moved = migrate(old_weights, old_place, new_place)
-    first_out = expert_block(
-        hidden[0], expert_ids[0], route_weights[0], old_place, old_weights[0], gain
-    )
-    second_out = expert_block(hidden[1], expert_ids[1], route_weights[1], new_place, moved[0], gain)
-    layer_out = jnp.stack([first_out, second_out])
+    layer_out = expert_all(hidden, expert_ids, route_weights, old_place, old_weights[0], gain)
     return (context, layer_out, moved)
 
 

time: 528 us -> 1360 us (2.58)
  waiting for transfers between devices: 334 us -> 946 us
  blocking collectives: 0 us -> 334 us
  local copies, waits for them, and re-layouts: 81 us -> 22 us
  starting transfers between devices: 60.2 us -> 13.3 us
    reduce_scatter x0 -> x2, waiting for transfers between devices: none -> 902 us  [the longest x1 885 us: expert_all(): mine = lax.psum_scatter(weighted, 'req', scatter_dimension=0, tiled=True)]
    all_gather x0 -> x1, blocking collectives: none -> 334 us  [expert_all(): all_coef = lax.all_gather(coef, 'req', axis=0, tiled=False)]
    all_to_all x4 -> x0, waiting for transfers between devices: 164 us -> none  [the longest x2 104 us: expert_block(): lax.all_to_all(outgoing, 'req', split_axis=0, concat_axis=0, tiled=True)]
    all_to_all x1, waiting for transfers between devices: 55.9 us -> 0.01 us  [migrate(): lax.all_to_all(sending, 'req', split_axis=0, concat_axis=0, tiled=True)]
    psum x1 -> x0, waiting for transfers between devices: 49.8 us -> none  [expert_block(): whole = lax.psum(partial_sum.astype(jnp.bfloat16), 'tp').astype(jnp.float32)]
    all_to_all x4 -> x0, starting transfers between devices: 45.1 us -> none  [the longest x2 29.2 us: expert_block(): lax.all_to_all(outgoing, 'req', split_axis=0, concat_axis=0, tiled=True)]
    reshape x10 -> x2, local copies, waits for them, and re-layouts: 40 us -> 1.66 us  [expert_all(): mine = mine.reshape(batches * tok_rows, ntp, width // ntp)]
    all_to_all x1, waiting for transfers between devices: 64.4 us -> 44 us  [migrate(): lax.all_to_all(pieces, 'req', split_axis=0, concat_axis=0, tiled=True)]
  transfers between devices with their start and end apart: 7 -> 5, of which waited for: 7 -> 3; matrix products, arithmetic and copies ran while one was open for 18% -> 2% of each run, Pallas kernels for 0% -> 0%
where the time goes in v1:
time: 1360 us
  waiting for transfers between devices  946 us (70%)
  blocking collectives  334 us (25%)
  local copies, waits for them, and re-layouts  22 us (2%)
  between operations  18.5 us (1%)
    reduce_scatter x1, waiting for transfers between devices, expert_all(): mine = lax.psum_scatter(weighted, 'req', scatter_dimension=0, tiled=True)  885 us
    all_gather x1, blocking collectives, expert_all(): all_coef = lax.all_gather(coef, 'req', axis=0, tiled=False)  334 us
    all_to_all x1, waiting for transfers between devices, migrate(): lax.all_to_all(pieces, 'req', split_axis=0, concat_axis=0, tiled=True)  44 us
  transfers between devices with their start and end apart: 5, of which 3 were waited for; matrix products, arithmetic and copies ran while one was open for 2% of the time, Pallas kernels for 0%

profile of v1, /device:TPU:1, one launch (start us, length us, event | category | flops | bytes accessed | tf_op | source)
XLA Modules:
  0.0 1355.6 jit_solution(4413715467472222030)
XLA Ops:
  7.2 1.1 multiply_reduce_fusion
  8.4 1.6 divide_convert_fusion
  10.1 1.2 dynamic_slice.10
  15.2 0.8 select_reduce_fusion.2
  16.0 0.6 dynamic_slice.11
  17.3 0.8 select_reduce_fusion.3
  18.0 334.0 %all-gather.1 = f32[256,8,8]{2,1,0:T(8,128)S(1)} all-gather(f32[2,8,8]{2,1,0:T(8,128)S(1)} %select_reduce_fusion.3), channel_id=3, replica_groups=mesh['req'=128,'tp'=4] {'req'}, dimensions={0}, use_global_device_ids=true | all-gather | bytes 66048 | tf_op jit(solution)/shard_map/all_gather | solution.py:68
  352.0 0.4 select_reduce_fusion
  352.8 5.5 fusion
  358.3 5.2 multiply_convert_fusion
  363.5 2.7 copy.44
  366.2 2.5 reshape.159
  368.7 6.4 all-to-all-start
  375.2 44.0 %all-to-all-done = bf16[128,18,432]{2,1,0:T(8,128)(2,1)S(1)} async-done(((bf16[128,18,432]{2,1,0:T(8,128)(2,1)}), bf16[128,18,432]{2,1,0:T(8,128)(2,1)S(1)}, u32[]{:S(2)}, u32[]{:S(2)}) %all-to-all-start) | async-done | bytes 1990688 | tf_op jit(solution)/shard_map/all_to_all | solution.py:106
  419.3 2.4 gather_fusion
  421.6 6.8 all-to-all-start.1
  428.5 0.7 convert_element_type.48
  429.4 0.8 reshape.151
  430.3 1.5 reshape.153
  431.7 0.9 fusion.11
  432.9 0.8 fusion.23
  433.7 0.7 reshape.161
  434.4 1.1 fusion.12
  435.6 885.3 %reduce-scatter.3.cloned.1.call-done = bf16[1,16,2304]{2,1,0:T(8,128)(2,1)} async-done(((bf16[128,16,2304]{2,1,0:T(8,128)(2,1)}), bf16[1,16,2304]{2,1,0:T(8,128)(2,1)}) %reduce-scatter.3.cloned.1.call-update) | async-done | bytes 73744 | tf_op jit(solution)/shard_map/reduce_scatter | solution.py:90
  1320.9 1.0 reshape.158
  1321.9 0.6 copy.43
  1322.6 1.3 fusion.7
  1323.9 0.7 reshape.155
  1324.6 2.6 reshape.160
  1327.2 4.1 copy.45
  1331.3 16.2 %reduce-scatter.5.cloned.1.call-done = bf16[16,1,576]{2,0,1:T(8,128)(2,1)} async-done(((bf16[16,4,576]{2,0,1:T(8,128)(2,1)}), bf16[16,1,576]{2,0,1:T(8,128)(2,1)}) %reduce-scatter.5.cloned.1.call-update) | async-done | bytes 18448 | tf_op jit(solution)/shard_map/reduce_scatter | solution.py:92
  1347.5 1.5 fusion.16
  (37 shorter events, 1.0 us)
Async XLA Ops:
  7.2 425.7 %copy-start = (bf16[256,576]{0,1:T(8,128)(2,1)S(1)}, bf16[256,576]{0,1:T(8,128)(2,1)}, u32[]{:S(2)}) copy-start(bf16[256,576]{0,1:T(8,128)(2,1)} %param.16) | copy-start | bytes 884740
  7.2 345.6 %copy-start.1 = (bf16[1,2304,432]{1,2,0:T(8,128)(2,1)S(1)}, bf16[1,2304,432]{1,2,0:T(8,128)(2,1)}, u32[]{:S(2)}) copy-start(bf16[1,2304,432]{1,2,0:T(8,128)(2,1)} %param.25) | copy-start | bytes 5971972
  7.2 345.6 %all-gather.4.cloned.1.call-start = ((), (), s32[]{:S(2)}) async-start(), calls=%async_computation.6 | async-start | bytes 9510912 | tf_op jit(solution)/shard_map/all_gather | solution.py:67
  10.0 1310.8 %reduce-scatter.3.cloned.1.call-start = ((), (), s32[]{:S(2)}) async-start(), calls=%async_computation.4 | async-start | bytes 9510912 | tf_op jit(solution)/shard_map/reduce_scatter | solution.py:90
  368.7 6.4 copy-start.5
  368.7 50.5 %all-to-all-start = ((bf16[128,18,432]{2,1,0:T(8,128)(2,1)}), bf16[128,18,432]{2,1,0:T(8,128)(2,1)S(1)}, u32[]{:S(2)}, u32[]{:S(2)}) async-start(bf16[128,18,432]{2,1,0:T(8,128)(2,1)} %reshape.159), calls=%async_computation.2 | async-start | bytes 6291456 | tf_op jit(solution)/shard_map/all_to_all | solution.py:106
  421.6 6.9 copy-start.2
  421.6 7.6 copy-start.4
  421.6 12.1 copy-start.3
  421.6 903.0 %all-to-all-start.1 = ((bf16[128,18,432]{2,1,0:T(8,128)(2,1)}), bf16[128,18,432]{2,1,0:T(8,128)(2,1)S(1)}, u32[]{:S(2)}, u32[]{:S(2)}) async-start(bf16[128,18,432]{2,1,0:T(8,128)(2,1)} %gather_fusion), calls=%async_computation.3 | async-start | bytes 6291456 | tf_op jit(solution)/shard_map/all_to_all | solution.py:116
  428.5 919.1 %reduce-scatter.5.cloned.1.call-start = ((), (), s32[]{:S(2)}) async-start(), calls=%async_computation.5 | async-start | bytes 102400 | tf_op jit(solution)/shard_map/reduce_scatter | solution.py:92
Sparse Core Ops, SparseCore 0:
  13.0 167.0 all-gather.3
  363.6 957.2 reduce-scatter.2
  1323.7 23.8 reduce-scatter.4

commit v2 on v0

--- a/solution.py
+++ b/solution.py
@@ -59,19 +59,30 @@
     return jnp.sum(jnp.where(match, devices[None, :], 0), axis=1)
 
 
-def expert_block(hidden_rows, chosen, weights_now, place, shard_weights, gain):
+CORE_PAIRS = [(0, 1), (1, 0), (2, 3), (3, 2)]
+Z_PAIRS = [(0, 2), (2, 0), (1, 3), (3, 1)]
+
+
+def expert_routed(hidden, chosen, route_weights, place, shard_weights, gain):
     nreq = lax.axis_size("req")
     me_index = lax.axis_index("req")
+    tp_index = lax.axis_index("tp")
+    core = tp_index % 2
+    zpos = tp_index // 2
     split_count = max(1, nreq // 16)
     shard_count = EXPERTS * split_count
-    tok_rows, width = hidden_rows.shape
+    batches, tok_rows, width = hidden.shape
+    slots = batches * CAP
+    half = width // 2
+    quarter = width // 4
     hid_dev = shard_weights.shape[1] // 3
-    resid = hidden_rows.astype(jnp.float32)
+    resid = hidden.astype(jnp.float32)
     normed = (
         resid * gain / jnp.sqrt(jnp.mean(resid * resid, axis=-1, keepdims=True) + 1e-05)
     ).astype(jnp.bfloat16)
     flat_ids = chosen.reshape(-1)
     assigns = flat_ids.shape[0]
+    topk = assigns // (batches * tok_rows)
     shard_dest = choose_holders(place, me_index, nreq, shard_count)
     shard_list = flat_ids[:, None] * split_count + jnp.arange(split_count, dtype=jnp.int32)[None, :]
     pick = shard_list[:, :, None] == jnp.arange(shard_count, dtype=jnp.int32)[None, None, :]
@@ -81,16 +92,19 @@
         assign_index[None, :] < assign_index[:, None]
     )
     rank_in = jnp.sum(earlier.astype(jnp.int32), axis=1)
-    slot = dest * CAP + rank_in[:, None]
+    slot = dest * slots + rank_in[:, None]
     hits = jnp.any(
-        slot[None, :, :] == jnp.arange(nreq * CAP, dtype=jnp.int32)[:, None, None], axis=-1
-    )
-    repeated = jnp.repeat(normed, assigns // tok_rows, axis=0)
-    outgoing = jnp.dot(hits.astype(jnp.bfloat16), repeated, preferred_element_type=jnp.float32)
-    outgoing = outgoing.astype(jnp.bfloat16).reshape(nreq, CAP, width)
+        slot[None, :, :] == jnp.arange(nreq * slots, dtype=jnp.int32)[:, None, None], axis=-1
+    )
+    repeated = jnp.repeat(normed.reshape(batches * tok_rows, width), topk, axis=0)
+    my_half = lax.dynamic_slice_in_dim(repeated, core * half, half, 1)
+    outgoing = jnp.dot(hits.astype(jnp.bfloat16), my_half, preferred_element_type=jnp.float32)
+    outgoing = outgoing.astype(jnp.bfloat16).reshape(nreq, slots, half)
     received = lax.all_to_all(outgoing, "req", split_axis=0, concat_axis=0, tiled=True)
-    sources, items, feat = received.shape
-    flat_rows = received.reshape(sources * items, feat)
+    other = lax.ppermute(received, "tp", CORE_PAIRS)
+    low = jnp.where(core == 0, received, other)
+    high = jnp.where(core == 0, other, received)
+    flat_rows = jnp.concatenate([low, high], axis=-1).reshape(nreq * slots, width)
     gate_up = jnp.dot(
         flat_rows, shard_weights[:, : 2 * hid_dev], preferred_element_type=jnp.float32
     )
@@ -100,22 +114,27 @@
         shard_weights[:, 2 * hid_dev :],
         (((1,), (1,)), ((), ())),
         preferred_element_type=jnp.float32,
-    )
-    part = part.astype(jnp.bfloat16).reshape(sources, items, feat)
-    returned = lax.all_to_all(part, "req", split_axis=0, concat_axis=0, tiled=True)
-    returned = returned.reshape(nreq * CAP, width)
+    ).astype(jnp.bfloat16)
+    part = part.reshape(nreq * slots, 2, 2, quarter)
+    keep = lax.dynamic_index_in_dim(part, core, 2, keepdims=False)
+    send = lax.dynamic_index_in_dim(part, 1 - core, 2, keepdims=False)
+    got = lax.ppermute(send, "tp", CORE_PAIRS)
+    pair_sum = (keep.astype(jnp.float32) + got.astype(jnp.float32)).astype(jnp.bfloat16)
+    pair_sum = pair_sum.reshape(nreq, slots, half)
+    returned = lax.all_to_all(pair_sum, "req", split_axis=0, concat_axis=0, tiled=True)
+    returned = returned.reshape(nreq * slots, 2, quarter)
     picked = (
         returned[slot.reshape(-1)]
         .astype(jnp.float32)
-        .reshape(tok_rows, assigns // tok_rows, split_count, width)
-    )
-    partial_sum = jnp.einsum("rksd,rk->rd", picked, weights_now)
-    tp_width = width // lax.axis_size("tp")
-    tp_start = lax.axis_index("tp") * tp_width
-    resid_share = lax.dynamic_slice_in_dim(resid, tp_start, tp_width, 1)
-    whole = lax.psum(partial_sum.astype(jnp.bfloat16), "tp").astype(jnp.float32)
-    share = lax.dynamic_slice_in_dim(whole, tp_start, tp_width, 1)
-    return (resid_share + share).astype(jnp.bfloat16)
+        .reshape(batches * tok_rows, topk, split_count, 2, quarter)
+    )
+    weights_now = route_weights.reshape(batches * tok_rows, topk)
+    partial_sum = jnp.einsum("rksze,rk->rze", picked, weights_now)
+    mine = lax.dynamic_index_in_dim(partial_sum, zpos, 1, keepdims=False)
+    away = lax.dynamic_index_in_dim(partial_sum, 1 - zpos, 1, keepdims=False)
+    total = mine + lax.ppermute(away, "tp", Z_PAIRS)
+    resid_share = lax.dynamic_slice_in_dim(resid, tp_index * quarter, quarter, 2)
+    return (resid_share + total.reshape(batches, tok_rows, quarter)).astype(jnp.bfloat16)
 
 
 def migrate(old_weights, old_place, new_place):
@@ -155,11 +174,7 @@
 ):
     context = attend(queries, new_keys, new_values, cache_keys, cache_values, lengths)
     moved = migrate(old_weights, old_place, new_place)
-    first_out = expert_block(
-        hidden[0], expert_ids[0], route_weights[0], old_place, old_weights[0], gain
-    )
-    second_out = expert_block(hidden[1], expert_ids[1], route_weights[1], new_place, moved[0], gain)
-    layer_out = jnp.stack([first_out, second_out])
+    layer_out = expert_routed(hidden, expert_ids, route_weights, old_place, old_weights[0], gain)
     return (context, layer_out, moved)
 
 

time: 528 us -> 353 us (0.67)
  waiting for transfers between devices: 334 us -> 133 us
  blocking collectives: 0 us -> 79.9 us
  starting transfers between devices: 60.2 us -> 34.1 us
  local copies, waits for them, and re-layouts: 81 us -> 66.1 us
  between operations: 14.3 us -> 0.94 us
  matrix products: 17 us -> 9.9 us
    all_to_all x4 -> x1, waiting for transfers between devices: 164 us -> 54.2 us  [expert_routed(): lax.all_to_all(pair_sum, 'req', split_axis=0, concat_axis=0, tiled=True)]
    all_to_all x0 -> x1, blocking collectives: none -> 79.9 us  [expert_routed(): lax.all_to_all(outgoing, 'req', split_axis=0, concat_axis=0, tiled=True)]
    psum x1 -> x0, waiting for transfers between devices: 49.8 us -> none  [expert_block(): whole = lax.psum(partial_sum.astype(jnp.bfloat16), 'tp').astype(jnp.float32)]
    all_to_all x4 -> x1, starting transfers between devices: 45.1 us -> 7.31 us  [expert_routed(): lax.all_to_all(pair_sum, 'req', split_axis=0, concat_axis=0, tiled=True)]
    all_to_all x1, waiting for transfers between devices: 64.4 us -> 31.4 us  [migrate(): lax.all_to_all(pieces, 'req', split_axis=0, concat_axis=0, tiled=True)]
    reshape x10 -> x6, local copies, waits for them, and re-layouts: 40 us -> 17.4 us  [the longest x1 6.74 us: expert_routed(): jnp.concatenate([low, high], axis=-1).reshape(nreq * slots, width)]
    all_to_all x1, waiting for transfers between devices: 55.9 us -> 43.3 us  [migrate(): lax.all_to_all(sending, 'req', split_axis=0, concat_axis=0, tiled=True)]
    convert_element_type x0 -> x2, local copies, waits for them, and re-layouts: none -> 11.9 us  [the longest x1 6.16 us: expert_routed(): (keep.astype(jnp.float32) + got.astype(jnp.float32)).astype(jnp.bfloat16)]
  transfers between devices with their start and end apart: 7 -> 6, of which waited for: 7 -> 4; matrix products, arithmetic and copies ran while one was open for 18% -> 25% of each run, Pallas kernels for 0% -> 0%
where the time goes in v2:
time: 353 us; the launch traced here: 348 us
  waiting for transfers between devices  133 us (38%)
  blocking collectives  79.9 us (23%)
  local copies, waits for them, and re-layouts  66.1 us (19%)
  starting transfers between devices  34.1 us (10%)
  other arithmetic  24.2 us (7%)
  matrix products  9.9 us (3%)
    all_to_all x1, blocking collectives, expert_routed(): lax.all_to_all(outgoing, 'req', split_axis=0, concat_axis=0, tiled=True)  79.9 us
    all_to_all x1, waiting for transfers between devices, expert_routed(): lax.all_to_all(pair_sum, 'req', split_axis=0, concat_axis=0, tiled=True)  54.2 us
    all_to_all x1, waiting for transfers between devices, migrate(): lax.all_to_all(sending, 'req', split_axis=0, concat_axis=0, tiled=True)  43.3 us
    all_to_all x1, waiting for transfers between devices, migrate(): lax.all_to_all(pieces, 'req', split_axis=0, concat_axis=0, tiled=True)  31.4 us
    unnamed x25, local copies, waits for them, and re-layouts  11.1 us
    all_to_all x1, starting transfers between devices, migrate(): lax.all_to_all(sending, 'req', split_axis=0, concat_axis=0, tiled=True)  8.42 us
    all_to_all x1, starting transfers between devices, migrate(): lax.all_to_all(pieces, 'req', split_axis=0, concat_axis=0, tiled=True)  7.48 us
    all_to_all x1, starting transfers between devices, expert_routed(): lax.all_to_all(pair_sum, 'req', split_axis=0, concat_axis=0, tiled=True)  7.31 us
  transfers between devices with their start and end apart: 6, of which 4 were waited for; matrix products, arithmetic and copies ran while one was open for 25% of the time, Pallas kernels for 0%

profile of v2, /device:TPU:1, one launch (start us, length us, event | category | flops | bytes accessed | tf_op | source)
XLA Modules:
  0.0 348.0 jit_solution(10176147187392722831)
XLA Ops:
  8.3 1.7 reshape.263
  10.0 79.9 %all_to_all.20 = bf16[128,6,1152]{2,1,0:T(8,128)(2,1)S(1)} all-to-all(bf16[128,6,1152]{2,1,0:T(8,128)(2,1)} %reshape.263), channel_id=1, replica_groups=mesh['req'=128,'tp'=4] {'req'}, dimensions={0} | all-to-all | bytes 3538944 | tf_op jit(solution)/shard_map/all_to_all | solution.py:103
  91.4 4.6 %collective-permute-start = (bf16[128,6,1152]{2,0,1:T(8,128)(2,1)}, bf16[128,6,1152]{2,0,1:T(8,128)(2,1)}, u32[]{:S(2)}, u32[]{:S(2)}) collective-permute-start(bf16[128,6,1152]{2,0,1:T(8,128)(2,1)} %copy.48), channel_id=1, source_target_pairs={{0,1},{1,0},{2,3},{3,2},{4,5},{5,4},{6,7},{7,6},{8,9},{9,8},{10,11... | collective-permute-start | bytes 5308424 | tf_op jit(solution)/shard_map/ppermute | solution.py:104
  96.1 4.1 %copy.54 = bf16[1,2304,432]{2,1,0:T(8,128)(2,1)} copy(bf16[1,2304,432]{1,2,0:T(8,128)(2,1)} %param.25) | data formatting | bytes 3981312 | tf_op args[12]
  100.2 5.2 %reshape.270 = bf16[128,18,432]{2,1,0:T(8,128)(2,1)} reshape(bf16[1,2304,432]{2,1,0:T(8,128)(2,1)} %copy.54) | data formatting | bytes 3981312 | tf_op jit(solution)/shard_map/reshape | solution.py:145
  105.4 7.5 %all-to-all-start.2 = ((bf16[128,18,432]{2,1,0:T(8,128)(2,1)}), bf16[128,18,432]{2,1,0:T(8,128)(2,1)}, u32[]{:S(2)}, u32[]{:S(2)}) async-start(bf16[128,18,432]{2,1,0:T(8,128)(2,1)} %reshape.270), calls=%async_computation.2 | async-start | bytes 6291456 | tf_op jit(solution)/shard_map/all_to_all | solution.py:146
  112.9 2.7 copy_select_fusion.1
  115.6 3.1 pad_maximum_fusion
  118.7 6.7 %reshape.264 = bf16[768,2304]{1,0:T(8,128)(2,1)} reshape(bf16[128,6,2304]{2,1,0:T(8,128)(2,1)} %pad_maximum_fusion) | data formatting | bytes 7077888 | tf_op jit(solution)/shard_map/reshape | solution.py:107
  125.4 3.2 fusion.1
  128.7 2.9 convolution_convert_fusion
  131.6 5.8 %copy.51 = bf16[768,2304]{0,1:T(8,128)(2,1)} copy(bf16[768,2304]{1,0:T(8,128)(2,1)} %convolution_convert_fusion) | data formatting | bytes 7077888 | tf_op jit(solution)/shard_map/convert_element_type | solution.py:117
  137.3 2.8 dynamic-slice_bitcast_fusion
  140.1 1.9 collective-permute-start.1
  142.1 3.9 %collective-permute-done.1 = bf16[768,2,576]{0,2,1:T(8,128)(2,1)S(1)} collective-permute-done((bf16[768,2,576]{0,2,1:T(8,128)(2,1)}, bf16[768,2,576]{0,2,1:T(8,128)(2,1)S(1)}, u32[]{:S(2)}, u32[]{:S(2)}) %collective-permute-start.1) | collective-permute-done | bytes 1769504 | tf_op jit(solution)/shard_map/ppermute | solution.py:121
  145.9 3.1 fusion
  149.0 6.2 %copy.52 = bf16[768,2,576]{2,1,0:T(2,128)(2,1)S(1)} copy(bf16[768,2,576]{0,2,1:T(8,128)(2,1)} %fusion) | data formatting | bytes 3538944 | tf_op jit(solution)/shard_map/convert_element_type | solution.py:122
  155.2 3.0 reshape.266
  158.2 31.4 %all-to-all-done.2 = bf16[128,18,432]{2,1,0:T(8,128)(2,1)} async-done(((bf16[128,18,432]{2,1,0:T(8,128)(2,1)}), bf16[128,18,432]{2,1,0:T(8,128)(2,1)}, u32[]{:S(2)}, u32[]{:S(2)}) %all-to-all-start.2) | async-done | bytes 1990688 | tf_op jit(solution)/shard_map/all_to_all | solution.py:146
  189.6 7.3 %all-to-all-start.1 = ((bf16[128,6,1152]{2,1,0:T(8,128)(2,1)}), bf16[128,6,1152]{2,1,0:T(8,128)(2,1)S(1)}, u32[]{:S(2)}, u32[]{:S(2)}) async-start(bf16[128,6,1152]{2,1,0:T(8,128)(2,1)} %reshape.266), calls=%async_computation.1 | async-start | bytes 4718592 | tf_op jit(solution)/shard_map/all_to_all | solution.py:124
  197.0 4.3 %gather_fusion.1 = bf16[128,18,432]{2,1,0:T(8,128)(2,1)} fusion(bf16[128,18,432]{2,1,0:T(8,128)(2,1)} %all-to-all-done.2, s32[1024]{0:T(1024)S(1)} %pad_clamp_fusion), kind=kCustom, calls=%fused_computation.1 | custom fusion | bytes 3981824 | tf_op jit(solution)/shard_map/gather | solution.py:155
  201.3 54.2 %all-to-all-done.1 = bf16[128,6,1152]{2,1,0:T(8,128)(2,1)S(1)} async-done(((bf16[128,6,1152]{2,1,0:T(8,128)(2,1)}), bf16[128,6,1152]{2,1,0:T(8,128)(2,1)S(1)}, u32[]{:S(2)}, u32[]{:S(2)}) %all-to-all-start.1) | async-done | bytes 1769504 | tf_op jit(solution)/shard_map/all_to_all | solution.py:124
  257.0 8.4 %all-to-all-start.3 = ((bf16[128,18,432]{2,1,0:T(8,128)(2,1)}), bf16[128,18,432]{2,1,0:T(8,128)(2,1)S(1)}, u32[]{:S(2)}, u32[]{:S(2)}) async-start(bf16[128,18,432]{2,1,0:T(8,128)(2,1)} %gather_fusion.1), calls=%async_computation.3 | async-start | bytes 6291456 | tf_op jit(solution)/shard_map/all_to_all | solution.py:156
  275.1 5.8 %reshape.267 = bf16[768,2,576]{2,1,0:T(2,128)(2,1)} reshape(bf16[128,6,1152]{2,1,0:T(8,128)(2,1)} %copy-done.1) | data formatting | bytes 3538944 | tf_op jit(solution)/shard_map/reshape | solution.py:125
  280.8 4.4 %gather_fusion = bf16[256,2,576]{2,1,0:T(2,128)(2,1)} fusion(bf16[768,2,576]{2,1,0:T(2,128)(2,1)} %reshape.267, s32[1024]{0:T(1024)S(1)} %pad_clamp_fusion.1), kind=kCustom, calls=%fused_computation | custom fusion | bytes 1180672 | tf_op jit(solution)/shard_map/gather | solution.py:127
  285.2 1.8 convert_reduce_fusion
  287.9 4.4 %collective-permute-start.2 = (f32[16,576]{1,0:T(8,128)S(1)}, f32[16,576]{1,0:T(8,128)}, u32[]{:S(2)}, u32[]{:S(2)}) collective-permute-start(f32[16,576]{1,0:T(8,128)S(1)} %dynamic-slice_bitcast_fusion.1), channel_id=1, source_target_pairs={{0,2},{2,0},{1,3},{3,1},{4,6},{6,4},{5,7},{7,5},{8,10},{10,8},{9,1... | collective-permute-start | bytes 110600 | tf_op jit(solution)/shard_map/ppermute | solution.py:135
  292.2 2.0 fusion.6
  296.4 43.3 %all-to-all-done.3 = bf16[128,18,432]{2,1,0:T(8,128)(2,1)S(1)} async-done(((bf16[128,18,432]{2,1,0:T(8,128)(2,1)}), bf16[128,18,432]{2,1,0:T(8,128)(2,1)S(1)}, u32[]{:S(2)}, u32[]{:S(2)}) %all-to-all-start.3) | async-done | bytes 1990688 | tf_op jit(solution)/shard_map/all_to_all | solution.py:156
  339.7 2.6 reshape.271
  342.3 4.1 %copy.55 = bf16[1,2304,432]{1,2,0:T(8,128)(2,1)} copy(bf16[1,2304,432]{2,1,0:T(8,128)(2,1)} %reshape.271) | data formatting | bytes 3981312
  346.5 1.5 fusion.22
  (71 shorter events, 23.2 us)
Async XLA Ops:
  0.6 270.5 %copy-start = (bf16[256,576]{0,1:T(8,128)(2,1)S(1)}, bf16[256,576]{0,1:T(8,128)(2,1)}, u32[]{:S(2)}) copy-start(bf16[256,576]{0,1:T(8,128)(2,1)} %param.16) | copy-start | bytes 884740
  91.4 21.5 %collective-permute-start = (bf16[128,6,1152]{2,0,1:T(8,128)(2,1)}, bf16[128,6,1152]{2,0,1:T(8,128)(2,1)}, u32[]{:S(2)}, u32[]{:S(2)}) collective-permute-start(bf16[128,6,1152]{2,0,1:T(8,128)(2,1)} %copy.48), channel_id=1, source_target_pairs={{0,1},{1,0},{2,3},{3,2},{4,5},{5,4},{6,7},{7,6},{8,9},{9,8},{10,11... | collective-permute-start | bytes 5308424 | tf_op jit(solution)/shard_map/ppermute | solution.py:104
  105.4 84.2 %all-to-all-start.2 = ((bf16[128,18,432]{2,1,0:T(8,128)(2,1)}), bf16[128,18,432]{2,1,0:T(8,128)(2,1)}, u32[]{:S(2)}, u32[]{:S(2)}) async-start(bf16[128,18,432]{2,1,0:T(8,128)(2,1)} %reshape.270), calls=%async_computation.2 | async-start | bytes 6291456 | tf_op jit(solution)/shard_map/all_to_all | solution.py:146
  118.7 6.7 %copy-start.2 = (bf16[1,2304,432]{1,2,0:T(8,128)(2,1)S(1)}, bf16[1,2304,432]{1,2,0:T(8,128)(2,1)}, u32[]{:S(2)}) copy-start(bf16[1,2304,432]{1,2,0:T(8,128)(2,1)} %param.25) | copy-start | bytes 5971972
  140.1 5.8 %collective-permute-start.1 = (bf16[768,2,576]{0,2,1:T(8,128)(2,1)}, bf16[768,2,576]{0,2,1:T(8,128)(2,1)S(1)}, u32[]{:S(2)}, u32[]{:S(2)}) collective-permute-start(bf16[768,2,576]{0,2,1:T(8,128)(2,1)} %dynamic-slice_bitcast_fusion), channel_id=1, source_target_pairs={{0,1},{1,0},{2,3},{3,2},{4,5},{5,4},{6,7},{7,6},{8,9},{9,8},{10,11... | collective-permute-start | bytes 5308424 | tf_op jit(solution)/shard_map/ppermute | solution.py:121
  158.2 38.7 %copy-start.10 = (s32[128]{0:T(128)S(1)}, s32[128]{0:T(128)}, u32[]{:S(2)}) copy-start(s32[128]{0:T(128)} %param.24) | copy-start | bytes 1540
  189.6 66.0 %all-to-all-start.1 = ((bf16[128,6,1152]{2,1,0:T(8,128)(2,1)}), bf16[128,6,1152]{2,1,0:T(8,128)(2,1)S(1)}, u32[]{:S(2)}, u32[]{:S(2)}) async-start(bf16[128,6,1152]{2,1,0:T(8,128)(2,1)} %reshape.266), calls=%async_computation.1 | async-start | bytes 4718592 | tf_op jit(solution)/shard_map/all_to_all | solution.py:124
  201.3 64.2 %copy-start.8 = (f32[2,8,2]{1,2,0:T(2,128)S(1)}, f32[2,8,2]{1,2,0:T(2,128)}, u32[]{:S(2)}) copy-start(f32[2,8,2]{1,2,0:T(2,128)} %param.22) | copy-start | bytes 388
  201.3 64.3 %copy-start.9 = (s32[1,16]{1,0:T(1,128)S(1)}, s32[1,16]{1,0:T(1,128)}, u32[]{:S(2)}) copy-start(s32[1,16]{1,0:T(1,128)} %param.18) | copy-start | bytes 196
  201.3 70.7 %copy-start.7 = (bf16[2,8,576]{2,1,0:T(8,128)(2,1)S(1)}, bf16[2,8,576]{2,1,0:T(8,128)(2,1)}, u32[]{:S(2)}) copy-start(bf16[2,8,576]{2,1,0:T(8,128)(2,1)} %param.15) | copy-start | bytes 55300
  255.6 1.4 copy-start.1
  257.0 82.7 %all-to-all-start.3 = ((bf16[128,18,432]{2,1,0:T(8,128)(2,1)}), bf16[128,18,432]{2,1,0:T(8,128)(2,1)S(1)}, u32[]{:S(2)}, u32[]{:S(2)}) async-start(bf16[128,18,432]{2,1,0:T(8,128)(2,1)} %gather_fusion.1), calls=%async_computation.3 | async-start | bytes 6291456 | tf_op jit(solution)/shard_map/all_to_all | solution.py:156
  272.0 3.1 copy-start.6
  280.8 13.4 %copy-start.3 = (bf16[2,8,2304]{2,1,0:T(8,128)(2,1)S(1)}, bf16[2,8,2304]{2,1,0:T(8,128)(2,1)}, u32[]{:S(2)}) copy-start(bf16[2,8,2304]{2,1,0:T(8,128)(2,1)} %param.19) | copy-start | bytes 221188
  287.2 0.6 copy-start.4
  287.9 58.6 %collective-permute-start.2 = (f32[16,576]{1,0:T(8,128)S(1)}, f32[16,576]{1,0:T(8,128)}, u32[]{:S(2)}, u32[]{:S(2)}) collective-permute-start(f32[16,576]{1,0:T(8,128)S(1)} %dynamic-slice_bitcast_fusion.1), channel_id=1, source_target_pairs={{0,2},{2,0},{1,3},{3,1},{4,6},{6,4},{5,7},{7,5},{8,10},{10,8},{9,1... | collective-permute-start | bytes 110600 | tf_op jit(solution)/shard_map/ppermute | solution.py:135
  342.3 4.1 %copy-start.5 = (f32[16,1,2,576]{3,0,2,1:T(8,128)S(1)}, f32[16,1,2,576]{3,0,2,1:T(8,128)}, u32[]{:S(2)}) copy-start(f32[16,1,2,576]{3,0,2,1:T(8,128)} %copy-done.4) | copy-start | bytes 221188

commit v3 on v2

--- a/solution.py
+++ b/solution.py
@@ -63,7 +63,7 @@
 Z_PAIRS = [(0, 2), (2, 0), (1, 3), (3, 1)]
 
 
-def expert_routed(hidden, chosen, route_weights, place, shard_weights, gain):
+def expert_routed(hidden, chosen, route_weights, place, shard_weights, gain, extra):
     nreq = lax.axis_size("req")
     me_index = lax.axis_index("req")
     tp_index = lax.axis_index("tp")
@@ -120,9 +120,13 @@
     send = lax.dynamic_index_in_dim(part, 1 - core, 2, keepdims=False)
     got = lax.ppermute(send, "tp", CORE_PAIRS)
     pair_sum = (keep.astype(jnp.float32) + got.astype(jnp.float32)).astype(jnp.bfloat16)
-    pair_sum = pair_sum.reshape(nreq, slots, half)
-    returned = lax.all_to_all(pair_sum, "req", split_axis=0, concat_axis=0, tiled=True)
-    returned = returned.reshape(nreq * slots, 2, quarter)
+    pair_sum = pair_sum.reshape(nreq, slots * half)
+    sending = extra.reshape(nreq, -1)
+    both = lax.all_to_all(
+        jnp.concatenate([pair_sum, sending], axis=1), "req", split_axis=0, concat_axis=0, tiled=True
+    )
+    returned = both[:, : slots * half].reshape(nreq * slots, 2, quarter)
+    collected = both[:, slots * half :]
     picked = (
         returned[slot.reshape(-1)]
         .astype(jnp.float32)
@@ -134,7 +138,7 @@
     away = lax.dynamic_index_in_dim(partial_sum, 1 - zpos, 1, keepdims=False)
     total = mine + lax.ppermute(away, "tp", Z_PAIRS)
     resid_share = lax.dynamic_slice_in_dim(resid, tp_index * quarter, quarter, 2)
-    return (resid_share + total.reshape(batches, tok_rows, quarter)).astype(jnp.bfloat16)
+    return (resid_share + total.reshape(batches, tok_rows, quarter)).astype(jnp.bfloat16), collected
 
 
 def migrate(old_weights, old_place, new_place):
@@ -152,9 +156,7 @@
     needed = jnp.sum(
         jnp.where(new_place[:, None] == shard_ids[None, :], first_old[None, :], 0), axis=1
     )
-    sending = spread[needed]
-    collected = lax.all_to_all(sending, "req", split_axis=0, concat_axis=0, tiled=True)
-    return collected.reshape(1, width, columns)
+    return spread[needed]
 
 
 def on_device(
@@ -173,8 +175,11 @@
     old_weights,
 ):
     context = attend(queries, new_keys, new_values, cache_keys, cache_values, lengths)
-    moved = migrate(old_weights, old_place, new_place)
-    layer_out = expert_routed(hidden, expert_ids, route_weights, old_place, old_weights[0], gain)
+    sending = migrate(old_weights, old_place, new_place)
+    layer_out, collected = expert_routed(
+        hidden, expert_ids, route_weights, old_place, old_weights[0], gain, sending
+    )
+    moved = collected.reshape(old_weights.shape)
     return (context, layer_out, moved)
 
 

time: 353 us -> 408 us (1.16)
  local copies, waits for them, and re-layouts: 66.1 us -> 123 us
  other arithmetic: 24.2 us -> 32.9 us
  starting transfers between devices: 34.1 us -> 25.6 us
    unnamed x25 -> x28, local copies, waits for them, and re-layouts: 11.1 us -> 43.3 us
    all_to_all x0 -> x2, local copies, waits for them, and re-layouts: none -> 15.9 us  [expert_routed(): lax.all_to_all(jnp.concatenate([pair_sum, sending], axis=1), 'req', split...]
    all_to_all x1, waiting for transfers between devices: 31.4 us -> 47.1 us  [migrate(): lax.all_to_all(pieces, 'req', split_axis=0, concat_axis=0, tiled=True)]
    all_to_all x0 -> x2, other arithmetic: none -> 15.6 us  [expert_routed(): lax.all_to_all(jnp.concatenate([pair_sum, sending], axis=1), 'req', split...]
    all_to_all x2 -> x1, waiting for transfers between devices: 97.6 us -> 87 us  [expert_routed(): lax.all_to_all(jnp.concatenate([pair_sum, sending], axis=1), 'req', split...]
    slice x0 -> x4, local copies, waits for them, and re-layouts: none -> 9.86 us  [the longest x2 5.42 us: expert_routed(): returned = both[:, :slots * half].reshape(nreq * slots, 2, quarter)]
    all_to_all x2 -> x1, starting transfers between devices: 15.7 us -> 7.92 us  [expert_routed(): lax.all_to_all(jnp.concatenate([pair_sum, sending], axis=1), 'req', split...]
    reshape x3 -> x4, local copies, waits for them, and re-layouts: 11.4 us -> 13 us  [the longest x2 6.26 us: expert_routed(): pair_sum = pair_sum.reshape(nreq, slots * half)]
  transfers between devices with their start and end apart: 6 -> 5, of which waited for: 4 -> 2; matrix products, arithmetic and copies ran while one was open for 25% -> 14% of each run, Pallas kernels for 0% -> 0%
where the time goes in v3:
time: 408 us; the launch traced here: 404 us
  waiting for transfers between devices  134 us (33%)
  local copies, waits for them, and re-layouts  123 us (30%)
  blocking collectives  79.9 us (20%)
  other arithmetic  32.9 us (8%)
  starting transfers between devices  25.6 us (6%)
  matrix products  7.59 us (2%)
    all_to_all x1, waiting for transfers between devices, expert_routed(): lax.all_to_all(jnp.concatenate([pair_sum, sending], axis=1), 'req', split...  87 us
    all_to_all x1, blocking collectives, expert_routed(): lax.all_to_all(outgoing, 'req', split_axis=0, concat_axis=0, tiled=True)  79.9 us
    all_to_all x1, waiting for transfers between devices, migrate(): lax.all_to_all(pieces, 'req', split_axis=0, concat_axis=0, tiled=True)  47.1 us
    unnamed x28, local copies, waits for them, and re-layouts  43.3 us
    all_to_all x2, local copies, waits for them, and re-layouts, expert_routed(): lax.all_to_all(jnp.concatenate([pair_sum, sending], axis=1), 'req', split...  15.9 us
    all_to_all x2, other arithmetic, expert_routed(): lax.all_to_all(jnp.concatenate([pair_sum, sending], axis=1), 'req', split...  15.6 us
  transfers between devices with their start and end apart: 5, of which 2 were waited for; matrix products, arithmetic and copies ran while one was open for 14% of the time, Pallas kernels for 0%

profile of v3, /device:TPU:1, one launch (start us, length us, event | category | flops | bytes accessed | tf_op | source)
XLA Modules:
  0.0 403.8 jit_solution(5485286495794096843)
XLA Ops:
  10.0 79.9 %all_to_all.22 = bf16[128,6,1152]{2,1,0:T(8,128)(2,1)S(1)} all-to-all(bf16[128,6,1152]{2,1,0:T(8,128)(2,1)} %reshape.268), channel_id=1, replica_groups=mesh['req'=128,'tp'=4] {'req'}, dimensions={0} | all-to-all | bytes 3538944 | tf_op jit(solution)/shard_map/all_to_all | solution.py:103
  91.4 4.6 %collective-permute-start = (bf16[128,6,1152]{2,0,1:T(8,128)(2,1)}, bf16[128,6,1152]{2,0,1:T(8,128)(2,1)}, u32[]{:S(2)}, u32[]{:S(2)}) collective-permute-start(bf16[128,6,1152]{2,0,1:T(8,128)(2,1)} %copy.74), channel_id=1, source_target_pairs={{0,1},{1,0},{2,3},{3,2},{4,5},{5,4},{6,7},{7,6},{8,9},{9,8},{10,11... | collective-permute-start | bytes 5308424 | tf_op jit(solution)/shard_map/ppermute | solution.py:104
  96.1 4.1 %copy.79 = bf16[1,2304,432]{2,1,0:T(8,128)(2,1)} copy(bf16[1,2304,432]{1,2,0:T(8,128)(2,1)} %param.25) | data formatting | bytes 3981312 | tf_op args[12]
  100.2 5.2 %reshape.272 = bf16[128,18,432]{2,1,0:T(8,128)(2,1)} reshape(bf16[1,2304,432]{2,1,0:T(8,128)(2,1)} %copy.79) | data formatting | bytes 3981312 | tf_op jit(solution)/shard_map/reshape | solution.py:149
  105.4 7.5 %all-to-all-start.1 = ((bf16[128,18,432]{2,1,0:T(8,128)(2,1)}), bf16[128,18,432]{2,1,0:T(8,128)(2,1)}, u32[]{:S(2)}, u32[]{:S(2)}) async-start(bf16[128,18,432]{2,1,0:T(8,128)(2,1)} %reshape.272), calls=%async_computation.1 | async-start | bytes 6291456 | tf_op jit(solution)/shard_map/all_to_all | solution.py:150
  112.9 2.7 copy_select_fusion.1
  115.6 3.1 pad_maximum_fusion
  118.7 6.7 %reshape.269 = bf16[768,2304]{1,0:T(8,128)(2,1)} reshape(bf16[128,6,2304]{2,1,0:T(8,128)(2,1)} %pad_maximum_fusion) | data formatting | bytes 7077888 | tf_op jit(solution)/shard_map/reshape | solution.py:107
  125.4 3.2 fusion.1
  128.7 3.0 convolution_convert_fusion
  131.6 5.7 %copy.77 = bf16[768,2304]{0,1:T(8,128)(2,1)} copy(bf16[768,2304]{1,0:T(8,128)(2,1)} %convolution_convert_fusion) | data formatting | bytes 7077888 | tf_op jit(solution)/shard_map/convert_element_type | solution.py:117
  137.4 2.9 dynamic-slice_bitcast_fusion
  142.5 47.1 %all-to-all-done.1 = bf16[128,18,432]{2,1,0:T(8,128)(2,1)} async-done(((bf16[128,18,432]{2,1,0:T(8,128)(2,1)}), bf16[128,18,432]{2,1,0:T(8,128)(2,1)}, u32[]{:S(2)}, u32[]{:S(2)}) %all-to-all-start.1) | async-done | bytes 1990688 | tf_op jit(solution)/shard_map/all_to_all | solution.py:150
  189.6 2.6 gather_fusion
  192.2 2.9 copy.80
  195.2 3.7 fusion
  198.9 6.2 %copy.78 = bf16[768,2,576]{2,1,0:T(2,128)(2,1)S(1)} copy(bf16[768,2,576]{0,2,1:T(8,128)(2,1)} %fusion) | data formatting | bytes 3538944 | tf_op jit(solution)/shard_map/convert_element_type | solution.py:122
  207.3 4.0 copy.81
  211.3 9.6 %maximum_bitcast_fusion = bf16[128,1,14688]{0,2,1:T(8,128)(2,1)} fusion(bf16[128,7776]{0,1:T(8,128)(2,1)S(1)} %bitcast.70, bf16[128,6912]{0,1:T(8,128)(2,1)} %copy.81), kind=kLoop, calls=%fused_computation.4 | loop fusion | flops 7520256 | bytes 7520256 | tf_op jit(solution)/shard_map/all_to_all | solution.py:125
  221.4 6.0 %reduce.3 = bf16[128,14688]{0,1:T(8,128)(2,1)} reduce(bf16[128,1,14688]{0,2,1:T(8,128)(2,1)} %maximum_bitcast_fusion, bf16[]{:T(256)} %broadcast.160), dimensions={1}, to_apply=%copy.82.reduce_sub_computation | reduce | bytes 7520258 | tf_op jit(solution)/shard_map/all_to_all | solution.py:125
  227.4 6.2 %copy.114 = bf16[128,14688]{1,0:T(8,128)(2,1)} copy(bf16[128,14688]{0,1:T(8,128)(2,1)} %reduce.3) | data formatting | bytes 7520256
  233.5 9.8 %reshape.304 = bf16[128,2,7344]{2,1,0:T(2,128)(2,1)} reshape(bf16[128,14688]{1,0:T(8,128)(2,1)} %copy.114) | data formatting | bytes 7520256
  243.4 7.9 %all-to-all-start.2 = ((bf16[128,2,7344]{2,1,0:T(2,128)(2,1)}), bf16[128,2,7344]{2,1,0:T(2,128)(2,1)}, u32[]{:S(2)}, u32[]{:S(2)}) async-start(bf16[128,2,7344]{2,1,0:T(2,128)(2,1)} %reshape.304), calls=%async_computation.2 | async-start | bytes 7602176 | tf_op jit(solution)/shard_map/all_to_all | solution.py:125
  252.9 87.0 %all-to-all-done.2 = bf16[128,2,7344]{2,1,0:T(2,128)(2,1)} async-done(((bf16[128,2,7344]{2,1,0:T(2,128)(2,1)}), bf16[128,2,7344]{2,1,0:T(2,128)(2,1)}, u32[]{:S(2)}, u32[]{:S(2)}) %all-to-all-start.2) | async-done | bytes 3760160 | tf_op jit(solution)/shard_map/all_to_all | solution.py:125
  339.8 20.0 %reshape.305 = bf16[128,1,14688]{2,1,0:T(2,128)(2,1)} reshape(bf16[128,2,7344]{2,1,0:T(2,128)(2,1)} %all-to-all-done.2) | data formatting | bytes 7520256
  359.9 15.4 %copy.83 = bf16[128,1,14688]{0,2,1:T(8,128)(2,1)} copy(bf16[128,1,14688]{2,1,0:T(2,128)(2,1)} %reshape.305) | data formatting | bytes 7520256 | tf_op jit(solution)/shard_map/all_to_all | solution.py:125
  375.2 2.8 slice.32
  380.7 2.6 reshape.274
  383.3 3.6 gather_fusion.1
  387.8 3.4 collective-permute-start.2
  394.0 2.8 copy.86
  396.7 4.1 %reshape.277 = bf16[1,2304,432]{2,1,0:T(8,128)(2,1)S(1)} reshape(bf16[128,7776]{1,0:T(8,128)(2,1)} %copy.86) | data formatting | bytes 3981312 | tf_op jit(solution)/shard_map/reshape | solution.py:182
  (82 shorter events, 26.4 us)
Async XLA Ops:
  0.6 251.6 %copy-start = (bf16[256,576]{0,1:T(8,128)(2,1)S(1)}, bf16[256,576]{0,1:T(8,128)(2,1)}, u32[]{:S(2)}) copy-start(bf16[256,576]{0,1:T(8,128)(2,1)} %param.16) | copy-start | bytes 884740
  91.4 21.5 %collective-permute-start = (bf16[128,6,1152]{2,0,1:T(8,128)(2,1)}, bf16[128,6,1152]{2,0,1:T(8,128)(2,1)}, u32[]{:S(2)}, u32[]{:S(2)}) collective-permute-start(bf16[128,6,1152]{2,0,1:T(8,128)(2,1)} %copy.74), channel_id=1, source_target_pairs={{0,1},{1,0},{2,3},{3,2},{4,5},{5,4},{6,7},{7,6},{8,9},{9,8},{10,11... | collective-permute-start | bytes 5308424 | tf_op jit(solution)/shard_map/ppermute | solution.py:104
  105.4 84.2 %all-to-all-start.1 = ((bf16[128,18,432]{2,1,0:T(8,128)(2,1)}), bf16[128,18,432]{2,1,0:T(8,128)(2,1)}, u32[]{:S(2)}, u32[]{:S(2)}) async-start(bf16[128,18,432]{2,1,0:T(8,128)(2,1)} %reshape.272), calls=%async_computation.1 | async-start | bytes 6291456 | tf_op jit(solution)/shard_map/all_to_all | solution.py:150
  118.7 6.7 %copy-start.2 = (bf16[1,2304,432]{1,2,0:T(8,128)(2,1)S(1)}, bf16[1,2304,432]{1,2,0:T(8,128)(2,1)}, u32[]{:S(2)}) copy-start(bf16[1,2304,432]{1,2,0:T(8,128)(2,1)} %param.25) | copy-start | bytes 5971972
  137.4 5.0 %copy-start.10 = (s32[128]{0:T(128)S(1)}, s32[128]{0:T(128)}, u32[]{:S(2)}) copy-start(s32[128]{0:T(128)} %param.24) | copy-start | bytes 1540
  140.3 54.9 %collective-permute-start.1 = (bf16[768,2,576]{0,2,1:T(8,128)(2,1)}, bf16[768,2,576]{0,2,1:T(8,128)(2,1)}, u32[]{:S(2)}, u32[]{:S(2)}) collective-permute-start(bf16[768,2,576]{0,2,1:T(8,128)(2,1)} %dynamic-slice_bitcast_fusion), channel_id=1, source_target_pairs={{0,1},{1,0},{2,3},{3,2},{4,5},{5,4},{6,7},{7,6},{8,9},{9,8},{10,11... | collective-permute-start | bytes 5308424 | tf_op jit(solution)/shard_map/ppermute | solution.py:121
  207.3 4.0 copy-start.1
  243.4 8.1 %copy-start.7 = (f32[2,8,2]{1,2,0:T(2,128)S(1)}, f32[2,8,2]{1,2,0:T(2,128)}, u32[]{:S(2)}) copy-start(f32[2,8,2]{1,2,0:T(2,128)} %param.22) | copy-start | bytes 388
  243.4 8.2 %copy-start.8 = (s32[1,16]{1,0:T(1,128)S(1)}, s32[1,16]{1,0:T(1,128)}, u32[]{:S(2)}) copy-start(s32[1,16]{1,0:T(1,128)} %param.18) | copy-start | bytes 196
  243.4 8.4 %copy-start.5 = (bf16[2,8,576]{2,1,0:T(8,128)(2,1)S(1)}, bf16[2,8,576]{2,1,0:T(8,128)(2,1)}, u32[]{:S(2)}) copy-start(bf16[2,8,576]{2,1,0:T(8,128)(2,1)} %param.13) | copy-start | bytes 55300
  243.4 8.5 %copy-start.6 = (bf16[2,8,576]{2,1,0:T(8,128)(2,1)S(1)}, bf16[2,8,576]{2,1,0:T(8,128)(2,1)}, u32[]{:S(2)}) copy-start(bf16[2,8,576]{2,1,0:T(8,128)(2,1)} %param.14) | copy-start | bytes 55300
  243.4 9.1 %copy-start.4 = (bf16[2,8,576]{2,1,0:T(8,128)(2,1)S(1)}, bf16[2,8,576]{2,1,0:T(8,128)(2,1)}, u32[]{:S(2)}) copy-start(bf16[2,8,576]{2,1,0:T(8,128)(2,1)} %param.15) | copy-start | bytes 55300
  243.4 96.4 %all-to-all-start.2 = ((bf16[128,2,7344]{2,1,0:T(2,128)(2,1)}), bf16[128,2,7344]{2,1,0:T(2,128)(2,1)}, u32[]{:S(2)}, u32[]{:S(2)}) async-start(bf16[128,2,7344]{2,1,0:T(2,128)(2,1)} %reshape.304), calls=%async_computation.2 | async-start | bytes 7602176 | tf_op jit(solution)/shard_map/all_to_all | solution.py:125
  380.7 10.6 %copy-start.9 = (bf16[256,576]{0,1:T(8,128)(2,1)S(1)}, bf16[256,576]{0,1:T(8,128)(2,1)}, u32[]{:S(2)}) copy-start(bf16[256,576]{0,1:T(8,128)(2,1)} %param.17) | copy-start | bytes 884740
  383.3 8.2 %copy-start.3 = (bf16[2,8,2304]{2,1,0:T(8,128)(2,1)S(1)}, bf16[2,8,2304]{2,1,0:T(8,128)(2,1)}, u32[]{:S(2)}) copy-start(bf16[2,8,2304]{2,1,0:T(8,128)(2,1)} %param.19) | copy-start | bytes 221188
  387.8 15.3 %collective-permute-start.2 = (f32[16,576]{1,0:T(8,128)S(1)}, f32[16,576]{1,0:T(8,128)S(1)}, u32[]{:S(2)}, u32[]{:S(2)}) collective-permute-start(f32[16,576]{1,0:T(8,128)S(1)} %dynamic-slice_bitcast_fusion.1), channel_id=1, source_target_pairs={{0,2},{2,0},{1,3},{3,1},{4,6},{6,4},{5,7},{7,5},{8,10},{10,8},{9,1... | collective-permute-start | bytes 110600 | tf_op jit(solution)/shard_map/ppermute | solution.py:139

commit v4 on v3

--- a/solution.py
+++ b/solution.py
@@ -120,13 +120,16 @@
     send = lax.dynamic_index_in_dim(part, 1 - core, 2, keepdims=False)
     got = lax.ppermute(send, "tp", CORE_PAIRS)
     pair_sum = (keep.astype(jnp.float32) + got.astype(jnp.float32)).astype(jnp.bfloat16)
+    piece_rows, piece_lanes = extra.shape[1:]
     pair_sum = pair_sum.reshape(nreq, slots * half)
-    sending = extra.reshape(nreq, -1)
+    pair_sum = jnp.pad(pair_sum, ((0, 0), (0, piece_rows * piece_lanes - slots * half)))
+    pair_sum = pair_sum.reshape(nreq, piece_rows, piece_lanes)
     both = lax.all_to_all(
-        jnp.concatenate([pair_sum, sending], axis=1), "req", split_axis=0, concat_axis=0, tiled=True
-    )
-    returned = both[:, : slots * half].reshape(nreq * slots, 2, quarter)
-    collected = both[:, slots * half :]
+        jnp.concatenate([extra, pair_sum], axis=1), "req", split_axis=0, concat_axis=0, tiled=True
+    )
+    collected = both[:, :piece_rows]
+    returned = both[:, piece_rows:].reshape(nreq, piece_rows * piece_lanes)[:, : slots * half]
+    returned = returned.reshape(nreq * slots, 2, quarter)
     picked = (
         returned[slot.reshape(-1)]
         .astype(jnp.float32)
@@ -145,8 +148,8 @@
     nreq = lax.axis_size("req")
     shard_count = EXPERTS * max(1, nreq // 16)
     _, width, columns = old_weights.shape
-    piece = width // nreq
-    pieces = old_weights.reshape(nreq, piece, columns)
+    piece = width * columns // nreq
+    pieces = old_weights.reshape(nreq, 16, piece // 16)
     spread = lax.all_to_all(pieces, "req", split_axis=0, concat_axis=0, tiled=True)
     devices = jnp.arange(nreq, dtype=jnp.int32)
     shard_ids = jnp.arange(shard_count, dtype=jnp.int32)

time: 408 us -> 339 us (0.83)
  local copies, waits for them, and re-layouts: 123 us -> 80.2 us
  waiting for transfers between devices: 134 us -> 120 us
  other arithmetic: 32.9 us -> 21.8 us
    unnamed x28 -> x23, local copies, waits for them, and re-layouts: 43.3 us -> 7.23 us
    all_to_all x1, waiting for transfers between devices: 47.1 us -> 24.8 us  [migrate(): lax.all_to_all(pieces, 'req', split_axis=0, concat_axis=0, tiled=True)]
    all_to_all x2 -> x0, local copies, waits for them, and re-layouts: 15.9 us -> none  [expert_routed(): lax.all_to_all(jnp.concatenate([pair_sum, sending], axis=1), 'req', split...]
    all_to_all x2 -> x0, other arithmetic: 15.6 us -> none  [expert_routed(): lax.all_to_all(jnp.concatenate([pair_sum, sending], axis=1), 'req', split...]
    reshape x2 -> x4, local copies, waits for them, and re-layouts: 7.86 us -> 21.7 us  [the longest x1 8.57 us: migrate(): pieces = old_weights.reshape(nreq, 16, piece // 16)]
    all_to_all x1, waiting for transfers between devices: 87 us -> 95 us  [expert_routed(): lax.all_to_all(jnp.concatenate([extra, pair_sum], axis=1), 'req', split_a...]
    concatenate x0 -> x1, other arithmetic: none -> 4.43 us  [expert_routed(): jnp.concatenate([extra, pair_sum], axis=1)]
    slice x4 -> x3, local copies, waits for them, and re-layouts: 9.86 us -> 5.49 us  [the longest x1 4.02 us: expert_routed(): collected = both[:, :piece_rows]]
  transfers between devices with their start and end apart: 5 -> 5, of which waited for: 2 -> 2; matrix products, arithmetic and copies ran while one was open for 14% -> 16% of each run, Pallas kernels for 0% -> 0%
where the time goes in v4:
time: 339 us; the launch traced here: 335 us
  waiting for transfers between devices  120 us (35%)
  local copies, waits for them, and re-layouts  80.2 us (24%)
  blocking collectives  79.9 us (24%)
  starting transfers between devices  24.8 us (7%)
  other arithmetic  21.8 us (6%)
  matrix products  7.6 us (2%)
    all_to_all x1, waiting for transfers between devices, expert_routed(): lax.all_to_all(jnp.concatenate([extra, pair_sum], axis=1), 'req', split_a...  95 us
    all_to_all x1, blocking collectives, expert_routed(): lax.all_to_all(outgoing, 'req', split_axis=0, concat_axis=0, tiled=True)  79.9 us
    all_to_all x1, waiting for transfers between devices, migrate(): lax.all_to_all(pieces, 'req', split_axis=0, concat_axis=0, tiled=True)  24.8 us
    reshape x1, local copies, waits for them, and re-layouts, migrate(): pieces = old_weights.reshape(nreq, 16, piece // 16)  8.57 us
    all_to_all x1, starting transfers between devices, expert_routed(): lax.all_to_all(jnp.concatenate([extra, pair_sum], axis=1), 'req', split_a...  7.75 us
    all_to_all x1, starting transfers between devices, migrate(): lax.all_to_all(pieces, 'req', split_axis=0, concat_axis=0, tiled=True)  7.52 us
    unnamed x23, local copies, waits for them, and re-layouts  7.23 us
  transfers between devices with their start and end apart: 5, of which 2 were waited for; matrix products, arithmetic and copies ran while one was open for 16% of the time, Pallas kernels for 0%

profile of v4, /device:TPU:1, one launch (start us, length us, event | category | flops | bytes accessed | tf_op | source)
XLA Modules:
  0.0 335.2 jit_solution(3959167274492174550)
XLA Ops:
  8.3 1.7 reshape.270
  10.0 79.9 %all_to_all.15 = bf16[128,6,1152]{2,1,0:T(8,128)(2,1)S(1)} all-to-all(bf16[128,6,1152]{2,1,0:T(8,128)(2,1)} %reshape.270), channel_id=1, replica_groups=mesh['req'=128,'tp'=4] {'req'}, dimensions={0} | all-to-all | bytes 3538944 | tf_op jit(solution)/shard_map/all_to_all | solution.py:103
  91.4 4.6 %collective-permute-start = (bf16[128,6,1152]{2,0,1:T(8,128)(2,1)}, bf16[128,6,1152]{2,0,1:T(8,128)(2,1)}, u32[]{:S(2)}, u32[]{:S(2)}) collective-permute-start(bf16[128,6,1152]{2,0,1:T(8,128)(2,1)} %copy.57), channel_id=1, source_target_pairs={{0,1},{1,0},{2,3},{3,2},{4,5},{5,4},{6,7},{7,6},{8,9},{9,8},{10,11... | collective-permute-start | bytes 5308424 | tf_op jit(solution)/shard_map/ppermute | solution.py:104
  96.1 4.1 %copy.55 = bf16[1,2304,432]{2,1,0:T(8,128)(2,1)} copy(bf16[1,2304,432]{1,2,0:T(8,128)(2,1)} %param.25) | data formatting | bytes 3981312 | tf_op args[12]
  100.2 8.6 %reshape.267 = bf16[128,16,486]{2,1,0:T(8,128)(2,1)} reshape(bf16[1,2304,432]{2,1,0:T(8,128)(2,1)} %copy.55) | data formatting | bytes 3981312 | tf_op jit(solution)/shard_map/reshape | solution.py:152
  108.7 7.5 %all-to-all-start = ((bf16[128,16,486]{2,1,0:T(8,128)(2,1)}), bf16[128,16,486]{2,1,0:T(8,128)(2,1)}, u32[]{:S(2)}, u32[]{:S(2)}) async-start(bf16[128,16,486]{2,1,0:T(8,128)(2,1)} %reshape.267), calls=%async_computation | async-start | bytes 4194304 | tf_op jit(solution)/shard_map/all_to_all | solution.py:153
  116.3 2.7 copy_select_fusion.1
  119.0 3.1 pad_maximum_fusion
  122.1 6.7 %reshape.271 = bf16[768,2304]{1,0:T(8,128)(2,1)} reshape(bf16[128,6,2304]{2,1,0:T(8,128)(2,1)} %pad_maximum_fusion) | data formatting | bytes 7077888 | tf_op jit(solution)/shard_map/reshape | solution.py:107
  128.8 3.2 fusion.1
  132.1 3.0 convolution_convert_fusion
  135.0 5.7 %copy.60 = bf16[768,2304]{0,1:T(8,128)(2,1)} copy(bf16[768,2304]{1,0:T(8,128)(2,1)} %convolution_convert_fusion) | data formatting | bytes 7077888 | tf_op jit(solution)/shard_map/convert_element_type | solution.py:117
  140.8 2.8 dynamic-slice_bitcast_fusion
  143.6 1.9 collective-permute-start.1
  145.6 24.8 %all-to-all-done = bf16[128,16,486]{2,1,0:T(8,128)(2,1)} async-done(((bf16[128,16,486]{2,1,0:T(8,128)(2,1)}), bf16[128,16,486]{2,1,0:T(8,128)(2,1)}, u32[]{:S(2)}, u32[]{:S(2)}) %all-to-all-start) | async-done | bytes 1990688 | tf_op jit(solution)/shard_map/all_to_all | solution.py:153
  170.5 2.3 gather_fusion
  172.8 3.7 %fusion = bf16[768,2,576]{0,2,1:T(8,128)(2,1)} fusion(bf16[768,2,576]{0,2,1:T(8,128)(2,1)} %collective-permute-done.1, bf16[768,2,2,576]{0,3,2,1:T(8,128)(2,1)} %bitcast.63, s32[]{:T(128)S(6)} %select_n.113), kind=kLoop, calls=%fused_computation.6 | loop fusion | flops 3538944 | bytes 5308420 | tf_op jit(solution)/shard_map/convert_element_type | solution.py:122
  176.4 6.5 %copy.61 = bf16[768,2,576]{2,1,0:T(2,128)(2,1)} copy(bf16[768,2,576]{0,2,1:T(8,128)(2,1)} %fusion) | data formatting | bytes 3538944 | tf_op jit(solution)/shard_map/convert_element_type | solution.py:122
  183.0 5.2 %reshape.273 = bf16[128,6912]{1,0:T(8,128)(2,1)} reshape(bf16[768,2,576]{2,1,0:T(2,128)(2,1)} %copy.61) | data formatting | bytes 3538944 | tf_op jit(solution)/shard_map/reshape | solution.py:124
  188.2 2.9 pad.4
  191.1 6.5 %reshape.304 = bf16[128,16,486]{2,1,0:T(8,128)(2,1)} reshape(bf16[128,7776]{1,0:T(8,128)(2,1)} %pad.4) | data formatting | bytes 3981312 | tf_op jit(solution)/shard_map/reshape | solution.py:126
  197.5 4.4 %pad_maximum_fusion.1 = bf16[128,32,486]{2,1,0:T(8,128)(2,1)} fusion(bf16[128,16,486]{2,1,0:T(8,128)(2,1)} %reshape.304, bf16[128,16,486]{2,1,0:T(8,128)(2,1)S(1)} %gather_fusion), kind=kLoop, calls=%fused_computation.4 | loop fusion | flops 7962624 | bytes 7962624 | tf_op jit(solution)/shard_map/concatenate | solution.py:128
  202.0 7.7 %all-to-all-start.2 = ((bf16[128,32,486]{2,1,0:T(8,128)(2,1)}), bf16[128,32,486]{2,1,0:T(8,128)(2,1)}, u32[]{:S(2)}, u32[]{:S(2)}) async-start(bf16[128,32,486]{2,1,0:T(8,128)(2,1)} %pad_maximum_fusion.1), calls=%async_computation.2 | async-start | bytes 8388608 | tf_op jit(solution)/shard_map/all_to_all | solution.py:127
  211.3 95.0 %all-to-all-done.2 = bf16[128,32,486]{2,1,0:T(8,128)(2,1)} async-done(((bf16[128,32,486]{2,1,0:T(8,128)(2,1)}), bf16[128,32,486]{2,1,0:T(8,128)(2,1)}, u32[]{:S(2)}, u32[]{:S(2)}) %all-to-all-start.2) | async-done | bytes 3981344 | tf_op jit(solution)/shard_map/all_to_all | solution.py:127
  306.3 4.0 %fusion.32 = (bf16[128,16,486]{2,1,0:T(8,128)(2,1)}, bf16[128,16,486]{2,1,0:T(8,128)(2,1)S(1)}) fusion(bf16[128,32,486]{2,1,0:T(8,128)(2,1)} %all-to-all-done.2), kind=kLoop, calls=%fused_computation.84 | loop fusion | bytes 7962624 | tf_op jit(solution)/shard_map/slice | solution.py:130
  310.3 4.0 %reshape.305 = bf16[128,7776]{1,0:T(8,128)(2,1)} reshape(bf16[128,16,486]{2,1,0:T(8,128)(2,1)S(1)} %get-tuple-element.15) | data formatting | bytes 3981312 | tf_op jit(solution)/shard_map/reshape | solution.py:131
  314.4 1.5 slice-done
  315.8 2.6 reshape.276
  318.5 3.6 %gather_fusion.1 = bf16[256,2,576]{2,1,0:T(2,128)(2,1)S(1)} fusion(bf16[768,2,576]{2,1,0:T(2,128)(2,1)} %reshape.276, s32[1024]{0:T(1024)S(1)} %pad_clamp_fusion), kind=kCustom, calls=%fused_computation.1 | custom fusion | bytes 1180672 | tf_op jit(solution)/shard_map/gather | solution.py:134
  323.0 2.9 collective-permute-start.2
  327.0 5.2 %reshape.279 = bf16[1,2304,432]{2,1,0:T(8,128)(2,1)S(1)} reshape(bf16[128,16,486]{2,1,0:T(8,128)(2,1)} %get-tuple-element.14) | data formatting | bytes 3981312 | tf_op jit(solution)/shard_map/reshape | solution.py:185
  332.2 2.3 copy.67
  (74 shorter events, 13.1 us)
Async XLA Ops:
  0.6 210.1 %copy-start = (bf16[256,576]{0,1:T(8,128)(2,1)S(1)}, bf16[256,576]{0,1:T(8,128)(2,1)}, u32[]{:S(2)}) copy-start(bf16[256,576]{0,1:T(8,128)(2,1)} %param.16) | copy-start | bytes 884740
  91.4 24.9 %collective-permute-start = (bf16[128,6,1152]{2,0,1:T(8,128)(2,1)}, bf16[128,6,1152]{2,0,1:T(8,128)(2,1)}, u32[]{:S(2)}, u32[]{:S(2)}) collective-permute-start(bf16[128,6,1152]{2,0,1:T(8,128)(2,1)} %copy.57), channel_id=1, source_target_pairs={{0,1},{1,0},{2,3},{3,2},{4,5},{5,4},{6,7},{7,6},{8,9},{9,8},{10,11... | collective-permute-start | bytes 5308424 | tf_op jit(solution)/shard_map/ppermute | solution.py:104
  108.7 61.7 %all-to-all-start = ((bf16[128,16,486]{2,1,0:T(8,128)(2,1)}), bf16[128,16,486]{2,1,0:T(8,128)(2,1)}, u32[]{:S(2)}, u32[]{:S(2)}) async-start(bf16[128,16,486]{2,1,0:T(8,128)(2,1)} %reshape.267), calls=%async_computation | async-start | bytes 4194304 | tf_op jit(solution)/shard_map/all_to_all | solution.py:153
  122.1 6.7 %copy-start.1 = (bf16[1,2304,432]{1,2,0:T(8,128)(2,1)S(1)}, bf16[1,2304,432]{1,2,0:T(8,128)(2,1)}, u32[]{:S(2)}) copy-start(bf16[1,2304,432]{1,2,0:T(8,128)(2,1)} %param.25) | copy-start | bytes 5971972
  140.8 4.7 %copy-start.9 = (s32[128]{0:T(128)S(1)}, s32[128]{0:T(128)}, u32[]{:S(2)}) copy-start(s32[128]{0:T(128)} %param.24) | copy-start | bytes 1540
  143.6 29.2 %collective-permute-start.1 = (bf16[768,2,576]{0,2,1:T(8,128)(2,1)}, bf16[768,2,576]{0,2,1:T(8,128)(2,1)}, u32[]{:S(2)}, u32[]{:S(2)}) collective-permute-start(bf16[768,2,576]{0,2,1:T(8,128)(2,1)} %dynamic-slice_bitcast_fusion), channel_id=1, source_target_pairs={{0,1},{1,0},{2,3},{3,2},{4,5},{5,4},{6,7},{7,6},{8,9},{9,8},{10,11... | collective-permute-start | bytes 5308424 | tf_op jit(solution)/shard_map/ppermute | solution.py:121
  202.0 7.9 %copy-start.6 = (f32[2,8,2]{1,2,0:T(2,128)S(1)}, f32[2,8,2]{1,2,0:T(2,128)}, u32[]{:S(2)}) copy-start(f32[2,8,2]{1,2,0:T(2,128)} %param.22) | copy-start | bytes 388
  202.0 8.0 %copy-start.7 = (s32[1,16]{1,0:T(1,128)S(1)}, s32[1,16]{1,0:T(1,128)}, u32[]{:S(2)}) copy-start(s32[1,16]{1,0:T(1,128)} %param.18) | copy-start | bytes 196
  202.0 8.2 %copy-start.4 = (bf16[2,8,576]{2,1,0:T(8,128)(2,1)S(1)}, bf16[2,8,576]{2,1,0:T(8,128)(2,1)}, u32[]{:S(2)}) copy-start(bf16[2,8,576]{2,1,0:T(8,128)(2,1)} %param.13) | copy-start | bytes 55300
  202.0 8.3 %copy-start.5 = (bf16[2,8,576]{2,1,0:T(8,128)(2,1)S(1)}, bf16[2,8,576]{2,1,0:T(8,128)(2,1)}, u32[]{:S(2)}) copy-start(bf16[2,8,576]{2,1,0:T(8,128)(2,1)} %param.14) | copy-start | bytes 55300
  202.0 9.0 %copy-start.3 = (bf16[2,8,576]{2,1,0:T(8,128)(2,1)S(1)}, bf16[2,8,576]{2,1,0:T(8,128)(2,1)}, u32[]{:S(2)}) copy-start(bf16[2,8,576]{2,1,0:T(8,128)(2,1)} %param.15) | copy-start | bytes 55300
  202.0 104.3 %all-to-all-start.2 = ((bf16[128,32,486]{2,1,0:T(8,128)(2,1)}), bf16[128,32,486]{2,1,0:T(8,128)(2,1)}, u32[]{:S(2)}, u32[]{:S(2)}) async-start(bf16[128,32,486]{2,1,0:T(8,128)(2,1)} %pad_maximum_fusion.1), calls=%async_computation.2 | async-start | bytes 8388608 | tf_op jit(solution)/shard_map/all_to_all | solution.py:127
  314.4 1.5 slice-start
  318.5 7.5 %copy-start.8 = (bf16[256,576]{0,1:T(8,128)(2,1)S(1)}, bf16[256,576]{0,1:T(8,128)(2,1)}, u32[]{:S(2)}) copy-start(bf16[256,576]{0,1:T(8,128)(2,1)} %param.17) | copy-start | bytes 884740
  318.5 7.8 %copy-start.2 = (bf16[2,8,2304]{2,1,0:T(8,128)(2,1)S(1)}, bf16[2,8,2304]{2,1,0:T(8,128)(2,1)}, u32[]{:S(2)}) copy-start(bf16[2,8,2304]{2,1,0:T(8,128)(2,1)} %param.19) | copy-start | bytes 221188
  323.0 11.6 %collective-permute-start.2 = (f32[16,576]{1,0:T(8,128)S(1)}, f32[16,576]{1,0:T(8,128)S(1)}, u32[]{:S(2)}, u32[]{:S(2)}) collective-permute-start(f32[16,576]{1,0:T(8,128)S(1)} %dynamic-slice_bitcast_fusion.1), channel_id=1, source_target_pairs={{0,2},{2,0},{1,3},{3,1},{4,6},{6,4},{5,7},{7,5},{8,10},{10,8},{9,1... | collective-permute-start | bytes 110600 | tf_op jit(solution)/shard_map/ppermute | solution.py:142

commit v5 on v4

--- a/solution.py
+++ b/solution.py
@@ -6,6 +6,7 @@
 HEAD_SIZE = 64
 EXPERTS = 8
 CAP = 3
+MIG_LANES = 1152
 
 
 def attend(queries, new_keys, new_values, cache_keys, cache_values, lengths):
@@ -120,16 +121,13 @@
     send = lax.dynamic_index_in_dim(part, 1 - core, 2, keepdims=False)
     got = lax.ppermute(send, "tp", CORE_PAIRS)
     pair_sum = (keep.astype(jnp.float32) + got.astype(jnp.float32)).astype(jnp.bfloat16)
-    piece_rows, piece_lanes = extra.shape[1:]
-    pair_sum = pair_sum.reshape(nreq, slots * half)
-    pair_sum = jnp.pad(pair_sum, ((0, 0), (0, piece_rows * piece_lanes - slots * half)))
-    pair_sum = pair_sum.reshape(nreq, piece_rows, piece_lanes)
+    pair_sum = pair_sum.reshape(nreq, slots, half)
+    piece_rows = extra.shape[1]
     both = lax.all_to_all(
         jnp.concatenate([extra, pair_sum], axis=1), "req", split_axis=0, concat_axis=0, tiled=True
     )
     collected = both[:, :piece_rows]
-    returned = both[:, piece_rows:].reshape(nreq, piece_rows * piece_lanes)[:, : slots * half]
-    returned = returned.reshape(nreq * slots, 2, quarter)
+    returned = both[:, piece_rows:].reshape(nreq * slots, 2, quarter)
     picked = (
         returned[slot.reshape(-1)]
         .astype(jnp.float32)
@@ -149,7 +147,10 @@
     shard_count = EXPERTS * max(1, nreq // 16)
     _, width, columns = old_weights.shape
     piece = width * columns // nreq
-    pieces = old_weights.reshape(nreq, 16, piece // 16)
+    piece_rows = -(-piece // MIG_LANES)
+    pieces = jnp.swapaxes(old_weights, 1, 2).reshape(nreq, piece)
+    pieces = jnp.pad(pieces, ((0, 0), (0, piece_rows * MIG_LANES - piece)))
+    pieces = pieces.reshape(nreq, piece_rows, MIG_LANES)
     spread = lax.all_to_all(pieces, "req", split_axis=0, concat_axis=0, tiled=True)
     devices = jnp.arange(nreq, dtype=jnp.int32)
     shard_ids = jnp.arange(shard_count, dtype=jnp.int32)
@@ -182,7 +183,10 @@
     layer_out, collected = expert_routed(
         hidden, expert_ids, route_weights, old_place, old_weights[0], gain, sending
     )
-    moved = collected.reshape(old_weights.shape)
+    shard_size = old_weights.shape[1] * old_weights.shape[2]
+    moved = collected.reshape(collected.shape[0], -1)[:, : shard_size // collected.shape[0]]
+    moved = moved.reshape(1, old_weights.shape[2], old_weights.shape[1])
+    moved = jnp.swapaxes(moved, 1, 2)
     return (context, layer_out, moved)
 
 

time: 339 us -> 355 us (1.047)
  waiting for transfers between devices: 120 us -> 137 us
    all_to_all x1, waiting for transfers between devices: 95 us -> 106 us  [expert_routed(): lax.all_to_all(jnp.concatenate([extra, pair_sum], axis=1), 'req', split_a...]
    reshape x6 -> x5, local copies, waits for them, and re-layouts: 32.1 us -> 24.1 us  [the longest x1 6.08 us: migrate(): pieces = jnp.swapaxes(old_weights, 1, 2).reshape(nreq, piece)]
    slice x2 -> x3, local copies, waits for them, and re-layouts: 1.48 us -> 8.87 us  [the longest x2 5.84 us: on_device(): collected.reshape(collected.shape[0], -1)]
    all_to_all x1, waiting for transfers between devices: 24.8 us -> 30.5 us  [migrate(): lax.all_to_all(pieces, 'req', split_axis=0, concat_axis=0, tiled=True)]
    unnamed x23 -> x22, local copies, waits for them, and re-layouts: 7.23 us -> 4.78 us
  transfers between devices with their start and end apart: 5 -> 5, of which waited for: 2 -> 2; matrix products, arithmetic and copies ran while one was open for 16% -> 19% of each run, Pallas kernels for 0% -> 0%
where the time goes in v5:
time: 355 us; the launch traced here: 351 us
  waiting for transfers between devices  137 us (39%)
  blocking collectives  79.9 us (23%)
  local copies, waits for them, and re-layouts  78.2 us (22%)
  starting transfers between devices  24.8 us (7%)
  other arithmetic  22.8 us (6%)
  matrix products  7.59 us (2%)
    all_to_all x1, waiting for transfers between devices, expert_routed(): lax.all_to_all(jnp.concatenate([extra, pair_sum], axis=1), 'req', split_a...  106 us
    all_to_all x1, blocking collectives, expert_routed(): lax.all_to_all(outgoing, 'req', split_axis=0, concat_axis=0, tiled=True)  79.9 us
    all_to_all x1, waiting for transfers between devices, migrate(): lax.all_to_all(pieces, 'req', split_axis=0, concat_axis=0, tiled=True)  30.5 us
    all_to_all x1, starting transfers between devices, expert_routed(): lax.all_to_all(jnp.concatenate([extra, pair_sum], axis=1), 'req', split_a...  7.71 us
    all_to_all x1, starting transfers between devices, migrate(): lax.all_to_all(pieces, 'req', split_axis=0, concat_axis=0, tiled=True)  7.46 us
  transfers between devices with their start and end apart: 5, of which 2 were waited for; matrix products, arithmetic and copies ran while one was open for 19% of the time, Pallas kernels for 0%

profile of v5, /device:TPU:1, one launch (start us, length us, event | category | flops | bytes accessed | tf_op | source)
XLA Modules:
  0.0 351.0 jit_solution(9661269245523167279)
XLA Ops:
  10.0 79.9 %all_to_all.15 = bf16[128,6,1152]{2,1,0:T(8,128)(2,1)S(1)} all-to-all(bf16[128,6,1152]{2,1,0:T(8,128)(2,1)} %reshape.271), channel_id=1, replica_groups=mesh['req'=128,'tp'=4] {'req'}, dimensions={0} | all-to-all | bytes 3538944 | tf_op jit(solution)/shard_map/all_to_all | solution.py:104
  91.4 4.6 %collective-permute-start = (bf16[128,6,1152]{2,0,1:T(8,128)(2,1)}, bf16[128,6,1152]{2,0,1:T(8,128)(2,1)}, u32[]{:S(2)}, u32[]{:S(2)}) collective-permute-start(bf16[128,6,1152]{2,0,1:T(8,128)(2,1)} %copy.66), channel_id=1, source_target_pairs={{0,1},{1,0},{2,3},{3,2},{4,5},{5,4},{6,7},{7,6},{8,9},{9,8},{10,11... | collective-permute-start | bytes 5308424 | tf_op jit(solution)/shard_map/ppermute | solution.py:105
  96.1 6.1 %reshape.267 = bf16[128,7776]{1,0:T(8,128)(2,1)} reshape(bf16[1,432,2304]{2,1,0:T(8,128)(2,1)} %bitcast.70) | data formatting | bytes 3981312 | tf_op jit(solution)/shard_map/reshape | solution.py:151
  102.1 4.0 %copy.87 = bf16[128,7776]{0,1:T(8,128)(2,1)} copy(bf16[128,7776]{1,0:T(8,128)(2,1)} %reshape.267) | data formatting | bytes 3981312
  106.1 3.0 pad.4.clone
  109.1 4.4 %copy.64 = bf16[128,7,1152]{2,1,0:T(8,128)(2,1)} copy(bf16[128,7,1152]{0,2,1:T(8,128)(2,1)} %bitcast.68) | data formatting | bytes 4128768 | tf_op jit(solution)/shard_map/reshape | solution.py:153
  113.5 7.5 %all-to-all-start = ((bf16[128,7,1152]{2,1,0:T(8,128)(2,1)}), bf16[128,7,1152]{2,1,0:T(8,128)(2,1)}, u32[]{:S(2)}, u32[]{:S(2)}) async-start(bf16[128,7,1152]{2,1,0:T(8,128)(2,1)} %copy.64), calls=%async_computation | async-start | bytes 4718592 | tf_op jit(solution)/shard_map/all_to_all | solution.py:154
  121.0 2.7 copy_select_fusion.1
  123.8 3.1 pad_maximum_fusion
  126.8 6.7 %reshape.272 = bf16[768,2304]{1,0:T(8,128)(2,1)} reshape(bf16[128,6,2304]{2,1,0:T(8,128)(2,1)} %pad_maximum_fusion) | data formatting | bytes 7077888 | tf_op jit(solution)/shard_map/reshape | solution.py:108
  133.6 3.2 fusion.1
  136.8 3.0 convolution_convert_fusion
  139.8 5.7 %copy.69 = bf16[768,2304]{0,1:T(8,128)(2,1)} copy(bf16[768,2304]{1,0:T(8,128)(2,1)} %convolution_convert_fusion) | data formatting | bytes 7077888 | tf_op jit(solution)/shard_map/convert_element_type | solution.py:118
  145.5 2.8 dynamic-slice_bitcast_fusion
  148.3 1.9 collective-permute-start.1
  150.4 30.5 %all-to-all-done = bf16[128,7,1152]{2,1,0:T(8,128)(2,1)} async-done(((bf16[128,7,1152]{2,1,0:T(8,128)(2,1)}), bf16[128,7,1152]{2,1,0:T(8,128)(2,1)}, u32[]{:S(2)}, u32[]{:S(2)}) %all-to-all-start) | async-done | bytes 2064416 | tf_op jit(solution)/shard_map/all_to_all | solution.py:154
  180.9 2.6 gather_fusion
  183.5 3.7 %fusion = bf16[768,2,576]{0,2,1:T(8,128)(2,1)} fusion(bf16[768,2,576]{0,2,1:T(8,128)(2,1)} %collective-permute-done.1, bf16[768,2,2,576]{0,3,2,1:T(8,128)(2,1)} %bitcast.67, s32[]{:T(128)S(6)} %select_n.113), kind=kLoop, calls=%fused_computation.6 | loop fusion | flops 3538944 | bytes 5308420 | tf_op jit(solution)/shard_map/convert_element_type | solution.py:123
  187.2 6.5 %copy.70 = bf16[768,2,576]{2,1,0:T(2,128)(2,1)} copy(bf16[768,2,576]{0,2,1:T(8,128)(2,1)} %fusion) | data formatting | bytes 3538944 | tf_op jit(solution)/shard_map/convert_element_type | solution.py:123
  193.7 5.7 %reshape.274 = bf16[128,6,1152]{2,1,0:T(8,128)(2,1)} reshape(bf16[768,2,576]{2,1,0:T(2,128)(2,1)} %copy.70) | data formatting | bytes 3538944 | tf_op jit(solution)/shard_map/reshape | solution.py:124
  199.4 5.5 %pad_maximum_fusion.1 = bf16[128,13,1152]{2,1,0:T(8,128)(2,1)} fusion(bf16[128,6,1152]{2,1,0:T(8,128)(2,1)} %reshape.274, bf16[128,7,1152]{2,1,0:T(8,128)(2,1)S(1)} %gather_fusion), kind=kLoop, calls=%fused_computation.4 | loop fusion | flops 7667712 | bytes 7667712 | tf_op jit(solution)/shard_map/concatenate | solution.py:127
  204.9 7.7 %all-to-all-start.2 = ((bf16[128,13,1152]{2,1,0:T(8,128)(2,1)}), bf16[128,13,1152]{2,1,0:T(8,128)(2,1)}, u32[]{:S(2)}, u32[]{:S(2)}) async-start(bf16[128,13,1152]{2,1,0:T(8,128)(2,1)} %pad_maximum_fusion.1), calls=%async_computation.2 | async-start | bytes 9437184 | tf_op jit(solution)/shard_map/all_to_all | solution.py:126
  214.2 106.2 %all-to-all-done.2 = bf16[128,13,1152]{2,1,0:T(8,128)(2,1)} async-done(((bf16[128,13,1152]{2,1,0:T(8,128)(2,1)}), bf16[128,13,1152]{2,1,0:T(8,128)(2,1)}, u32[]{:S(2)}, u32[]{:S(2)}) %all-to-all-start.2) | async-done | bytes 3833888 | tf_op jit(solution)/shard_map/all_to_all | solution.py:126
  320.4 3.0 slice.36
  323.4 3.2 reshape.275
  326.6 3.6 %gather_fusion.1 = bf16[256,2,576]{2,1,0:T(2,128)(2,1)S(1)} fusion(bf16[768,2,576]{2,1,0:T(2,128)(2,1)} %reshape.275, s32[1024]{0:T(1024)S(1)} %pad_clamp_fusion), kind=kCustom, calls=%fused_computation.1 | custom fusion | bytes 1180672 | tf_op jit(solution)/shard_map/gather | solution.py:132
  331.1 3.0 collective-permute-start.2
  335.2 1.8 slice.37
  337.1 2.7 copy.72
  339.7 3.0 slice.38
  342.7 2.9 copy.73
  345.6 4.7 %reshape.279 = bf16[1,432,2304]{2,1,0:T(8,128)(2,1)} reshape(bf16[128,7776]{1,0:T(8,128)(2,1)S(1)} %copy.73) | data formatting | bytes 3981312 | tf_op jit(solution)/shard_map/reshape | solution.py:188
  (74 shorter events, 14.9 us)
Async XLA Ops:
  0.6 213.0 %copy-start = (bf16[256,576]{0,1:T(8,128)(2,1)S(1)}, bf16[256,576]{0,1:T(8,128)(2,1)}, u32[]{:S(2)}) copy-start(bf16[256,576]{0,1:T(8,128)(2,1)} %param.16) | copy-start | bytes 884740
  91.4 29.6 %collective-permute-start = (bf16[128,6,1152]{2,0,1:T(8,128)(2,1)}, bf16[128,6,1152]{2,0,1:T(8,128)(2,1)}, u32[]{:S(2)}, u32[]{:S(2)}) collective-permute-start(bf16[128,6,1152]{2,0,1:T(8,128)(2,1)} %copy.66), channel_id=1, source_target_pairs={{0,1},{1,0},{2,3},{3,2},{4,5},{5,4},{6,7},{7,6},{8,9},{9,8},{10,11... | collective-permute-start | bytes 5308424 | tf_op jit(solution)/shard_map/ppermute | solution.py:105
  113.5 67.3 %all-to-all-start = ((bf16[128,7,1152]{2,1,0:T(8,128)(2,1)}), bf16[128,7,1152]{2,1,0:T(8,128)(2,1)}, u32[]{:S(2)}, u32[]{:S(2)}) async-start(bf16[128,7,1152]{2,1,0:T(8,128)(2,1)} %copy.64), calls=%async_computation | async-start | bytes 4718592 | tf_op jit(solution)/shard_map/all_to_all | solution.py:154
  126.8 6.7 %copy-start.1 = (bf16[1,2304,432]{1,2,0:T(8,128)(2,1)S(1)}, bf16[1,2304,432]{1,2,0:T(8,128)(2,1)}, u32[]{:S(2)}) copy-start(bf16[1,2304,432]{1,2,0:T(8,128)(2,1)} %param.25) | copy-start | bytes 5971972
  145.5 4.7 %copy-start.9 = (s32[128]{0:T(128)S(1)}, s32[128]{0:T(128)}, u32[]{:S(2)}) copy-start(s32[128]{0:T(128)} %param.24) | copy-start | bytes 1540
  148.3 35.2 %collective-permute-start.1 = (bf16[768,2,576]{0,2,1:T(8,128)(2,1)}, bf16[768,2,576]{0,2,1:T(8,128)(2,1)}, u32[]{:S(2)}, u32[]{:S(2)}) collective-permute-start(bf16[768,2,576]{0,2,1:T(8,128)(2,1)} %dynamic-slice_bitcast_fusion), channel_id=1, source_target_pairs={{0,1},{1,0},{2,3},{3,2},{4,5},{5,4},{6,7},{7,6},{8,9},{9,8},{10,11... | collective-permute-start | bytes 5308424 | tf_op jit(solution)/shard_map/ppermute | solution.py:122
  204.9 7.8 %copy-start.6 = (f32[2,8,2]{1,2,0:T(2,128)S(1)}, f32[2,8,2]{1,2,0:T(2,128)}, u32[]{:S(2)}) copy-start(f32[2,8,2]{1,2,0:T(2,128)} %param.22) | copy-start | bytes 388
  204.9 7.9 %copy-start.7 = (s32[1,16]{1,0:T(1,128)S(1)}, s32[1,16]{1,0:T(1,128)}, u32[]{:S(2)}) copy-start(s32[1,16]{1,0:T(1,128)} %param.18) | copy-start | bytes 196
  204.9 8.2 %copy-start.4 = (bf16[2,8,576]{2,1,0:T(8,128)(2,1)S(1)}, bf16[2,8,576]{2,1,0:T(8,128)(2,1)}, u32[]{:S(2)}) copy-start(bf16[2,8,576]{2,1,0:T(8,128)(2,1)} %param.13) | copy-start | bytes 55300
  204.9 8.3 %copy-start.5 = (bf16[2,8,576]{2,1,0:T(8,128)(2,1)S(1)}, bf16[2,8,576]{2,1,0:T(8,128)(2,1)}, u32[]{:S(2)}) copy-start(bf16[2,8,576]{2,1,0:T(8,128)(2,1)} %param.14) | copy-start | bytes 55300
  204.9 8.9 %copy-start.3 = (bf16[2,8,576]{2,1,0:T(8,128)(2,1)S(1)}, bf16[2,8,576]{2,1,0:T(8,128)(2,1)}, u32[]{:S(2)}) copy-start(bf16[2,8,576]{2,1,0:T(8,128)(2,1)} %param.15) | copy-start | bytes 55300
  204.9 115.4 %all-to-all-start.2 = ((bf16[128,13,1152]{2,1,0:T(8,128)(2,1)}), bf16[128,13,1152]{2,1,0:T(8,128)(2,1)}, u32[]{:S(2)}, u32[]{:S(2)}) async-start(bf16[128,13,1152]{2,1,0:T(8,128)(2,1)} %pad_maximum_fusion.1), calls=%async_computation.2 | async-start | bytes 9437184 | tf_op jit(solution)/shard_map/all_to_all | solution.py:126
  326.6 7.6 %copy-start.8 = (bf16[256,576]{0,1:T(8,128)(2,1)S(1)}, bf16[256,576]{0,1:T(8,128)(2,1)}, u32[]{:S(2)}) copy-start(bf16[256,576]{0,1:T(8,128)(2,1)} %param.17) | copy-start | bytes 884740
  326.6 7.8 %copy-start.2 = (bf16[2,8,2304]{2,1,0:T(8,128)(2,1)S(1)}, bf16[2,8,2304]{2,1,0:T(8,128)(2,1)}, u32[]{:S(2)}) copy-start(bf16[2,8,2304]{2,1,0:T(8,128)(2,1)} %param.19) | copy-start | bytes 221188
  331.1 19.2 %collective-permute-start.2 = (f32[16,576]{1,0:T(8,128)S(1)}, f32[16,576]{1,0:T(8,128)S(1)}, u32[]{:S(2)}, u32[]{:S(2)}) collective-permute-start(f32[16,576]{1,0:T(8,128)S(1)} %dynamic-slice_bitcast_fusion.1), channel_id=1, source_target_pairs={{0,2},{2,0},{1,3},{3,1},{4,6},{6,4},{5,7},{7,5},{8,10},{10,8},{9,1... | collective-permute-start | bytes 110600 | tf_op jit(solution)/shard_map/ppermute | solution.py:140

commit v6 on v4

--- a/solution.py
+++ b/solution.py
@@ -97,14 +97,19 @@
         slot[None, :, :] == jnp.arange(nreq * slots, dtype=jnp.int32)[:, None, None], axis=-1
     )
     repeated = jnp.repeat(normed.reshape(batches * tok_rows, width), topk, axis=0)
-    my_half = lax.dynamic_slice_in_dim(repeated, core * half, half, 1)
-    outgoing = jnp.dot(hits.astype(jnp.bfloat16), my_half, preferred_element_type=jnp.float32)
-    outgoing = outgoing.astype(jnp.bfloat16).reshape(nreq, slots, half)
+    my_quarter = lax.dynamic_slice_in_dim(repeated, tp_index * quarter, quarter, 1)
+    outgoing = jnp.dot(hits.astype(jnp.bfloat16), my_quarter, preferred_element_type=jnp.float32)
+    outgoing = outgoing.astype(jnp.bfloat16).reshape(nreq, slots, quarter)
     received = lax.all_to_all(outgoing, "req", split_axis=0, concat_axis=0, tiled=True)
-    other = lax.ppermute(received, "tp", CORE_PAIRS)
-    low = jnp.where(core == 0, received, other)
-    high = jnp.where(core == 0, other, received)
-    flat_rows = jnp.concatenate([low, high], axis=-1).reshape(nreq * slots, width)
+    z_other = lax.ppermute(received, "tp", Z_PAIRS)
+    own_pair = jnp.stack(
+        [jnp.where(zpos == 0, received, z_other), jnp.where(zpos == 0, z_other, received)]
+    )
+    core_pair = lax.ppermute(own_pair, "tp", CORE_PAIRS)
+    first = jnp.where(core == 0, own_pair, core_pair)
+    second = jnp.where(core == 0, core_pair, own_pair)
+    flat_rows = jnp.concatenate([first[0], second[0], first[1], second[1]], axis=-1)
+    flat_rows = flat_rows.reshape(nreq * slots, width)
     gate_up = jnp.dot(
         flat_rows, shard_weights[:, : 2 * hid_dev], preferred_element_type=jnp.float32
     )

time: 339 us -> 349 us (1.029)
  local copies, waits for them, and re-layouts: 80.2 us -> 103 us
  blocking collectives: 79.9 us -> 57.4 us
  starting transfers between devices: 24.8 us -> 30.3 us
    all_to_all x1, blocking collectives: 79.9 us -> 57.4 us  [expert_routed(): lax.all_to_all(outgoing, 'req', split_axis=0, concat_axis=0, tiled=True)]
    ppermute x1 -> x2, waiting for transfers between devices: 0.01 us -> 17.6 us  [the longest x1 17.6 us: expert_routed(): z_other = lax.ppermute(received, 'tp', Z_PAIRS)]
    concatenate x0 -> x5, local copies, waits for them, and re-layouts: none -> 15.8 us  [expert_routed(): jnp.concatenate([first[0], second[0], first[1], second[1]], axis=-1)]
    all_to_all x1, waiting for transfers between devices: 24.8 us -> 9.46 us  [migrate(): lax.all_to_all(pieces, 'req', split_axis=0, concat_axis=0, tiled=True)]
    reshape x2 -> x1, local copies, waits for them, and re-layouts: 8.46 us -> 0.41 us  [expert_routed(): outgoing = outgoing.astype(jnp.bfloat16).reshape(nreq, slots, quarter)]
    ppermute x0 -> x2, local copies, waits for them, and re-layouts: none -> 6.79 us  [the longest x1 4.88 us: expert_routed(): core_pair = lax.ppermute(own_pair, 'tp', CORE_PAIRS)]
    another operation x1 -> x2, local copies, waits for them, and re-layouts: 0.08 us -> 4.54 us  [the longest x1 4.46 us: expert_routed(): jnp.stack([jnp.where(zpos == 0, received, z_other), jnp.where(zpos == 0,...]
    another operation x2 -> x4, other arithmetic: 0.16 us -> 3.98 us  [the longest x2 3.82 us: expert_routed(): jnp.stack([jnp.where(zpos == 0, received, z_other), jnp.where(zpos == 0,...]
  transfers between devices with their start and end apart: 5 -> 6, of which waited for: 2 -> 3; matrix products, arithmetic and copies ran while one was open for 16% -> 19% of each run, Pallas kernels for 0% -> 0%
where the time goes in v6:
time: 349 us; the launch traced here: 345 us
  waiting for transfers between devices  122 us (35%)
  local copies, waits for them, and re-layouts  103 us (30%)
  blocking collectives  57.4 us (16%)
  starting transfers between devices  30.3 us (9%)
  other arithmetic  22.7 us (7%)
  matrix products  8.92 us (3%)
    all_to_all x1, waiting for transfers between devices, expert_routed(): lax.all_to_all(jnp.concatenate([extra, pair_sum], axis=1), 'req', split_a...  95.1 us
    all_to_all x1, blocking collectives, expert_routed(): lax.all_to_all(outgoing, 'req', split_axis=0, concat_axis=0, tiled=True)  57.4 us
    ppermute x1, waiting for transfers between devices, expert_routed(): z_other = lax.ppermute(received, 'tp', Z_PAIRS)  17.6 us
    concatenate x5, local copies, waits for them, and re-layouts, expert_routed(): jnp.concatenate([first[0], second[0], first[1], second[1]], axis=-1)  15.8 us
    all_to_all x1, waiting for transfers between devices, migrate(): lax.all_to_all(pieces, 'req', split_axis=0, concat_axis=0, tiled=True)  9.46 us
    reshape x1, local copies, waits for them, and re-layouts, migrate(): pieces = old_weights.reshape(nreq, 16, piece // 16)  8.6 us
    unnamed x27, local copies, waits for them, and re-layouts  8.3 us
    all_to_all x1, starting transfers between devices, expert_routed(): lax.all_to_all(jnp.concatenate([extra, pair_sum], axis=1), 'req', split_a...  8.12 us
  transfers between devices with their start and end apart: 6, of which 3 were waited for; matrix products, arithmetic and copies ran while one was open for 19% of the time, Pallas kernels for 0%

profile of v6, /device:TPU:1, one launch (start us, length us, event | category | flops | bytes accessed | tf_op | source)
XLA Modules:
  0.0 345.5 jit_solution(1702658050305854535)
XLA Ops:
  9.2 57.4 %all_to_all.15 = bf16[128,6,576]{2,1,0:T(8,128)(2,1)S(1)} all-to-all(bf16[128,6,576]{2,1,0:T(8,128)(2,1)S(1)} %reshape.276), channel_id=1, replica_groups=mesh['req'=128,'tp'=4] {'req'}, dimensions={0} | all-to-all | bytes 1769472 | tf_op jit(solution)/shard_map/all_to_all | solution.py:103
  68.2 3.1 collective-permute-start
  71.3 17.6 %collective-permute-done = bf16[128,6,576]{0,2,1:T(8,128)(2,1)S(1)} collective-permute-done((bf16[128,6,576]{0,2,1:T(8,128)(2,1)}, bf16[128,6,576]{0,2,1:T(8,128)(2,1)S(1)}, u32[]{:S(2)}, u32[]{:S(2)}) %collective-permute-start) | collective-permute-done | bytes 884768 | tf_op jit(solution)/shard_map/ppermute | solution.py:104
  95.7 4.5 %copy.66 = bf16[2,128,6,576]{1,3,2,0:T(8,128)(2,1)} copy(bf16[2,128,6,576]{3,2,1,0:T(8,128)(2,1)} %pad_maximum_fusion.1) | data formatting | bytes 3538944 | tf_op jit(solution)/shard_map/stack | solution.py:105
  100.2 5.4 %collective-permute-start.1 = (bf16[2,128,6,576]{1,3,2,0:T(8,128)(2,1)}, bf16[2,128,6,576]{1,3,2,0:T(8,128)(2,1)}, u32[]{:S(2)}, u32[]{:S(2)}) collective-permute-start(bf16[2,128,6,576]{1,3,2,0:T(8,128)(2,1)} %copy.66), channel_id=1, source_target_pairs={{0,1},{1,0},{2,3},{3,2},{4,5},{5,4},{6,7},{7,6},{8,9},{9,8},{10,11... | collective-permute-start | bytes 5308424 | tf_op jit(solution)/shard_map/ppermute | solution.py:108
  105.6 4.1 %copy.60 = bf16[1,2304,432]{2,1,0:T(8,128)(2,1)} copy(bf16[1,2304,432]{1,2,0:T(8,128)(2,1)} %param.25) | data formatting | bytes 3981312 | tf_op args[12]
  109.7 8.6 %reshape.273 = bf16[128,16,486]{2,1,0:T(8,128)(2,1)} reshape(bf16[1,2304,432]{2,1,0:T(8,128)(2,1)} %copy.60) | data formatting | bytes 3981312 | tf_op jit(solution)/shard_map/reshape | solution.py:157
  118.3 7.9 %all-to-all-start = ((bf16[128,16,486]{2,1,0:T(8,128)(2,1)}), bf16[128,16,486]{2,1,0:T(8,128)(2,1)}, u32[]{:S(2)}, u32[]{:S(2)}) async-start(bf16[128,16,486]{2,1,0:T(8,128)(2,1)} %reshape.273), calls=%async_computation | async-start | bytes 4194304 | tf_op jit(solution)/shard_map/all_to_all | solution.py:158
  126.3 4.9 %copy.67 = bf16[2,128,6,576]{3,2,1,0:T(8,128)(2,1)} copy(bf16[2,128,6,576]{1,3,2,0:T(8,128)(2,1)} %collective-permute-done.1) | data formatting | bytes 3538944 | tf_op jit(solution)/shard_map/ppermute | solution.py:108
  131.2 2.8 broadcast_select_fusion
  135.9 3.0 concatenate.15
  138.9 3.0 concatenate.16
  144.7 7.0 %concatenate.19 = bf16[768,2304]{1,0:T(8,128)(2,1)} concatenate(bf16[768,576]{1,0:T(8,128)(2,1)S(1)} %copy-done.3, bf16[768,576]{1,0:T(8,128)(2,1)} %concatenate.16, bf16[768,576]{1,0:T(8,128)(2,1)} %concatenate.17, bf16[768,576]{1,0:T(8,128)(2,1)} %concatenate.18), dimensions={1} | concatenate | bytes 7077888 | tf_op jit(solution)/shard_map/concatenate | solution.py:111
  151.7 3.6 %fusion.1 = f32[768,288]{0,1:T(8,128)S(1)} fusion(bf16[768,2304]{1,0:T(8,128)(2,1)} %concatenate.19, bf16[2304,432]{0,1:T(8,128)(2,1)} %bitcast.68), kind=kOutput, calls=%fused_computation.11 | convolution fusion | flops 1019215872 | bytes 5750784 | tf_op jit(solution)/shard_map/dot_general | solution.py:113
  155.3 4.1 %convolution_convert_fusion = bf16[768,2304]{1,0:T(8,128)(2,1)} fusion(bf16[2304,432]{0,1:T(8,128)(2,1)} %bitcast.69, f32[768,288]{0,1:T(8,128)S(1)} %fusion.1), kind=kOutput, calls=%fused_computation.2 | convolution fusion | flops 512040960 | bytes 5087232 | tf_op jit(solution)/shard_map/dot_general | solution.py:117
  159.4 5.7 %copy.69 = bf16[768,2304]{0,1:T(8,128)(2,1)} copy(bf16[768,2304]{1,0:T(8,128)(2,1)} %convolution_convert_fusion) | data formatting | bytes 7077888 | tf_op jit(solution)/shard_map/convert_element_type | solution.py:122
  165.2 2.8 dynamic-slice_bitcast_fusion
  170.3 9.5 %all-to-all-done = bf16[128,16,486]{2,1,0:T(8,128)(2,1)} async-done(((bf16[128,16,486]{2,1,0:T(8,128)(2,1)}), bf16[128,16,486]{2,1,0:T(8,128)(2,1)}, u32[]{:S(2)}, u32[]{:S(2)}) %all-to-all-start) | async-done | bytes 1990688 | tf_op jit(solution)/shard_map/all_to_all | solution.py:158
  182.0 3.7 %fusion = bf16[768,2,576]{0,2,1:T(8,128)(2,1)} fusion(bf16[768,2,576]{0,2,1:T(8,128)(2,1)} %collective-permute-done.2, bf16[768,2,2,576]{0,3,2,1:T(8,128)(2,1)} %bitcast.67, s32[]{:T(128)S(6)} %select_n.126), kind=kLoop, calls=%fused_computation.5 | loop fusion | flops 3538944 | bytes 5308420 | tf_op jit(solution)/shard_map/convert_element_type | solution.py:127
  185.7 6.5 %copy.70 = bf16[768,2,576]{2,1,0:T(2,128)(2,1)} copy(bf16[768,2,576]{0,2,1:T(8,128)(2,1)} %fusion) | data formatting | bytes 3538944 | tf_op jit(solution)/shard_map/convert_element_type | solution.py:127
  192.3 5.2 %reshape.278 = bf16[128,6912]{1,0:T(8,128)(2,1)} reshape(bf16[768,2,576]{2,1,0:T(2,128)(2,1)} %copy.70) | data formatting | bytes 3538944 | tf_op jit(solution)/shard_map/reshape | solution.py:129
  197.5 2.9 pad.4
  200.4 6.5 %reshape.309 = bf16[128,16,486]{2,1,0:T(8,128)(2,1)} reshape(bf16[128,7776]{1,0:T(8,128)(2,1)} %pad.4) | data formatting | bytes 3981312 | tf_op jit(solution)/shard_map/reshape | solution.py:131
  206.8 4.4 %pad_maximum_fusion = bf16[128,32,486]{2,1,0:T(8,128)(2,1)} fusion(bf16[128,16,486]{2,1,0:T(8,128)(2,1)} %reshape.309, bf16[128,16,486]{2,1,0:T(8,128)(2,1)S(1)} %gather_fusion), kind=kLoop, calls=%fused_computation.3 | loop fusion | flops 7962624 | bytes 7962624 | tf_op jit(solution)/shard_map/concatenate | solution.py:133
  211.3 8.1 %all-to-all-start.2 = ((bf16[128,32,486]{2,1,0:T(8,128)(2,1)}), bf16[128,32,486]{2,1,0:T(8,128)(2,1)}, u32[]{:S(2)}, u32[]{:S(2)}) async-start(bf16[128,32,486]{2,1,0:T(8,128)(2,1)} %pad_maximum_fusion), calls=%async_computation.2 | async-start | bytes 8388608 | tf_op jit(solution)/shard_map/all_to_all | solution.py:132
  220.9 95.1 %all-to-all-done.2 = bf16[128,32,486]{2,1,0:T(8,128)(2,1)} async-done(((bf16[128,32,486]{2,1,0:T(8,128)(2,1)}), bf16[128,32,486]{2,1,0:T(8,128)(2,1)}, u32[]{:S(2)}, u32[]{:S(2)}) %all-to-all-start.2) | async-done | bytes 3981344 | tf_op jit(solution)/shard_map/all_to_all | solution.py:132
  316.0 4.0 %fusion.32 = (bf16[128,16,486]{2,1,0:T(8,128)(2,1)}, bf16[128,16,486]{2,1,0:T(8,128)(2,1)S(1)}) fusion(bf16[128,32,486]{2,1,0:T(8,128)(2,1)} %all-to-all-done.2), kind=kLoop, calls=%fused_computation.86 | loop fusion | bytes 7962624 | tf_op jit(solution)/shard_map/slice | solution.py:135
  320.0 4.0 %reshape.310 = bf16[128,7776]{1,0:T(8,128)(2,1)} reshape(bf16[128,16,486]{2,1,0:T(8,128)(2,1)S(1)} %get-tuple-element.17) | data formatting | bytes 3981312 | tf_op jit(solution)/shard_map/reshape | solution.py:136
  325.5 2.6 reshape.281
  328.1 3.6 %gather_fusion.1 = bf16[256,2,576]{2,1,0:T(2,128)(2,1)S(1)} fusion(bf16[768,2,576]{2,1,0:T(2,128)(2,1)} %reshape.281, s32[1024]{0:T(1024)S(1)} %pad_clamp_fusion), kind=kCustom, calls=%fused_computation.1 | custom fusion | bytes 1180672 | tf_op jit(solution)/shard_map/gather | solution.py:139
  332.6 3.5 %collective-permute-start.3 = (f32[16,576]{1,0:T(8,128)S(1)}, f32[16,576]{1,0:T(8,128)S(1)}, u32[]{:S(2)}, u32[]{:S(2)}) collective-permute-start(f32[16,576]{1,0:T(8,128)S(1)} %dynamic-slice_bitcast_fusion.1), channel_id=1, source_target_pairs={{0,2},{2,0},{1,3},{3,1},{4,6},{6,4},{5,7},{7,5},{8,10},{10,8},{9,1... | collective-permute-start | bytes 110600 | tf_op jit(solution)/shard_map/ppermute | solution.py:147
  337.2 5.2 %reshape.284 = bf16[1,2304,432]{2,1,0:T(8,128)(2,1)S(1)} reshape(bf16[128,16,486]{2,1,0:T(8,128)(2,1)} %get-tuple-element.16) | data formatting | bytes 3981312 | tf_op jit(solution)/shard_map/reshape | solution.py:190
  (90 shorter events, 34.0 us)
Async XLA Ops:
  0.6 219.7 %copy-start = (bf16[256,576]{0,1:T(8,128)(2,1)S(1)}, bf16[256,576]{0,1:T(8,128)(2,1)}, u32[]{:S(2)}) copy-start(bf16[256,576]{0,1:T(8,128)(2,1)} %param.16) | copy-start | bytes 884740
  68.2 20.7 %collective-permute-start = (bf16[128,6,576]{0,2,1:T(8,128)(2,1)}, bf16[128,6,576]{0,2,1:T(8,128)(2,1)S(1)}, u32[]{:S(2)}, u32[]{:S(2)}) collective-permute-start(bf16[128,6,576]{0,2,1:T(8,128)(2,1)} %copy.63), channel_id=1, source_target_pairs={{0,2},{2,0},{1,3},{3,1},{4,6},{6,4},{5,7},{7,5},{8,10},{10,8},{9,1... | collective-permute-start | bytes 2654216 | tf_op jit(solution)/shard_map/ppermute | solution.py:104
  92.4 1.1 copy-start.1
  100.2 26.1 %collective-permute-start.1 = (bf16[2,128,6,576]{1,3,2,0:T(8,128)(2,1)}, bf16[2,128,6,576]{1,3,2,0:T(8,128)(2,1)}, u32[]{:S(2)}, u32[]{:S(2)}) collective-permute-start(bf16[2,128,6,576]{1,3,2,0:T(8,128)(2,1)} %copy.66), channel_id=1, source_target_pairs={{0,1},{1,0},{2,3},{3,2},{4,5},{5,4},{6,7},{7,6},{8,9},{9,8},{10,11... | collective-permute-start | bytes 5308424 | tf_op jit(solution)/shard_map/ppermute | solution.py:108
  118.3 61.5 %all-to-all-start = ((bf16[128,16,486]{2,1,0:T(8,128)(2,1)}), bf16[128,16,486]{2,1,0:T(8,128)(2,1)}, u32[]{:S(2)}, u32[]{:S(2)}) async-start(bf16[128,16,486]{2,1,0:T(8,128)(2,1)} %reshape.273), calls=%async_computation | async-start | bytes 4194304 | tf_op jit(solution)/shard_map/all_to_all | solution.py:158
  126.3 4.9 %copy-start.2 = (bf16[1,128,6,576]{3,2,1,0:T(8,128)(2,1)S(1)}, bf16[1,128,6,576]{3,2,1,0:T(8,128)(2,1)}, u32[]{:S(2)}) copy-start(bf16[1,128,6,576]{3,2,1,0:T(8,128)(2,1)} %copy-done.1) | copy-start | bytes 2654212
  143.3 1.4 copy-start.3
  165.2 5.0 %copy-start.11 = (s32[128]{0:T(128)S(1)}, s32[128]{0:T(128)}, u32[]{:S(2)}) copy-start(s32[128]{0:T(128)} %param.24) | copy-start | bytes 1540
  168.0 14.1 %collective-permute-start.2 = (bf16[768,2,576]{0,2,1:T(8,128)(2,1)}, bf16[768,2,576]{0,2,1:T(8,128)(2,1)}, u32[]{:S(2)}, u32[]{:S(2)}) collective-permute-start(bf16[768,2,576]{0,2,1:T(8,128)(2,1)} %dynamic-slice_bitcast_fusion), channel_id=1, source_target_pairs={{0,1},{1,0},{2,3},{3,2},{4,5},{5,4},{6,7},{7,6},{8,9},{9,8},{10,11... | collective-permute-start | bytes 5308424 | tf_op jit(solution)/shard_map/ppermute | solution.py:126
  211.2 8.2 %copy-start.8 = (f32[2,8,2]{1,2,0:T(2,128)S(1)}, f32[2,8,2]{1,2,0:T(2,128)}, u32[]{:S(2)}) copy-start(f32[2,8,2]{1,2,0:T(2,128)} %param.22) | copy-start | bytes 388
  211.3 8.3 %copy-start.9 = (s32[1,16]{1,0:T(1,128)S(1)}, s32[1,16]{1,0:T(1,128)}, u32[]{:S(2)}) copy-start(s32[1,16]{1,0:T(1,128)} %param.18) | copy-start | bytes 196
  211.3 8.6 %copy-start.6 = (bf16[2,8,576]{2,1,0:T(8,128)(2,1)S(1)}, bf16[2,8,576]{2,1,0:T(8,128)(2,1)}, u32[]{:S(2)}) copy-start(bf16[2,8,576]{2,1,0:T(8,128)(2,1)} %param.13) | copy-start | bytes 55300
  211.3 8.7 %copy-start.7 = (bf16[2,8,576]{2,1,0:T(8,128)(2,1)S(1)}, bf16[2,8,576]{2,1,0:T(8,128)(2,1)}, u32[]{:S(2)}) copy-start(bf16[2,8,576]{2,1,0:T(8,128)(2,1)} %param.14) | copy-start | bytes 55300
  211.3 9.3 %copy-start.5 = (bf16[2,8,576]{2,1,0:T(8,128)(2,1)S(1)}, bf16[2,8,576]{2,1,0:T(8,128)(2,1)}, u32[]{:S(2)}) copy-start(bf16[2,8,576]{2,1,0:T(8,128)(2,1)} %param.15) | copy-start | bytes 55300
  211.3 104.7 %all-to-all-start.2 = ((bf16[128,32,486]{2,1,0:T(8,128)(2,1)}), bf16[128,32,486]{2,1,0:T(8,128)(2,1)}, u32[]{:S(2)}, u32[]{:S(2)}) async-start(bf16[128,32,486]{2,1,0:T(8,128)(2,1)} %pad_maximum_fusion), calls=%async_computation.2 | async-start | bytes 8388608 | tf_op jit(solution)/shard_map/all_to_all | solution.py:132
  324.0 1.5 slice-start
  328.1 8.1 %copy-start.10 = (bf16[256,576]{0,1:T(8,128)(2,1)S(1)}, bf16[256,576]{0,1:T(8,128)(2,1)}, u32[]{:S(2)}) copy-start(bf16[256,576]{0,1:T(8,128)(2,1)} %param.17) | copy-start | bytes 884740
  328.1 8.4 %copy-start.4 = (bf16[2,8,2304]{2,1,0:T(8,128)(2,1)S(1)}, bf16[2,8,2304]{2,1,0:T(8,128)(2,1)}, u32[]{:S(2)}) copy-start(bf16[2,8,2304]{2,1,0:T(8,128)(2,1)} %param.19) | copy-start | bytes 221188
  332.6 12.2 %collective-permute-start.3 = (f32[16,576]{1,0:T(8,128)S(1)}, f32[16,576]{1,0:T(8,128)S(1)}, u32[]{:S(2)}, u32[]{:S(2)}) collective-permute-start(f32[16,576]{1,0:T(8,128)S(1)} %dynamic-slice_bitcast_fusion.1), channel_id=1, source_target_pairs={{0,2},{2,0},{1,3},{3,1},{4,6},{6,4},{5,7},{7,5},{8,10},{10,8},{9,1... | collective-permute-start | bytes 110600 | tf_op jit(solution)/shard_map/ppermute | solution.py:147

commit v7 on v4

--- a/solution.py
+++ b/solution.py
@@ -116,14 +116,17 @@
         preferred_element_type=jnp.float32,
     ).astype(jnp.bfloat16)
     part = part.reshape(nreq * slots, 2, 2, quarter)
-    keep = lax.dynamic_index_in_dim(part, core, 2, keepdims=False)
-    send = lax.dynamic_index_in_dim(part, 1 - core, 2, keepdims=False)
+    piece_rows, piece_lanes = extra.shape[1:]
+
+    def to_payload(block):
+        block = block.reshape(nreq, slots * half)
+        block = jnp.pad(block, ((0, 0), (0, piece_rows * piece_lanes - slots * half)))
+        return block.reshape(nreq, piece_rows, piece_lanes)
+
+    keep = to_payload(lax.dynamic_index_in_dim(part, core, 2, keepdims=False))
+    send = to_payload(lax.dynamic_index_in_dim(part, 1 - core, 2, keepdims=False))
     got = lax.ppermute(send, "tp", CORE_PAIRS)
     pair_sum = (keep.astype(jnp.float32) + got.astype(jnp.float32)).astype(jnp.bfloat16)
-    piece_rows, piece_lanes = extra.shape[1:]
-    pair_sum = pair_sum.reshape(nreq, slots * half)
-    pair_sum = jnp.pad(pair_sum, ((0, 0), (0, piece_rows * piece_lanes - slots * half)))
-    pair_sum = pair_sum.reshape(nreq, piece_rows, piece_lanes)
     both = lax.all_to_all(
         jnp.concatenate([extra, pair_sum], axis=1), "req", split_axis=0, concat_axis=0, tiled=True
     )

time: 339 us -> 352 us (1.038)
  local copies, waits for them, and re-layouts: 80.2 us -> 109 us
  waiting for transfers between devices: 120 us -> 98.3 us
  starting transfers between devices: 24.8 us -> 32.4 us
    all_to_all x1, waiting for transfers between devices: 24.8 us -> 2.36 us  [migrate(): lax.all_to_all(pieces, 'req', split_axis=0, concat_axis=0, tiled=True)]
    dynamic_slice x0 -> x3, local copies, waits for them, and re-layouts: none -> 16.4 us  [the longest x2 10.2 us: expert_routed(): lax.dynamic_index_in_dim(part, 1 - core, 2, keepdims=False)]
    concatenate x0 -> x1, local copies, waits for them, and re-layouts: none -> 8.54 us  [expert_routed(): jnp.concatenate([extra, pair_sum], axis=1)]
    all_to_all x1, starting transfers between devices: 7.75 us -> 14.3 us  [expert_routed(): lax.all_to_all(jnp.concatenate([extra, pair_sum], axis=1), 'req', split_a...]
    reshape x2 -> x5, local copies, waits for them, and re-layouts: 11.7 us -> 16.9 us  [the longest x2 9.65 us: to_payload(): return block.reshape(nreq, piece_rows, piece_lanes)]
    gather x1 -> x2, local copies, waits for them, and re-layouts: 2.27 us -> 6.13 us  [migrate(): return spread[needed]]
    unnamed x23 -> x25, local copies, waits for them, and re-layouts: 7.23 us -> 7.23 us
  transfers between devices with their start and end apart: 5 -> 5, of which waited for: 2 -> 2; matrix products, arithmetic and copies ran while one was open for 16% -> 27% of each run, Pallas kernels for 0% -> 0%
where the time goes in v7:
time: 352 us; the launch traced here: 350 us
  local copies, waits for them, and re-layouts  109 us (31%)
  waiting for transfers between devices  98.3 us (28%)
  blocking collectives  79.9 us (23%)
  starting transfers between devices  32.4 us (9%)
  other arithmetic  22.3 us (6%)
  matrix products  7.59 us (2%)
    all_to_all x1, waiting for transfers between devices, expert_routed(): lax.all_to_all(jnp.concatenate([extra, pair_sum], axis=1), 'req', split_a...  95.9 us
    all_to_all x1, blocking collectives, expert_routed(): lax.all_to_all(outgoing, 'req', split_axis=0, concat_axis=0, tiled=True)  79.9 us
    all_to_all x1, starting transfers between devices, expert_routed(): lax.all_to_all(jnp.concatenate([extra, pair_sum], axis=1), 'req', split_a...  14.3 us
    dynamic_slice x2, local copies, waits for them, and re-layouts, expert_routed(): lax.dynamic_index_in_dim(part, 1 - core, 2, keepdims=False)  10.2 us
    reshape x2, local copies, waits for them, and re-layouts, to_payload(): return block.reshape(nreq, piece_rows, piece_lanes)  9.65 us
    reshape x1, local copies, waits for them, and re-layouts, migrate(): pieces = old_weights.reshape(nreq, 16, piece // 16)  8.58 us
    concatenate x1, local copies, waits for them, and re-layouts, expert_routed(): jnp.concatenate([extra, pair_sum], axis=1)  8.54 us
    all_to_all x1, starting transfers between devices, migrate(): lax.all_to_all(pieces, 'req', split_axis=0, concat_axis=0, tiled=True)  7.52 us
  transfers between devices with their start and end apart: 5, of which 2 were waited for; matrix products, arithmetic and copies ran while one was open for 27% of the time, Pallas kernels for 0%

profile of v7, /device:TPU:1, one launch (start us, length us, event | category | flops | bytes accessed | tf_op | source)
XLA Modules:
  0.0 350.1 jit_solution(4026110636850895768)
XLA Ops:
  10.0 79.9 %all_to_all.15 = bf16[128,6,1152]{2,1,0:T(8,128)(2,1)S(1)} all-to-all(bf16[128,6,1152]{2,1,0:T(8,128)(2,1)} %reshape.276), channel_id=1, replica_groups=mesh['req'=128,'tp'=4] {'req'}, dimensions={0} | all-to-all | bytes 3538944 | tf_op jit(solution)/shard_map/all_to_all | solution.py:103
  91.4 4.6 %collective-permute-start = (bf16[128,6,1152]{2,0,1:T(8,128)(2,1)}, bf16[128,6,1152]{2,0,1:T(8,128)(2,1)}, u32[]{:S(2)}, u32[]{:S(2)}) collective-permute-start(bf16[128,6,1152]{2,0,1:T(8,128)(2,1)} %copy.151), channel_id=1, source_target_pairs={{0,1},{1,0},{2,3},{3,2},{4,5},{5,4},{6,7},{7,6},{8,9},{9,8},{10,11... | collective-permute-start | bytes 5308424 | tf_op jit(solution)/shard_map/ppermute | solution.py:104
  96.1 4.1 %copy.149 = bf16[1,2304,432]{2,1,0:T(8,128)(2,1)} copy(bf16[1,2304,432]{1,2,0:T(8,128)(2,1)} %param.25) | data formatting | bytes 3981312 | tf_op args[12]
  100.2 8.6 %reshape.273 = bf16[128,16,486]{2,1,0:T(8,128)(2,1)} reshape(bf16[1,2304,432]{2,1,0:T(8,128)(2,1)} %copy.149) | data formatting | bytes 3981312 | tf_op jit(solution)/shard_map/reshape | solution.py:155
  108.7 7.5 %all-to-all-start = ((bf16[128,16,486]{2,1,0:T(8,128)(2,1)}), bf16[128,16,486]{2,1,0:T(8,128)(2,1)}, u32[]{:S(2)}, u32[]{:S(2)}) async-start(bf16[128,16,486]{2,1,0:T(8,128)(2,1)} %reshape.273), calls=%async_computation | async-start | bytes 4194304 | tf_op jit(solution)/shard_map/all_to_all | solution.py:156
  116.3 2.7 copy_select_fusion.1
  119.0 3.1 pad_maximum_fusion
  122.1 6.7 %reshape.277 = bf16[768,2304]{1,0:T(8,128)(2,1)} reshape(bf16[128,6,2304]{2,1,0:T(8,128)(2,1)} %pad_maximum_fusion) | data formatting | bytes 7077888 | tf_op jit(solution)/shard_map/reshape | solution.py:107
  128.9 3.2 fusion.1
  132.1 3.0 convolution_convert_fusion
  135.1 5.8 %copy.154 = bf16[768,2304]{0,1:T(8,128)(2,1)} copy(bf16[768,2304]{1,0:T(8,128)(2,1)} %convolution_convert_fusion) | data formatting | bytes 7077888 | tf_op jit(solution)/shard_map/convert_element_type | solution.py:117
  140.8 4.0 %constant_dynamic-slice_fusion = (bf16[768,2,1,576]{0,3,2,1:T(8,128)(2,1)}, bf16[768,2,1,576]{0,3,2,1:T(8,128)(2,1)}) fusion(bf16[768,2,2,576]{0,3,2,1:T(8,128)(2,1)} %bitcast.63, s32[]{:T(128)S(6)} %select_n.114, s32[]{:T(128)S(6)} %select_n.113), kind=kLoop, calls=%fused_computation.77 | loop fusion | bytes 7077896 | tf_op jit(solution)/shard_map/jit(dynamic_index_in_dim)/dynamic_slice | solution.py:127
  144.9 6.2 %copy.157 = bf16[768,2,1,576]{3,1,0,2:T(2,128)(2,1)S(1)} copy(bf16[768,2,1,576]{0,3,2,1:T(8,128)(2,1)} %get-tuple-element.30) | data formatting | bytes 3538944 | tf_op jit(solution)/shard_map/jit(dynamic_index_in_dim)/dynamic_slice | solution.py:127
  153.3 2.9 pad.8
  156.2 5.8 %reshape.311 = bf16[128,16,486]{2,1,0:T(8,128)(2,1)S(1)} reshape(bf16[128,7776]{1,0:T(8,128)(2,1)} %pad.8) | data formatting | bytes 3981312 | tf_op jit(solution)/shard_map/reshape | solution.py:124
  162.0 3.9 %copy.159 = bf16[128,16,486]{0,1,2:T(8,128)(2,1)} copy(bf16[128,16,486]{2,1,0:T(8,128)(2,1)S(1)} %reshape.311) | data formatting | bytes 3981312 | tf_op jit(solution)/shard_map/reshape | solution.py:124
  168.1 2.4 all-to-all-done
  172.8 3.9 %copy.161 = bf16[128,16,486]{0,1,2:T(8,128)(2,1)} copy(bf16[128,16,486]{2,1,0:T(8,128)(2,1)S(1)} %gather_fusion) | data formatting | bytes 3981312 | tf_op jit(solution)/shard_map/gather | solution.py:165
  176.6 6.2 %copy.155 = bf16[768,2,1,576]{3,1,0,2:T(2,128)(2,1)S(1)} copy(bf16[768,2,1,576]{0,3,2,1:T(8,128)(2,1)} %get-tuple-element.31) | data formatting | bytes 3538944 | tf_op jit(solution)/shard_map/jit(dynamic_index_in_dim)/dynamic_slice | solution.py:126
  185.0 2.7 copy.156
  190.1 3.6 %reshape.288 = f32[128,16,486]{0,2,1:T(8,128)} reshape(f32[128,7776]{0,1:T(8,128)} %pad_convert_fusion) | data formatting | bytes 7962624 | tf_op jit(solution)/shard_map/convert_element_type | solution.py:129
  193.7 3.7 %fusion = bf16[128,16,486]{0,1,2:T(8,128)(2,1)S(1)} fusion(f32[128,16,486]{0,2,1:T(8,128)} %reshape.288, bf16[128,16,486]{0,1,2:T(8,128)(2,1)} %collective-permute-done.1), kind=kLoop, calls=%fused_computation.6 | loop fusion | flops 2985984 | bytes 7962624 | tf_op jit(solution)/shard_map/convert_element_type | solution.py:129
  197.5 2.6 pad_maximum_fusion.1
  200.0 8.5 %copy.162 = bf16[128,32,486]{2,1,0:T(8,128)(2,1)} copy(bf16[128,32,486]{0,1,2:T(8,128)(2,1)} %pad_maximum_fusion.1) | data formatting | bytes 7962624 | tf_op jit(solution)/shard_map/concatenate | solution.py:131
  208.6 14.3 %all-to-all-start.2 = ((bf16[128,32,486]{2,1,0:T(8,128)(2,1)}), bf16[128,32,486]{2,1,0:T(8,128)(2,1)}, u32[]{:S(2)}, u32[]{:S(2)}) async-start(bf16[128,32,486]{2,1,0:T(8,128)(2,1)} %copy.162), calls=%async_computation.2 | async-start | bytes 8388608 | tf_op jit(solution)/shard_map/all_to_all | solution.py:130
  224.4 95.9 %all-to-all-done.2 = bf16[128,32,486]{2,1,0:T(8,128)(2,1)} async-done(((bf16[128,32,486]{2,1,0:T(8,128)(2,1)}), bf16[128,32,486]{2,1,0:T(8,128)(2,1)}, u32[]{:S(2)}, u32[]{:S(2)}) %all-to-all-start.2) | async-done | bytes 3981344 | tf_op jit(solution)/shard_map/all_to_all | solution.py:130
  320.4 4.0 %fusion.32 = (bf16[128,16,486]{2,1,0:T(8,128)(2,1)}, bf16[128,16,486]{2,1,0:T(8,128)(2,1)S(1)}) fusion(bf16[128,32,486]{2,1,0:T(8,128)(2,1)} %all-to-all-done.2), kind=kLoop, calls=%fused_computation.86 | loop fusion | bytes 7962624 | tf_op jit(solution)/shard_map/slice | solution.py:133
  324.4 4.0 %reshape.312 = bf16[128,7776]{1,0:T(8,128)(2,1)} reshape(bf16[128,16,486]{2,1,0:T(8,128)(2,1)S(1)} %get-tuple-element.27) | data formatting | bytes 3981312 | tf_op jit(solution)/shard_map/reshape | solution.py:134
  329.9 2.6 reshape.283
  332.5 3.6 %gather_fusion.1 = bf16[256,2,576]{2,1,0:T(2,128)(2,1)S(1)} fusion(bf16[768,2,576]{2,1,0:T(2,128)(2,1)} %reshape.283, s32[1024]{0:T(1024)S(1)} %pad_clamp_fusion), kind=kCustom, calls=%fused_computation.1 | custom fusion | bytes 1180672 | tf_op jit(solution)/shard_map/gather | solution.py:137
  337.0 3.8 %collective-permute-start.2 = (f32[16,576]{1,0:T(8,128)S(1)}, f32[16,576]{1,0:T(8,128)S(1)}, u32[]{:S(2)}, u32[]{:S(2)}) collective-permute-start(f32[16,576]{1,0:T(8,128)S(1)} %dynamic-slice_bitcast_fusion), channel_id=1, source_target_pairs={{0,2},{2,0},{1,3},{3,1},{4,6},{6,4},{5,7},{7,5},{8,10},{10,8},{9,1... | collective-permute-start | bytes 110600 | tf_op jit(solution)/shard_map/ppermute | solution.py:145
  341.9 5.2 %reshape.286 = bf16[1,2304,432]{2,1,0:T(8,128)(2,1)S(1)} reshape(bf16[128,16,486]{2,1,0:T(8,128)(2,1)} %get-tuple-element.26) | data formatting | bytes 3981312 | tf_op jit(solution)/shard_map/reshape | solution.py:188
  (84 shorter events, 29.8 us)
Async XLA Ops:
  0.6 223.2 %copy-start = (bf16[256,576]{0,1:T(8,128)(2,1)S(1)}, bf16[256,576]{0,1:T(8,128)(2,1)}, u32[]{:S(2)}) copy-start(bf16[256,576]{0,1:T(8,128)(2,1)} %param.16) | copy-start | bytes 884740
  91.4 24.9 %collective-permute-start = (bf16[128,6,1152]{2,0,1:T(8,128)(2,1)}, bf16[128,6,1152]{2,0,1:T(8,128)(2,1)}, u32[]{:S(2)}, u32[]{:S(2)}) collective-permute-start(bf16[128,6,1152]{2,0,1:T(8,128)(2,1)} %copy.151), channel_id=1, source_target_pairs={{0,1},{1,0},{2,3},{3,2},{4,5},{5,4},{6,7},{7,6},{8,9},{9,8},{10,11... | collective-permute-start | bytes 5308424 | tf_op jit(solution)/shard_map/ppermute | solution.py:104
  108.7 61.7 %all-to-all-start = ((bf16[128,16,486]{2,1,0:T(8,128)(2,1)}), bf16[128,16,486]{2,1,0:T(8,128)(2,1)}, u32[]{:S(2)}, u32[]{:S(2)}) async-start(bf16[128,16,486]{2,1,0:T(8,128)(2,1)} %reshape.273), calls=%async_computation | async-start | bytes 4194304 | tf_op jit(solution)/shard_map/all_to_all | solution.py:156
  122.1 6.7 %copy-start.2 = (bf16[1,2304,432]{1,2,0:T(8,128)(2,1)S(1)}, bf16[1,2304,432]{1,2,0:T(8,128)(2,1)}, u32[]{:S(2)}) copy-start(bf16[1,2304,432]{1,2,0:T(8,128)(2,1)} %param.25) | copy-start | bytes 5971972
  162.0 6.0 %copy-start.10 = (s32[128]{0:T(128)S(1)}, s32[128]{0:T(128)}, u32[]{:S(2)}) copy-start(s32[128]{0:T(128)} %param.24) | copy-start | bytes 1540
  165.9 27.9 %collective-permute-start.1 = (bf16[128,16,486]{0,1,2:T(8,128)(2,1)}, bf16[128,16,486]{0,1,2:T(8,128)(2,1)}, u32[]{:S(2)}, u32[]{:S(2)}) collective-permute-start(bf16[128,16,486]{0,1,2:T(8,128)(2,1)} %copy.159), channel_id=1, source_target_pairs={{0,1},{1,0},{2,3},{3,2},{4,5},{5,4},{6,7},{7,6},{8,9},{9,8},{10,11... | collective-permute-start | bytes 5971976 | tf_op jit(solution)/shard_map/ppermute | solution.py:128
  193.7 3.7 %copy-start.1 = (bf16[128,16,486]{0,1,2:T(8,128)(2,1)S(1)}, bf16[128,16,486]{0,1,2:T(8,128)(2,1)}, u32[]{:S(2)}) copy-start(bf16[128,16,486]{0,1,2:T(8,128)(2,1)} %copy.161) | copy-start | bytes 5971972
  208.6 14.4 %copy-start.7 = (f32[2,8,2]{1,2,0:T(2,128)S(1)}, f32[2,8,2]{1,2,0:T(2,128)}, u32[]{:S(2)}) copy-start(f32[2,8,2]{1,2,0:T(2,128)} %param.22) | copy-start | bytes 388
  208.6 14.5 %copy-start.8 = (s32[1,16]{1,0:T(1,128)S(1)}, s32[1,16]{1,0:T(1,128)}, u32[]{:S(2)}) copy-start(s32[1,16]{1,0:T(1,128)} %param.18) | copy-start | bytes 196
  208.6 14.8 %copy-start.5 = (bf16[2,8,576]{2,1,0:T(8,128)(2,1)S(1)}, bf16[2,8,576]{2,1,0:T(8,128)(2,1)}, u32[]{:S(2)}) copy-start(bf16[2,8,576]{2,1,0:T(8,128)(2,1)} %param.13) | copy-start | bytes 55300
  208.6 14.9 %copy-start.6 = (bf16[2,8,576]{2,1,0:T(8,128)(2,1)S(1)}, bf16[2,8,576]{2,1,0:T(8,128)(2,1)}, u32[]{:S(2)}) copy-start(bf16[2,8,576]{2,1,0:T(8,128)(2,1)} %param.14) | copy-start | bytes 55300
  208.6 15.5 %copy-start.4 = (bf16[2,8,576]{2,1,0:T(8,128)(2,1)S(1)}, bf16[2,8,576]{2,1,0:T(8,128)(2,1)}, u32[]{:S(2)}) copy-start(bf16[2,8,576]{2,1,0:T(8,128)(2,1)} %param.15) | copy-start | bytes 55300
  208.6 111.8 %all-to-all-start.2 = ((bf16[128,32,486]{2,1,0:T(8,128)(2,1)}), bf16[128,32,486]{2,1,0:T(8,128)(2,1)}, u32[]{:S(2)}, u32[]{:S(2)}) async-start(bf16[128,32,486]{2,1,0:T(8,128)(2,1)} %copy.162), calls=%async_computation.2 | async-start | bytes 8388608 | tf_op jit(solution)/shard_map/all_to_all | solution.py:130
  328.4 1.5 slice-start
  332.5 8.3 %copy-start.9 = (bf16[256,576]{0,1:T(8,128)(2,1)S(1)}, bf16[256,576]{0,1:T(8,128)(2,1)}, u32[]{:S(2)}) copy-start(bf16[256,576]{0,1:T(8,128)(2,1)} %param.17) | copy-start | bytes 884740
  332.5 8.6 %copy-start.3 = (bf16[2,8,2304]{2,1,0:T(8,128)(2,1)S(1)}, bf16[2,8,2304]{2,1,0:T(8,128)(2,1)}, u32[]{:S(2)}) copy-start(bf16[2,8,2304]{2,1,0:T(8,128)(2,1)} %param.19) | copy-start | bytes 221188
  337.0 12.4 %collective-permute-start.2 = (f32[16,576]{1,0:T(8,128)S(1)}, f32[16,576]{1,0:T(8,128)S(1)}, u32[]{:S(2)}, u32[]{:S(2)}) collective-permute-start(f32[16,576]{1,0:T(8,128)S(1)} %dynamic-slice_bitcast_fusion), channel_id=1, source_target_pairs={{0,2},{2,0},{1,3},{3,1},{4,6},{6,4},{5,7},{7,5},{8,10},{10,8},{9,1... | collective-permute-start | bytes 110600 | tf_op jit(solution)/shard_map/ppermute | solution.py:145

commit v8 on v4

--- a/solution.py
+++ b/solution.py
@@ -149,7 +149,7 @@
     shard_count = EXPERTS * max(1, nreq // 16)
     _, width, columns = old_weights.shape
     piece = width * columns // nreq
-    pieces = old_weights.reshape(nreq, 16, piece // 16)
+    pieces = jnp.swapaxes(old_weights, 1, 2).reshape(nreq, 16, piece // 16)
     spread = lax.all_to_all(pieces, "req", split_axis=0, concat_axis=0, tiled=True)
     devices = jnp.arange(nreq, dtype=jnp.int32)
     shard_ids = jnp.arange(shard_count, dtype=jnp.int32)
@@ -182,7 +182,8 @@
     layer_out, collected = expert_routed(
         hidden, expert_ids, route_weights, old_place, old_weights[0], gain, sending
     )
-    moved = collected.reshape(old_weights.shape)
+    moved = collected.reshape(1, old_weights.shape[2], old_weights.shape[1])
+    moved = jnp.swapaxes(moved, 1, 2)
     return (context, layer_out, moved)
 
 

time: 339 us -> 338 us (level)
    unnamed x23 -> x19, local copies, waits for them, and re-layouts: 7.23 us -> 0.81 us
  transfers between devices with their start and end apart: 5 -> 5, of which waited for: 2 -> 2; matrix products, arithmetic and copies ran while one was open for 16% -> 14% of each run, Pallas kernels for 0% -> 0%
where the time goes in v8:
time: 338 us; the launch traced here: 334 us
  waiting for transfers between devices  120 us (36%)
  blocking collectives  79.9 us (24%)
  local copies, waits for them, and re-layouts  78.2 us (23%)
  starting transfers between devices  24.7 us (7%)
  other arithmetic  21.8 us (6%)
  matrix products  8.55 us (3%)
    all_to_all x1, waiting for transfers between devices, expert_routed(): lax.all_to_all(jnp.concatenate([extra, pair_sum], axis=1), 'req', split_a...  95 us
    all_to_all x1, blocking collectives, expert_routed(): lax.all_to_all(outgoing, 'req', split_axis=0, concat_axis=0, tiled=True)  79.9 us
    all_to_all x1, waiting for transfers between devices, migrate(): lax.all_to_all(pieces, 'req', split_axis=0, concat_axis=0, tiled=True)  24.8 us
    all_to_all x1, starting transfers between devices, expert_routed(): lax.all_to_all(jnp.concatenate([extra, pair_sum], axis=1), 'req', split_a...  7.75 us
    all_to_all x1, starting transfers between devices, migrate(): lax.all_to_all(pieces, 'req', split_axis=0, concat_axis=0, tiled=True)  7.52 us
    reshape x1, local copies, waits for them, and re-layouts, migrate(): pieces = jnp.swapaxes(old_weights, 1, 2).reshape(nreq, 16, piece // 16)  7.03 us
  transfers between devices with their start and end apart: 5, of which 2 were waited for; matrix products, arithmetic and copies ran while one was open for 14% of the time, Pallas kernels for 0%

profile of v8, /device:TPU:1, one launch (start us, length us, event | category | flops | bytes accessed | tf_op | source)
XLA Modules:
  0.0 334.1 jit_solution(4888957332900902227)
XLA Ops:
  8.3 1.7 reshape.270
  10.0 79.9 %all_to_all.15 = bf16[128,6,1152]{2,1,0:T(8,128)(2,1)S(1)} all-to-all(bf16[128,6,1152]{2,1,0:T(8,128)(2,1)} %reshape.270), channel_id=1, replica_groups=mesh['req'=128,'tp'=4] {'req'}, dimensions={0} | all-to-all | bytes 3538944 | tf_op jit(solution)/shard_map/all_to_all | solution.py:103
  90.0 1.5 copy.52
  91.4 4.6 %collective-permute-start = (bf16[128,6,1152]{2,0,1:T(8,128)(2,1)}, bf16[128,6,1152]{2,0,1:T(8,128)(2,1)}, u32[]{:S(2)}, u32[]{:S(2)}) collective-permute-start(bf16[128,6,1152]{2,0,1:T(8,128)(2,1)} %copy.52), channel_id=1, source_target_pairs={{0,1},{1,0},{2,3},{3,2},{4,5},{5,4},{6,7},{7,6},{8,9},{9,8},{10,11... | collective-permute-start | bytes 5308424 | tf_op jit(solution)/shard_map/ppermute | solution.py:104
  96.1 7.0 %reshape.267 = bf16[128,16,486]{2,1,0:T(8,128)(2,1)} reshape(bf16[1,432,2304]{2,1,0:T(8,128)(2,1)} %bitcast.66) | data formatting | bytes 3981312 | tf_op jit(solution)/shard_map/reshape | solution.py:152
  103.1 7.5 %all-to-all-start = ((bf16[128,16,486]{2,1,0:T(8,128)(2,1)}), bf16[128,16,486]{2,1,0:T(8,128)(2,1)}, u32[]{:S(2)}, u32[]{:S(2)}) async-start(bf16[128,16,486]{2,1,0:T(8,128)(2,1)} %reshape.267), calls=%async_computation | async-start | bytes 4194304 | tf_op jit(solution)/shard_map/all_to_all | solution.py:153
  110.6 2.7 copy_select_fusion.1
  113.4 3.1 pad_maximum_fusion
  116.4 6.7 %reshape.271 = bf16[768,2304]{1,0:T(8,128)(2,1)} reshape(bf16[128,6,2304]{2,1,0:T(8,128)(2,1)} %pad_maximum_fusion) | data formatting | bytes 7077888 | tf_op jit(solution)/shard_map/reshape | solution.py:107
  123.2 3.2 fusion.1
  126.4 3.0 convolution_convert_fusion
  129.4 5.7 %copy.55 = bf16[768,2304]{0,1:T(8,128)(2,1)} copy(bf16[768,2304]{1,0:T(8,128)(2,1)} %convolution_convert_fusion) | data formatting | bytes 7077888 | tf_op jit(solution)/shard_map/convert_element_type | solution.py:117
  135.1 2.8 dynamic-slice_bitcast_fusion
  137.9 1.9 collective-permute-start.1
  140.0 24.8 %all-to-all-done = bf16[128,16,486]{2,1,0:T(8,128)(2,1)} async-done(((bf16[128,16,486]{2,1,0:T(8,128)(2,1)}), bf16[128,16,486]{2,1,0:T(8,128)(2,1)}, u32[]{:S(2)}, u32[]{:S(2)}) %all-to-all-start) | async-done | bytes 1990688 | tf_op jit(solution)/shard_map/all_to_all | solution.py:153
  164.8 2.3 gather_fusion
  167.1 3.7 %fusion = bf16[768,2,576]{0,2,1:T(8,128)(2,1)} fusion(bf16[768,2,576]{0,2,1:T(8,128)(2,1)} %collective-permute-done.1, bf16[768,2,2,576]{0,3,2,1:T(8,128)(2,1)} %bitcast.65, s32[]{:T(128)S(6)} %select_n.113), kind=kLoop, calls=%fused_computation.6 | loop fusion | flops 3538944 | bytes 5308420 | tf_op jit(solution)/shard_map/convert_element_type | solution.py:122
  170.8 6.5 %copy.56 = bf16[768,2,576]{2,1,0:T(2,128)(2,1)} copy(bf16[768,2,576]{0,2,1:T(8,128)(2,1)} %fusion) | data formatting | bytes 3538944 | tf_op jit(solution)/shard_map/convert_element_type | solution.py:122
  177.4 5.2 %reshape.273 = bf16[128,6912]{1,0:T(8,128)(2,1)} reshape(bf16[768,2,576]{2,1,0:T(2,128)(2,1)} %copy.56) | data formatting | bytes 3538944 | tf_op jit(solution)/shard_map/reshape | solution.py:124
  182.6 2.9 pad.4
  185.4 6.5 %reshape.304 = bf16[128,16,486]{2,1,0:T(8,128)(2,1)} reshape(bf16[128,7776]{1,0:T(8,128)(2,1)} %pad.4) | data formatting | bytes 3981312 | tf_op jit(solution)/shard_map/reshape | solution.py:126
  191.9 4.4 %pad_maximum_fusion.1 = bf16[128,32,486]{2,1,0:T(8,128)(2,1)} fusion(bf16[128,16,486]{2,1,0:T(8,128)(2,1)} %reshape.304, bf16[128,16,486]{2,1,0:T(8,128)(2,1)S(1)} %gather_fusion), kind=kLoop, calls=%fused_computation.4 | loop fusion | flops 7962624 | bytes 7962624 | tf_op jit(solution)/shard_map/concatenate | solution.py:128
  196.4 7.7 %all-to-all-start.2 = ((bf16[128,32,486]{2,1,0:T(8,128)(2,1)}), bf16[128,32,486]{2,1,0:T(8,128)(2,1)}, u32[]{:S(2)}, u32[]{:S(2)}) async-start(bf16[128,32,486]{2,1,0:T(8,128)(2,1)} %pad_maximum_fusion.1), calls=%async_computation.2 | async-start | bytes 8388608 | tf_op jit(solution)/shard_map/all_to_all | solution.py:127
  205.6 95.0 %all-to-all-done.2 = bf16[128,32,486]{2,1,0:T(8,128)(2,1)} async-done(((bf16[128,32,486]{2,1,0:T(8,128)(2,1)}), bf16[128,32,486]{2,1,0:T(8,128)(2,1)}, u32[]{:S(2)}, u32[]{:S(2)}) %all-to-all-start.2) | async-done | bytes 3981344 | tf_op jit(solution)/shard_map/all_to_all | solution.py:127
  300.7 4.0 %fusion.32 = (bf16[128,16,486]{2,1,0:T(8,128)(2,1)S(1)}, bf16[128,16,486]{2,1,0:T(8,128)(2,1)}) fusion(bf16[128,32,486]{2,1,0:T(8,128)(2,1)} %all-to-all-done.2), kind=kLoop, calls=%fused_computation.84 | loop fusion | bytes 7962624 | tf_op jit(solution)/shard_map/slice | solution.py:130
  304.7 5.0 %reshape.305 = bf16[128,7776]{1,0:T(8,128)(2,1)} reshape(bf16[128,16,486]{2,1,0:T(8,128)(2,1)} %get-tuple-element.6) | data formatting | bytes 3981312 | tf_op jit(solution)/shard_map/reshape | solution.py:131
  309.7 2.8 slice.37
  312.5 5.4 %reshape.276 = bf16[768,2,576]{2,1,0:T(2,128)(2,1)} reshape(bf16[128,6912]{1,0:T(8,128)(2,1)} %slice.37) | data formatting | bytes 3538944 | tf_op jit(solution)/shard_map/reshape | solution.py:132
  318.0 3.6 %gather_fusion.1 = bf16[256,2,576]{2,1,0:T(2,128)(2,1)S(1)} fusion(bf16[768,2,576]{2,1,0:T(2,128)(2,1)} %reshape.276, s32[1024]{0:T(1024)S(1)} %pad_clamp_fusion), kind=kCustom, calls=%fused_computation.1 | custom fusion | bytes 1180672 | tf_op jit(solution)/shard_map/gather | solution.py:134
  322.5 2.9 collective-permute-start.2
  325.4 1.2 fusion.6
  327.4 6.0 %reshape.279 = bf16[1,432,2304]{2,1,0:T(8,128)(2,1)} reshape(bf16[128,16,486]{2,1,0:T(8,128)(2,1)S(1)} %get-tuple-element.5) | data formatting | bytes 3981312 | tf_op jit(solution)/shard_map/reshape | solution.py:185
  (69 shorter events, 11.4 us)
Async XLA Ops:
  0.6 204.4 %copy-start = (bf16[256,576]{0,1:T(8,128)(2,1)S(1)}, bf16[256,576]{0,1:T(8,128)(2,1)}, u32[]{:S(2)}) copy-start(bf16[256,576]{0,1:T(8,128)(2,1)} %param.16) | copy-start | bytes 884740
  91.4 19.2 %collective-permute-start = (bf16[128,6,1152]{2,0,1:T(8,128)(2,1)}, bf16[128,6,1152]{2,0,1:T(8,128)(2,1)}, u32[]{:S(2)}, u32[]{:S(2)}) collective-permute-start(bf16[128,6,1152]{2,0,1:T(8,128)(2,1)} %copy.52), channel_id=1, source_target_pairs={{0,1},{1,0},{2,3},{3,2},{4,5},{5,4},{6,7},{7,6},{8,9},{9,8},{10,11... | collective-permute-start | bytes 5308424 | tf_op jit(solution)/shard_map/ppermute | solution.py:104
  103.1 61.7 %all-to-all-start = ((bf16[128,16,486]{2,1,0:T(8,128)(2,1)}), bf16[128,16,486]{2,1,0:T(8,128)(2,1)}, u32[]{:S(2)}, u32[]{:S(2)}) async-start(bf16[128,16,486]{2,1,0:T(8,128)(2,1)} %reshape.267), calls=%async_computation | async-start | bytes 4194304 | tf_op jit(solution)/shard_map/all_to_all | solution.py:153
  116.4 6.7 %copy-start.1 = (bf16[1,2304,432]{1,2,0:T(8,128)(2,1)S(1)}, bf16[1,2304,432]{1,2,0:T(8,128)(2,1)}, u32[]{:S(2)}) copy-start(bf16[1,2304,432]{1,2,0:T(8,128)(2,1)} %param.25) | copy-start | bytes 5971972
  135.1 4.7 %copy-start.8 = (s32[128]{0:T(128)S(1)}, s32[128]{0:T(128)}, u32[]{:S(2)}) copy-start(s32[128]{0:T(128)} %param.24) | copy-start | bytes 1540
  137.9 29.2 %collective-permute-start.1 = (bf16[768,2,576]{0,2,1:T(8,128)(2,1)}, bf16[768,2,576]{0,2,1:T(8,128)(2,1)}, u32[]{:S(2)}, u32[]{:S(2)}) collective-permute-start(bf16[768,2,576]{0,2,1:T(8,128)(2,1)} %dynamic-slice_bitcast_fusion), channel_id=1, source_target_pairs={{0,1},{1,0},{2,3},{3,2},{4,5},{5,4},{6,7},{7,6},{8,9},{9,8},{10,11... | collective-permute-start | bytes 5308424 | tf_op jit(solution)/shard_map/ppermute | solution.py:121
  196.3 7.9 %copy-start.6 = (f32[2,8,2]{1,2,0:T(2,128)S(1)}, f32[2,8,2]{1,2,0:T(2,128)}, u32[]{:S(2)}) copy-start(f32[2,8,2]{1,2,0:T(2,128)} %param.22) | copy-start | bytes 388
  196.3 8.0 %copy-start.7 = (s32[1,16]{1,0:T(1,128)S(1)}, s32[1,16]{1,0:T(1,128)}, u32[]{:S(2)}) copy-start(s32[1,16]{1,0:T(1,128)} %param.18) | copy-start | bytes 196
  196.3 8.2 %copy-start.4 = (bf16[2,8,576]{2,1,0:T(8,128)(2,1)S(1)}, bf16[2,8,576]{2,1,0:T(8,128)(2,1)}, u32[]{:S(2)}) copy-start(bf16[2,8,576]{2,1,0:T(8,128)(2,1)} %param.13) | copy-start | bytes 55300
  196.3 8.3 %copy-start.5 = (bf16[2,8,576]{2,1,0:T(8,128)(2,1)S(1)}, bf16[2,8,576]{2,1,0:T(8,128)(2,1)}, u32[]{:S(2)}) copy-start(bf16[2,8,576]{2,1,0:T(8,128)(2,1)} %param.14) | copy-start | bytes 55300
  196.3 9.0 %copy-start.3 = (bf16[2,8,576]{2,1,0:T(8,128)(2,1)S(1)}, bf16[2,8,576]{2,1,0:T(8,128)(2,1)}, u32[]{:S(2)}) copy-start(bf16[2,8,576]{2,1,0:T(8,128)(2,1)} %param.15) | copy-start | bytes 55300
  196.4 104.3 %all-to-all-start.2 = ((bf16[128,32,486]{2,1,0:T(8,128)(2,1)}), bf16[128,32,486]{2,1,0:T(8,128)(2,1)}, u32[]{:S(2)}, u32[]{:S(2)}) async-start(bf16[128,32,486]{2,1,0:T(8,128)(2,1)} %pad_maximum_fusion.1), calls=%async_computation.2 | async-start | bytes 8388608 | tf_op jit(solution)/shard_map/all_to_all | solution.py:127
  318.0 8.7 %copy-start.2 = (bf16[2,8,2304]{2,1,0:T(8,128)(2,1)S(1)}, bf16[2,8,2304]{2,1,0:T(8,128)(2,1)}, u32[]{:S(2)}) copy-start(bf16[2,8,2304]{2,1,0:T(8,128)(2,1)} %param.19) | copy-start | bytes 221188
  322.5 10.9 %collective-permute-start.2 = (f32[16,576]{1,0:T(8,128)S(1)}, f32[16,576]{1,0:T(8,128)S(1)}, u32[]{:S(2)}, u32[]{:S(2)}) collective-permute-start(f32[16,576]{1,0:T(8,128)S(1)} %dynamic-slice_bitcast_fusion.1), channel_id=1, source_target_pairs={{0,2},{2,0},{1,3},{3,1},{4,6},{6,4},{5,7},{7,5},{8,10},{10,8},{9,1... | collective-permute-start | bytes 110600 | tf_op jit(solution)/shard_map/ppermute | solution.py:142

commit v9 on v8

--- a/solution.py
+++ b/solution.py
@@ -99,8 +99,9 @@
     repeated = jnp.repeat(normed.reshape(batches * tok_rows, width), topk, axis=0)
     my_half = lax.dynamic_slice_in_dim(repeated, core * half, half, 1)
     outgoing = jnp.dot(hits.astype(jnp.bfloat16), my_half, preferred_element_type=jnp.float32)
-    outgoing = outgoing.astype(jnp.bfloat16).reshape(nreq, slots, half)
+    outgoing = outgoing.astype(jnp.bfloat16).reshape(nreq, 16, slots * half // 16)
     received = lax.all_to_all(outgoing, "req", split_axis=0, concat_axis=0, tiled=True)
+    received = received.reshape(nreq, slots, half)
     other = lax.ppermute(received, "tp", CORE_PAIRS)
     low = jnp.where(core == 0, received, other)
     high = jnp.where(core == 0, other, received)

time: 338 us -> 337 us (level)
  local copies, waits for them, and re-layouts: 78.2 us -> 87.7 us
  waiting for transfers between devices: 120 us -> 113 us
  blocking collectives: 79.9 us -> 74.3 us
    all_to_all x1, waiting for transfers between devices: 24.8 us -> 18 us  [migrate(): lax.all_to_all(pieces, 'req', split_axis=0, concat_axis=0, tiled=True)]
    concatenate x0 -> x1, local copies, waits for them, and re-layouts: none -> 6.73 us  [expert_routed(): jnp.concatenate([low, high], axis=-1).reshape(nreq * slots, width)]
    all_to_all x1, blocking collectives: 79.9 us -> 74.3 us  [expert_routed(): lax.all_to_all(outgoing, 'req', split_axis=0, concat_axis=0, tiled=True)]
    reshape x1, local copies, waits for them, and re-layouts: 1.72 us -> 6.05 us  [expert_routed(): outgoing.astype(jnp.bfloat16).reshape(nreq, 16, slots * half // 16)]
  transfers between devices with their start and end apart: 5 -> 5, of which waited for: 2 -> 2; matrix products, arithmetic and copies ran while one was open for 14% -> 15% of each run, Pallas kernels for 0% -> 0%
where the time goes in v9:
time: 337 us; the launch traced here: 332 us
  waiting for transfers between devices  113 us (34%)
  local copies, waits for them, and re-layouts  87.7 us (26%)
  blocking collectives  74.3 us (22%)
  starting transfers between devices  24.7 us (7%)
  other arithmetic  20.2 us (6%)
  matrix products  11.2 us (3%)
    all_to_all x1, waiting for transfers between devices, expert_routed(): lax.all_to_all(jnp.concatenate([extra, pair_sum], axis=1), 'req', split_a...  94.9 us
    all_to_all x1, blocking collectives, expert_routed(): lax.all_to_all(outgoing, 'req', split_axis=0, concat_axis=0, tiled=True)  74.3 us
    all_to_all x1, waiting for transfers between devices, migrate(): lax.all_to_all(pieces, 'req', split_axis=0, concat_axis=0, tiled=True)  18 us
    all_to_all x1, starting transfers between devices, expert_routed(): lax.all_to_all(jnp.concatenate([extra, pair_sum], axis=1), 'req', split_a...  7.75 us
  transfers between devices with their start and end apart: 5, of which 2 were waited for; matrix products, arithmetic and copies ran while one was open for 15% of the time, Pallas kernels for 0%

profile of v9, /device:TPU:1, one launch (start us, length us, event | category | flops | bytes accessed | tf_op | source)
XLA Modules:
  0.0 332.1 jit_solution(12148094549247758055)
XLA Ops:
  9.5 6.0 %reshape.273 = bf16[128,16,432]{2,1,0:T(8,128)(2,1)S(1)} reshape(bf16[768,1152]{1,0:T(8,128)(2,1)} %convolution_convert_fusion.1) | data formatting | bytes 3538944 | tf_op jit(solution)/shard_map/reshape | solution.py:102
  15.6 74.3 %all_to_all.15 = bf16[128,16,432]{2,1,0:T(8,128)(2,1)} all-to-all(bf16[128,16,432]{2,1,0:T(8,128)(2,1)S(1)} %reshape.273), channel_id=1, replica_groups=mesh['req'=128,'tp'=4] {'req'}, dimensions={0} | all-to-all | bytes 3538944 | tf_op jit(solution)/shard_map/all_to_all | solution.py:103
  89.9 4.6 %copy.39 = bf16[128,16,432]{0,2,1:T(8,128)(2,1)} copy(bf16[128,16,432]{2,1,0:T(8,128)(2,1)} %all_to_all.15) | data formatting | bytes 3538944 | tf_op jit(solution)/shard_map/all_to_all | solution.py:103
  94.5 4.5 %collective-permute-start = (bf16[128,6,1152]{0,2,1:T(8,128)(2,1)}, bf16[128,6,1152]{0,2,1:T(8,128)(2,1)}, u32[]{:S(2)}, u32[]{:S(2)}) collective-permute-start(bf16[128,6,1152]{0,2,1:T(8,128)(2,1)} %bitcast.15), channel_id=1, source_target_pairs={{0,1},{1,0},{2,3},{3,2},{4,5},{5,4},{6,7},{7,6},{8,9},{9,8},{10,11... | collective-permute-start | bytes 5308424 | tf_op jit(solution)/shard_map/ppermute | solution.py:105
  99.0 5.9 %reshape.270 = bf16[128,16,486]{2,1,0:T(8,128)(2,1)} reshape(bf16[1,432,2304]{2,1,0:T(8,128)(2,1)S(1)} %bitcast.69) | data formatting | bytes 3981312 | tf_op jit(solution)/shard_map/reshape | solution.py:153
  104.9 6.4 %all-to-all-start = ((bf16[128,16,486]{2,1,0:T(8,128)(2,1)}), bf16[128,16,486]{2,1,0:T(8,128)(2,1)S(1)}, u32[]{:S(2)}, u32[]{:S(2)}) async-start(bf16[128,16,486]{2,1,0:T(8,128)(2,1)} %reshape.270), calls=%async_computation | async-start | bytes 4194304 | tf_op jit(solution)/shard_map/all_to_all | solution.py:154
  111.3 2.2 broadcast_select_fusion.1
  113.6 2.0 pad_maximum_fusion.1
  115.6 6.7 %copy.40 = bf16[128,6,2304]{2,1,0:T(8,128)(2,1)} copy(bf16[128,6,2304]{0,2,1:T(8,128)(2,1)} %pad_maximum_fusion.1) | data formatting | bytes 7077888 | tf_op jit(solution)/shard_map/concatenate | solution.py:108
  122.3 6.6 %reshape.275 = bf16[768,2304]{1,0:T(8,128)(2,1)} reshape(bf16[128,6,2304]{2,1,0:T(8,128)(2,1)} %copy.40) | data formatting | bytes 7077888 | tf_op jit(solution)/shard_map/reshape | solution.py:108
  128.9 3.6 %fusion.1 = f32[768,288]{0,1:T(8,128)S(1)} fusion(bf16[768,2304]{1,0:T(8,128)(2,1)} %reshape.275, bf16[2304,432]{0,1:T(8,128)(2,1)} %bitcast.67), kind=kOutput, calls=%fused_computation.11 | convolution fusion | flops 1019215872 | bytes 5750784 | tf_op jit(solution)/shard_map/dot_general | solution.py:109
  132.5 4.1 %convolution_convert_fusion = bf16[768,2304]{1,0:T(8,128)(2,1)} fusion(bf16[2304,432]{0,1:T(8,128)(2,1)} %bitcast.68, f32[768,288]{0,1:T(8,128)S(1)} %fusion.1), kind=kOutput, calls=%fused_computation.2 | convolution fusion | flops 512040960 | bytes 5087232 | tf_op jit(solution)/shard_map/dot_general | solution.py:113
  136.6 5.7 %copy.41 = bf16[768,2304]{0,1:T(8,128)(2,1)} copy(bf16[768,2304]{1,0:T(8,128)(2,1)} %convolution_convert_fusion) | data formatting | bytes 7077888 | tf_op jit(solution)/shard_map/convert_element_type | solution.py:118
  142.3 2.8 dynamic-slice_bitcast_fusion
  145.1 2.1 collective-permute-start.1
  147.4 18.0 %all-to-all-done = bf16[128,16,486]{2,1,0:T(8,128)(2,1)S(1)} async-done(((bf16[128,16,486]{2,1,0:T(8,128)(2,1)}), bf16[128,16,486]{2,1,0:T(8,128)(2,1)S(1)}, u32[]{:S(2)}, u32[]{:S(2)}) %all-to-all-start) | async-done | bytes 1990688 | tf_op jit(solution)/shard_map/all_to_all | solution.py:154
  165.4 2.0 gather_fusion
  167.4 3.6 %fusion = bf16[768,2,576]{0,2,1:T(8,128)(2,1)} fusion(bf16[768,2,576]{0,2,1:T(8,128)(2,1)} %collective-permute-done.1, bf16[768,2,2,576]{0,3,2,1:T(8,128)(2,1)} %bitcast.66, s32[]{:T(128)S(6)} %select_n.113), kind=kLoop, calls=%fused_computation.6 | loop fusion | flops 3538944 | bytes 5308420 | tf_op jit(solution)/shard_map/convert_element_type | solution.py:123
  171.1 6.2 %copy.42 = bf16[768,2,576]{2,1,0:T(2,128)(2,1)S(1)} copy(bf16[768,2,576]{0,2,1:T(8,128)(2,1)} %fusion) | data formatting | bytes 3538944 | tf_op jit(solution)/shard_map/convert_element_type | solution.py:123
  177.2 2.2 reshape.277
  179.5 2.9 pad.4
  182.4 6.6 %reshape.308 = bf16[128,16,486]{2,1,0:T(8,128)(2,1)} reshape(bf16[128,7776]{1,0:T(8,128)(2,1)} %pad.4) | data formatting | bytes 3981312 | tf_op jit(solution)/shard_map/reshape | solution.py:127
  189.0 4.4 %pad_maximum_fusion = bf16[128,32,486]{2,1,0:T(8,128)(2,1)} fusion(bf16[128,16,486]{2,1,0:T(8,128)(2,1)} %reshape.308, bf16[128,16,486]{2,1,0:T(8,128)(2,1)S(1)} %copy-done.1), kind=kLoop, calls=%fused_computation.3 | loop fusion | flops 7962624 | bytes 7962624 | tf_op jit(solution)/shard_map/concatenate | solution.py:129
  193.5 7.7 %all-to-all-start.2 = ((bf16[128,32,486]{2,1,0:T(8,128)(2,1)}), bf16[128,32,486]{2,1,0:T(8,128)(2,1)}, u32[]{:S(2)}, u32[]{:S(2)}) async-start(bf16[128,32,486]{2,1,0:T(8,128)(2,1)} %pad_maximum_fusion), calls=%async_computation.2 | async-start | bytes 8388608 | tf_op jit(solution)/shard_map/all_to_all | solution.py:128
  202.8 94.9 %all-to-all-done.2 = bf16[128,32,486]{2,1,0:T(8,128)(2,1)} async-done(((bf16[128,32,486]{2,1,0:T(8,128)(2,1)}), bf16[128,32,486]{2,1,0:T(8,128)(2,1)}, u32[]{:S(2)}, u32[]{:S(2)}) %all-to-all-start.2) | async-done | bytes 3981344 | tf_op jit(solution)/shard_map/all_to_all | solution.py:128
  297.7 4.0 %fusion.32 = (bf16[128,16,486]{2,1,0:T(8,128)(2,1)S(1)}, bf16[128,16,486]{2,1,0:T(8,128)(2,1)}) fusion(bf16[128,32,486]{2,1,0:T(8,128)(2,1)} %all-to-all-done.2), kind=kLoop, calls=%fused_computation.84 | loop fusion | bytes 7962624 | tf_op jit(solution)/shard_map/slice | solution.py:131
  301.7 5.0 %reshape.309 = bf16[128,7776]{1,0:T(8,128)(2,1)} reshape(bf16[128,16,486]{2,1,0:T(8,128)(2,1)} %get-tuple-element.6) | data formatting | bytes 3981312 | tf_op jit(solution)/shard_map/reshape | solution.py:132
  306.7 2.8 slice.37
  309.5 5.4 %reshape.280 = bf16[768,2,576]{2,1,0:T(2,128)(2,1)} reshape(bf16[128,6912]{1,0:T(8,128)(2,1)} %slice.37) | data formatting | bytes 3538944 | tf_op jit(solution)/shard_map/reshape | solution.py:133
  315.0 3.6 %gather_fusion.1 = bf16[256,2,576]{2,1,0:T(2,128)(2,1)S(1)} fusion(bf16[768,2,576]{2,1,0:T(2,128)(2,1)} %reshape.280, s32[1024]{0:T(1024)S(1)} %pad_clamp_fusion), kind=kCustom, calls=%fused_computation.1 | custom fusion | bytes 1180672 | tf_op jit(solution)/shard_map/gather | solution.py:135
  319.5 3.9 %collective-permute-start.2 = (f32[16,576]{1,0:T(8,128)S(1)}, f32[16,576]{1,0:T(8,128)S(1)}, u32[]{:S(2)}, u32[]{:S(2)}) collective-permute-start(f32[16,576]{1,0:T(8,128)S(1)} %dynamic-slice_bitcast_fusion.1), channel_id=1, source_target_pairs={{0,2},{2,0},{1,3},{3,1},{4,6},{6,4},{5,7},{7,5},{8,10},{10,8},{9,1... | collective-permute-start | bytes 110600 | tf_op jit(solution)/shard_map/ppermute | solution.py:143
  325.3 6.0 %reshape.283 = bf16[1,432,2304]{2,1,0:T(8,128)(2,1)} reshape(bf16[128,16,486]{2,1,0:T(8,128)(2,1)S(1)} %get-tuple-element.5) | data formatting | bytes 3981312 | tf_op jit(solution)/shard_map/reshape | solution.py:186
  (72 shorter events, 13.9 us)
Async XLA Ops:
  0.6 201.5 %copy-start = (bf16[256,576]{0,1:T(8,128)(2,1)S(1)}, bf16[256,576]{0,1:T(8,128)(2,1)}, u32[]{:S(2)}) copy-start(bf16[256,576]{0,1:T(8,128)(2,1)} %param.16) | copy-start | bytes 884740
  89.9 9.2 %copy-start.2 = (bf16[1,2304,432]{1,2,0:T(8,128)(2,1)S(1)}, bf16[1,2304,432]{1,2,0:T(8,128)(2,1)}, u32[]{:S(2)}) copy-start(bf16[1,2304,432]{1,2,0:T(8,128)(2,1)} %param.25) | copy-start | bytes 5971972
  94.5 16.8 %collective-permute-start = (bf16[128,6,1152]{0,2,1:T(8,128)(2,1)}, bf16[128,6,1152]{0,2,1:T(8,128)(2,1)}, u32[]{:S(2)}, u32[]{:S(2)}) collective-permute-start(bf16[128,6,1152]{0,2,1:T(8,128)(2,1)} %bitcast.15), channel_id=1, source_target_pairs={{0,1},{1,0},{2,3},{3,2},{4,5},{5,4},{6,7},{7,6},{8,9},{9,8},{10,11... | collective-permute-start | bytes 5308424 | tf_op jit(solution)/shard_map/ppermute | solution.py:105
  104.9 60.5 %all-to-all-start = ((bf16[128,16,486]{2,1,0:T(8,128)(2,1)}), bf16[128,16,486]{2,1,0:T(8,128)(2,1)S(1)}, u32[]{:S(2)}, u32[]{:S(2)}) async-start(bf16[128,16,486]{2,1,0:T(8,128)(2,1)} %reshape.270), calls=%async_computation | async-start | bytes 4194304 | tf_op jit(solution)/shard_map/all_to_all | solution.py:154
  142.3 4.9 %copy-start.9 = (s32[128]{0:T(128)S(1)}, s32[128]{0:T(128)}, u32[]{:S(2)}) copy-start(s32[128]{0:T(128)} %param.24) | copy-start | bytes 1540
  145.1 22.3 %collective-permute-start.1 = (bf16[768,2,576]{0,2,1:T(8,128)(2,1)}, bf16[768,2,576]{0,2,1:T(8,128)(2,1)}, u32[]{:S(2)}, u32[]{:S(2)}) collective-permute-start(bf16[768,2,576]{0,2,1:T(8,128)(2,1)} %dynamic-slice_bitcast_fusion), channel_id=1, source_target_pairs={{0,1},{1,0},{2,3},{3,2},{4,5},{5,4},{6,7},{7,6},{8,9},{9,8},{10,11... | collective-permute-start | bytes 5308424 | tf_op jit(solution)/shard_map/ppermute | solution.py:122
  182.4 6.6 %copy-start.1 = (bf16[128,16,486]{2,1,0:T(8,128)(2,1)S(1)}, bf16[128,16,486]{2,1,0:T(8,128)(2,1)}, u32[]{:S(2)}) copy-start(bf16[128,16,486]{2,1,0:T(8,128)(2,1)} %gather_fusion) | copy-start | bytes 5971972
  193.4 7.9 %copy-start.7 = (f32[2,8,2]{1,2,0:T(2,128)S(1)}, f32[2,8,2]{1,2,0:T(2,128)}, u32[]{:S(2)}) copy-start(f32[2,8,2]{1,2,0:T(2,128)} %param.22) | copy-start | bytes 388
  193.4 8.0 %copy-start.8 = (s32[1,16]{1,0:T(1,128)S(1)}, s32[1,16]{1,0:T(1,128)}, u32[]{:S(2)}) copy-start(s32[1,16]{1,0:T(1,128)} %param.18) | copy-start | bytes 196
  193.5 8.2 %copy-start.5 = (bf16[2,8,576]{2,1,0:T(8,128)(2,1)S(1)}, bf16[2,8,576]{2,1,0:T(8,128)(2,1)}, u32[]{:S(2)}) copy-start(bf16[2,8,576]{2,1,0:T(8,128)(2,1)} %param.13) | copy-start | bytes 55300
  193.5 8.3 %copy-start.6 = (bf16[2,8,576]{2,1,0:T(8,128)(2,1)S(1)}, bf16[2,8,576]{2,1,0:T(8,128)(2,1)}, u32[]{:S(2)}) copy-start(bf16[2,8,576]{2,1,0:T(8,128)(2,1)} %param.14) | copy-start | bytes 55300
  193.5 9.0 %copy-start.4 = (bf16[2,8,576]{2,1,0:T(8,128)(2,1)S(1)}, bf16[2,8,576]{2,1,0:T(8,128)(2,1)}, u32[]{:S(2)}) copy-start(bf16[2,8,576]{2,1,0:T(8,128)(2,1)} %param.15) | copy-start | bytes 55300
  193.5 104.2 %all-to-all-start.2 = ((bf16[128,32,486]{2,1,0:T(8,128)(2,1)}), bf16[128,32,486]{2,1,0:T(8,128)(2,1)}, u32[]{:S(2)}, u32[]{:S(2)}) async-start(bf16[128,32,486]{2,1,0:T(8,128)(2,1)} %pad_maximum_fusion), calls=%async_computation.2 | async-start | bytes 8388608 | tf_op jit(solution)/shard_map/all_to_all | solution.py:128
  315.0 9.6 %copy-start.3 = (bf16[2,8,2304]{2,1,0:T(8,128)(2,1)S(1)}, bf16[2,8,2304]{2,1,0:T(8,128)(2,1)}, u32[]{:S(2)}) copy-start(bf16[2,8,2304]{2,1,0:T(8,128)(2,1)} %param.19) | copy-start | bytes 221188
  319.5 11.9 %collective-permute-start.2 = (f32[16,576]{1,0:T(8,128)S(1)}, f32[16,576]{1,0:T(8,128)S(1)}, u32[]{:S(2)}, u32[]{:S(2)}) collective-permute-start(f32[16,576]{1,0:T(8,128)S(1)} %dynamic-slice_bitcast_fusion.1), channel_id=1, source_target_pairs={{0,2},{2,0},{1,3},{3,1},{4,6},{6,4},{5,7},{7,5},{8,10},{10,8},{9,1... | collective-permute-start | bytes 110600 | tf_op jit(solution)/shard_map/ppermute | solution.py:143

commit v10 on v9

--- a/solution.py
+++ b/solution.py
@@ -99,8 +99,18 @@
     repeated = jnp.repeat(normed.reshape(batches * tok_rows, width), topk, axis=0)
     my_half = lax.dynamic_slice_in_dim(repeated, core * half, half, 1)
     outgoing = jnp.dot(hits.astype(jnp.bfloat16), my_half, preferred_element_type=jnp.float32)
-    outgoing = outgoing.astype(jnp.bfloat16).reshape(nreq, 16, slots * half // 16)
-    received = lax.all_to_all(outgoing, "req", split_axis=0, concat_axis=0, tiled=True)
+    pieces, needed = extra
+    piece_rows, piece_lanes = pieces.shape[1:]
+    outgoing = outgoing.astype(jnp.bfloat16).reshape(nreq, slots * half)
+    outgoing = jnp.pad(outgoing, ((0, 0), (0, piece_rows * piece_lanes - slots * half)))
+    outgoing = outgoing.reshape(nreq, piece_rows, piece_lanes)
+    first = lax.all_to_all(
+        jnp.concatenate([pieces, outgoing], axis=1), "req", split_axis=0, concat_axis=0, tiled=True
+    )
+    collected = lax.all_to_all(
+        first[:, :piece_rows][needed], "req", split_axis=0, concat_axis=0, tiled=True
+    )
+    received = first[:, piece_rows:].reshape(nreq, piece_rows * piece_lanes)[:, : slots * half]
     received = received.reshape(nreq, slots, half)
     other = lax.ppermute(received, "tp", CORE_PAIRS)
     low = jnp.where(core == 0, received, other)
@@ -121,15 +131,8 @@
     send = lax.dynamic_index_in_dim(part, 1 - core, 2, keepdims=False)
     got = lax.ppermute(send, "tp", CORE_PAIRS)
     pair_sum = (keep.astype(jnp.float32) + got.astype(jnp.float32)).astype(jnp.bfloat16)
-    piece_rows, piece_lanes = extra.shape[1:]
-    pair_sum = pair_sum.reshape(nreq, slots * half)
-    pair_sum = jnp.pad(pair_sum, ((0, 0), (0, piece_rows * piece_lanes - slots * half)))
-    pair_sum = pair_sum.reshape(nreq, piece_rows, piece_lanes)
-    both = lax.all_to_all(
-        jnp.concatenate([extra, pair_sum], axis=1), "req", split_axis=0, concat_axis=0, tiled=True
-    )
-    collected = both[:, :piece_rows]
-    returned = both[:, piece_rows:].reshape(nreq, piece_rows * piece_lanes)[:, : slots * half]
+    pair_sum = pair_sum.reshape(nreq, 16, slots * half // 16)
+    returned = lax.all_to_all(pair_sum, "req", split_axis=0, concat_axis=0, tiled=True)
     returned = returned.reshape(nreq * slots, 2, quarter)
     picked = (
         returned[slot.reshape(-1)]
@@ -151,7 +154,6 @@
     _, width, columns = old_weights.shape
     piece = width * columns // nreq
     pieces = jnp.swapaxes(old_weights, 1, 2).reshape(nreq, 16, piece // 16)
-    spread = lax.all_to_all(pieces, "req", split_axis=0, concat_axis=0, tiled=True)
     devices = jnp.arange(nreq, dtype=jnp.int32)
     shard_ids = jnp.arange(shard_count, dtype=jnp.int32)
     first_old = jnp.min(
@@ -160,7 +162,7 @@
     needed = jnp.sum(
         jnp.where(new_place[:, None] == shard_ids[None, :], first_old[None, :], 0), axis=1
     )
-    return spread[needed]
+    return pieces, needed
 
 
 def on_device(

time: 337 us -> 352 us (1.045)
  blocking collectives: 74.3 us -> 118 us
  waiting for transfers between devices: 113 us -> 91.3 us
    all_to_all x1, blocking collectives: 74.3 us -> 118 us  [expert_routed(): lax.all_to_all(jnp.concatenate([pieces, outgoing], axis=1), 'req', split_...]
    all_to_all x2, waiting for transfers between devices: 113 us -> 84.5 us  [the longest x1 50 us: expert_routed(): lax.all_to_all(pair_sum, 'req', split_axis=0, concat_axis=0, tiled=True)]
    all_to_all x1 -> x0, local copies, waits for them, and re-layouts: 4.59 us -> none  [expert_routed(): lax.all_to_all(outgoing, 'req', split_axis=0, concat_axis=0, tiled=True)]
    reshape x4 -> x6, local copies, waits for them, and re-layouts: 19.9 us -> 19.4 us  [the longest x2 5.54 us: expert_routed(): outgoing = outgoing.astype(jnp.bfloat16).reshape(nreq, slots * half)]
  transfers between devices with their start and end apart: 5 -> 5, of which waited for: 2 -> 4; matrix products, arithmetic and copies ran while one was open for 15% -> 7% of each run, Pallas kernels for 0% -> 0%
where the time goes in v10:
time: 352 us; the launch traced here: 350 us
  blocking collectives  118 us (34%)
  waiting for transfers between devices  91.3 us (26%)
  local copies, waits for them, and re-layouts  86.2 us (24%)
  starting transfers between devices  26.3 us (7%)
  other arithmetic  17 us (5%)
  matrix products  9.72 us (3%)
    all_to_all x1, blocking collectives, expert_routed(): lax.all_to_all(jnp.concatenate([pieces, outgoing], axis=1), 'req', split_...  118 us
    all_to_all x1, waiting for transfers between devices, expert_routed(): lax.all_to_all(pair_sum, 'req', split_axis=0, concat_axis=0, tiled=True)  50 us
    all_to_all x1, waiting for transfers between devices, expert_routed(): lax.all_to_all(first[:, :piece_rows][needed], 'req', split_axis=0, concat...  34.5 us
    all_to_all x1, starting transfers between devices, expert_routed(): lax.all_to_all(pair_sum, 'req', split_axis=0, concat_axis=0, tiled=True)  8.15 us
    reshape x1, local copies, waits for them, and re-layouts, expert_routed(): returned = returned.reshape(nreq * slots, 2, quarter)  7.39 us
    all_to_all x1, starting transfers between devices, expert_routed(): lax.all_to_all(first[:, :piece_rows][needed], 'req', split_axis=0, concat...  7.34 us
    reshape x1, local copies, waits for them, and re-layouts, migrate(): pieces = jnp.swapaxes(old_weights, 1, 2).reshape(nreq, 16, piece // 16)  7.11 us
  transfers between devices with their start and end apart: 5, of which 4 were waited for; matrix products, arithmetic and copies ran while one was open for 7% of the time, Pallas kernels for 0%

profile of v10, /device:TPU:1, one launch (start us, length us, event | category | flops | bytes accessed | tf_op | source)
XLA Modules:
  0.0 349.8 jit_solution(14449324961823106608)
XLA Ops:
  7.6 1.9 convolution_convert_fusion.1
  9.5 3.3 reshape.273
  12.9 2.2 copy.37
  18.3 3.4 copy.38
  21.7 7.1 %reshape.270 = bf16[128,16,486]{2,1,0:T(8,128)(2,1)} reshape(bf16[1,432,2304]{2,1,0:T(8,128)(2,1)} %bitcast.71) | data formatting | bytes 3981312 | tf_op jit(solution)/shard_map/reshape | solution.py:156
  28.8 2.4 pad_maximum_fusion
  31.1 118.2 %all_to_all.15 = bf16[128,32,486]{2,1,0:T(8,128)(2,1)S(1)} all-to-all(bf16[128,32,486]{2,1,0:T(8,128)(2,1)S(1)} %pad_maximum_fusion), channel_id=1, replica_groups=mesh['req'=128,'tp'=4] {'req'}, dimensions={0} | all-to-all | bytes 7962624 | tf_op jit(solution)/shard_map/all_to_all | solution.py:107
  151.2 4.0 %reshape.308 = bf16[128,7776]{1,0:T(8,128)(2,1)} reshape(bf16[128,16,486]{2,1,0:T(8,128)(2,1)S(1)} %get-tuple-element.6) | data formatting | bytes 3981312 | tf_op jit(solution)/shard_map/reshape | solution.py:113
  156.7 2.2 copy.58
  158.9 5.6 %collective-permute-start = (bf16[128,6,1152]{0,2,1:T(8,128)(2,1)}, bf16[128,6,1152]{0,2,1:T(8,128)(2,1)S(1)}, u32[]{:S(2)}, u32[]{:S(2)}) collective-permute-start(bf16[128,6,1152]{0,2,1:T(8,128)(2,1)} %bitcast.69), channel_id=1, source_target_pairs={{0,1},{1,0},{2,3},{3,2},{4,5},{5,4},{6,7},{7,6},{8,9},{9,8},{10,11... | collective-permute-start | bytes 5308424 | tf_op jit(solution)/shard_map/ppermute | solution.py:115
  164.6 3.3 collective-permute-done
  169.6 2.0 pad_maximum_fusion.1
  171.6 6.7 %copy.40 = bf16[128,6,2304]{2,1,0:T(8,128)(2,1)} copy(bf16[128,6,2304]{0,2,1:T(8,128)(2,1)} %pad_maximum_fusion.1) | data formatting | bytes 7077888 | tf_op jit(solution)/shard_map/concatenate | solution.py:118
  178.3 6.7 %reshape.277 = bf16[768,2304]{1,0:T(8,128)(2,1)} reshape(bf16[128,6,2304]{2,1,0:T(8,128)(2,1)} %copy.40) | data formatting | bytes 7077888 | tf_op jit(solution)/shard_map/reshape | solution.py:118
  185.1 3.2 fusion.1
  188.3 2.9 convolution_convert_fusion
  191.2 5.8 %copy.41 = bf16[768,2304]{0,1:T(8,128)(2,1)} copy(bf16[768,2304]{1,0:T(8,128)(2,1)} %convolution_convert_fusion) | data formatting | bytes 7077888 | tf_op jit(solution)/shard_map/convert_element_type | solution.py:128
  197.0 2.8 dynamic-slice_bitcast_fusion
  199.8 2.3 collective-permute-start.1
  202.1 3.5 %collective-permute-done.1 = bf16[768,2,576]{0,2,1:T(8,128)(2,1)S(1)} collective-permute-done((bf16[768,2,576]{0,2,1:T(8,128)(2,1)}, bf16[768,2,576]{0,2,1:T(8,128)(2,1)S(1)}, u32[]{:S(2)}, u32[]{:S(2)}) %collective-permute-start.1) | collective-permute-done | bytes 1769504 | tf_op jit(solution)/shard_map/ppermute | solution.py:132
  205.6 3.1 fusion
  208.7 6.2 %copy.42 = bf16[768,2,576]{2,1,0:T(2,128)(2,1)S(1)} copy(bf16[768,2,576]{0,2,1:T(8,128)(2,1)} %fusion) | data formatting | bytes 3538944 | tf_op jit(solution)/shard_map/convert_element_type | solution.py:133
  214.8 4.8 %reshape.279 = bf16[128,16,432]{2,1,0:T(8,128)(2,1)} reshape(bf16[768,2,576]{2,1,0:T(2,128)(2,1)S(1)} %copy.42) | data formatting | bytes 3538944 | tf_op jit(solution)/shard_map/reshape | solution.py:134
  219.7 8.1 %all-to-all-start.1 = ((bf16[128,16,432]{2,1,0:T(8,128)(2,1)}), bf16[128,16,432]{2,1,0:T(8,128)(2,1)S(1)}, u32[]{:S(2)}, u32[]{:S(2)}) async-start(bf16[128,16,432]{2,1,0:T(8,128)(2,1)} %reshape.279), calls=%async_computation.1 | async-start | bytes 4194304 | tf_op jit(solution)/shard_map/all_to_all | solution.py:135
  228.0 3.6 %gather_fusion.1 = bf16[128,16,486]{2,1,0:T(8,128)(2,1)} fusion(bf16[128,16,486]{2,1,0:T(8,128)(2,1)} %get-tuple-element.5, s32[1024]{0:T(1024)S(1)} %pad_clamp_fusion), kind=kCustom, calls=%fused_computation.1 | custom fusion | bytes 3981824 | tf_op jit(solution)/shard_map/gather | solution.py:111
  231.6 50.0 %all-to-all-done.1 = bf16[128,16,432]{2,1,0:T(8,128)(2,1)S(1)} async-done(((bf16[128,16,432]{2,1,0:T(8,128)(2,1)}), bf16[128,16,432]{2,1,0:T(8,128)(2,1)S(1)}, u32[]{:S(2)}, u32[]{:S(2)}) %all-to-all-start.1) | async-done | bytes 1769504 | tf_op jit(solution)/shard_map/all_to_all | solution.py:135
  282.9 7.3 %all-to-all-start.2 = ((bf16[128,16,486]{2,1,0:T(8,128)(2,1)}), bf16[128,16,486]{2,1,0:T(8,128)(2,1)S(1)}, u32[]{:S(2)}, u32[]{:S(2)}) async-start(bf16[128,16,486]{2,1,0:T(8,128)(2,1)} %gather_fusion.1), calls=%async_computation.2 | async-start | bytes 4194304 | tf_op jit(solution)/shard_map/all_to_all | solution.py:110
  291.8 7.4 %reshape.280 = bf16[768,2,576]{2,1,0:T(2,128)(2,1)} reshape(bf16[128,16,432]{2,1,0:T(8,128)(2,1)} %copy-done.1) | data formatting | bytes 3538944 | tf_op jit(solution)/shard_map/reshape | solution.py:136
  299.2 3.6 %gather_fusion = bf16[256,2,576]{2,1,0:T(2,128)(2,1)S(1)} fusion(bf16[768,2,576]{2,1,0:T(2,128)(2,1)} %reshape.280, s32[1024]{0:T(1024)S(1)} %pad_clamp_fusion.1), kind=kCustom, calls=%fused_computation | custom fusion | bytes 1180672 | tf_op jit(solution)/shard_map/gather | solution.py:138
  303.7 2.9 collective-permute-start.2
  308.5 34.5 %all-to-all-done.2 = bf16[128,16,486]{2,1,0:T(8,128)(2,1)S(1)} async-done(((bf16[128,16,486]{2,1,0:T(8,128)(2,1)}), bf16[128,16,486]{2,1,0:T(8,128)(2,1)S(1)}, u32[]{:S(2)}, u32[]{:S(2)}) %all-to-all-start.2) | async-done | bytes 1990688 | tf_op jit(solution)/shard_map/all_to_all | solution.py:110
  343.1 6.0 %reshape.283 = bf16[1,432,2304]{2,1,0:T(8,128)(2,1)} reshape(bf16[128,16,486]{2,1,0:T(8,128)(2,1)S(1)} %all-to-all-done.2) | data formatting | bytes 3981312 | tf_op jit(solution)/shard_map/reshape | solution.py:188
  (75 shorter events, 21.5 us)
Async XLA Ops:
  0.6 290.6 %copy-start = (bf16[256,576]{0,1:T(8,128)(2,1)S(1)}, bf16[256,576]{0,1:T(8,128)(2,1)}, u32[]{:S(2)}) copy-start(bf16[256,576]{0,1:T(8,128)(2,1)} %param.16) | copy-start | bytes 884740
  155.3 1.5 slice-start
  158.9 9.0 %collective-permute-start = (bf16[128,6,1152]{0,2,1:T(8,128)(2,1)}, bf16[128,6,1152]{0,2,1:T(8,128)(2,1)S(1)}, u32[]{:S(2)}, u32[]{:S(2)}) collective-permute-start(bf16[128,6,1152]{0,2,1:T(8,128)(2,1)} %bitcast.69), channel_id=1, source_target_pairs={{0,1},{1,0},{2,3},{3,2},{4,5},{5,4},{6,7},{7,6},{8,9},{9,8},{10,11... | collective-permute-start | bytes 5308424 | tf_op jit(solution)/shard_map/ppermute | solution.py:115
  178.3 6.7 %copy-start.2 = (bf16[1,2304,432]{1,2,0:T(8,128)(2,1)S(1)}, bf16[1,2304,432]{1,2,0:T(8,128)(2,1)}, u32[]{:S(2)}) copy-start(bf16[1,2304,432]{1,2,0:T(8,128)(2,1)} %param.25) | copy-start | bytes 5971972
  199.8 5.8 %collective-permute-start.1 = (bf16[768,2,576]{0,2,1:T(8,128)(2,1)}, bf16[768,2,576]{0,2,1:T(8,128)(2,1)S(1)}, u32[]{:S(2)}, u32[]{:S(2)}) collective-permute-start(bf16[768,2,576]{0,2,1:T(8,128)(2,1)} %dynamic-slice_bitcast_fusion), channel_id=1, source_target_pairs={{0,1},{1,0},{2,3},{3,2},{4,5},{5,4},{6,7},{7,6},{8,9},{9,8},{10,11... | collective-permute-start | bytes 5308424 | tf_op jit(solution)/shard_map/ppermute | solution.py:132
  219.7 8.2 %copy-start.9 = (s32[128]{0:T(128)S(1)}, s32[128]{0:T(128)}, u32[]{:S(2)}) copy-start(s32[128]{0:T(128)} %param.24) | copy-start | bytes 1540
  219.7 62.0 %all-to-all-start.1 = ((bf16[128,16,432]{2,1,0:T(8,128)(2,1)}), bf16[128,16,432]{2,1,0:T(8,128)(2,1)S(1)}, u32[]{:S(2)}, u32[]{:S(2)}) async-start(bf16[128,16,432]{2,1,0:T(8,128)(2,1)} %reshape.279), calls=%async_computation.1 | async-start | bytes 4194304 | tf_op jit(solution)/shard_map/all_to_all | solution.py:135
  231.6 58.8 %copy-start.7 = (f32[2,8,2]{1,2,0:T(2,128)S(1)}, f32[2,8,2]{1,2,0:T(2,128)}, u32[]{:S(2)}) copy-start(f32[2,8,2]{1,2,0:T(2,128)} %param.22) | copy-start | bytes 388
  231.6 58.9 %copy-start.8 = (s32[1,16]{1,0:T(1,128)S(1)}, s32[1,16]{1,0:T(1,128)}, u32[]{:S(2)}) copy-start(s32[1,16]{1,0:T(1,128)} %param.18) | copy-start | bytes 196
  231.6 59.1 %copy-start.5 = (bf16[2,8,576]{2,1,0:T(8,128)(2,1)S(1)}, bf16[2,8,576]{2,1,0:T(8,128)(2,1)}, u32[]{:S(2)}) copy-start(bf16[2,8,576]{2,1,0:T(8,128)(2,1)} %param.13) | copy-start | bytes 55300
  231.6 59.2 %copy-start.6 = (bf16[2,8,576]{2,1,0:T(8,128)(2,1)S(1)}, bf16[2,8,576]{2,1,0:T(8,128)(2,1)}, u32[]{:S(2)}) copy-start(bf16[2,8,576]{2,1,0:T(8,128)(2,1)} %param.14) | copy-start | bytes 55300
  231.6 59.9 %copy-start.4 = (bf16[2,8,576]{2,1,0:T(8,128)(2,1)S(1)}, bf16[2,8,576]{2,1,0:T(8,128)(2,1)}, u32[]{:S(2)}) copy-start(bf16[2,8,576]{2,1,0:T(8,128)(2,1)} %param.15) | copy-start | bytes 55300
  281.6 1.3 copy-start.1
  282.9 60.1 %all-to-all-start.2 = ((bf16[128,16,486]{2,1,0:T(8,128)(2,1)}), bf16[128,16,486]{2,1,0:T(8,128)(2,1)S(1)}, u32[]{:S(2)}, u32[]{:S(2)}) async-start(bf16[128,16,486]{2,1,0:T(8,128)(2,1)} %gather_fusion.1), calls=%async_computation.2 | async-start | bytes 4194304 | tf_op jit(solution)/shard_map/all_to_all | solution.py:110
  299.2 8.6 %copy-start.3 = (bf16[2,8,2304]{2,1,0:T(8,128)(2,1)S(1)}, bf16[2,8,2304]{2,1,0:T(8,128)(2,1)}, u32[]{:S(2)}) copy-start(bf16[2,8,2304]{2,1,0:T(8,128)(2,1)} %param.19) | copy-start | bytes 221188
  303.7 45.4 %collective-permute-start.2 = (f32[16,576]{1,0:T(8,128)S(1)}, f32[16,576]{1,0:T(8,128)S(1)}, u32[]{:S(2)}, u32[]{:S(2)}) collective-permute-start(f32[16,576]{1,0:T(8,128)S(1)} %dynamic-slice_bitcast_fusion.1), channel_id=1, source_target_pairs={{0,2},{2,0},{1,3},{3,1},{4,6},{6,4},{5,7},{7,5},{8,10},{10,8},{9,1... | collective-permute-start | bytes 110600 | tf_op jit(solution)/shard_map/ppermute | solution.py:146

commit v11 on v9

--- a/solution.py
+++ b/solution.py
@@ -121,15 +121,11 @@
     send = lax.dynamic_index_in_dim(part, 1 - core, 2, keepdims=False)
     got = lax.ppermute(send, "tp", CORE_PAIRS)
     pair_sum = (keep.astype(jnp.float32) + got.astype(jnp.float32)).astype(jnp.bfloat16)
-    piece_rows, piece_lanes = extra.shape[1:]
-    pair_sum = pair_sum.reshape(nreq, slots * half)
-    pair_sum = jnp.pad(pair_sum, ((0, 0), (0, piece_rows * piece_lanes - slots * half)))
-    pair_sum = pair_sum.reshape(nreq, piece_rows, piece_lanes)
-    both = lax.all_to_all(
-        jnp.concatenate([extra, pair_sum], axis=1), "req", split_axis=0, concat_axis=0, tiled=True
-    )
-    collected = both[:, :piece_rows]
-    returned = both[:, piece_rows:].reshape(nreq, piece_rows * piece_lanes)[:, : slots * half]
+    spread, needed = extra
+    pair_sum = pair_sum.reshape(nreq, 16, slots * half // 16)
+    returned = lax.all_to_all(pair_sum, "req", split_axis=0, concat_axis=0, tiled=True)
+    returned, spread = lax.optimization_barrier((returned, spread))
+    collected = lax.all_to_all(spread[needed], "req", split_axis=0, concat_axis=0, tiled=True)
     returned = returned.reshape(nreq * slots, 2, quarter)
     picked = (
         returned[slot.reshape(-1)]
@@ -160,7 +156,7 @@
     needed = jnp.sum(
         jnp.where(new_place[:, None] == shard_ids[None, :], first_old[None, :], 0), axis=1
     )
-    return spread[needed]
+    return spread, needed
 
 
 def on_device(

time: 337 us -> 313 us (0.929)
  waiting for transfers between devices: 113 us -> 90.6 us
  starting transfers between devices: 24.7 us -> 39.9 us
  local copies, waits for them, and re-layouts: 87.7 us -> 76.9 us
  other arithmetic: 20.2 us -> 15.8 us
    all_to_all x1 -> x2, waiting for transfers between devices: 94.9 us -> 61.4 us  [the longest x1 53.7 us: expert_routed(): lax.all_to_all(pair_sum, 'req', split_axis=0, concat_axis=0, tiled=True)]
    ppermute x1, waiting for transfers between devices: 0.01 us -> 25.5 us  [expert_routed(): total = mine + lax.ppermute(away, 'tp', Z_PAIRS)]
    all_to_all x1, waiting for transfers between devices: 18 us -> 0.01 us  [migrate(): lax.all_to_all(pieces, 'req', split_axis=0, concat_axis=0, tiled=True)]
    all_to_all x1 -> x2, starting transfers between devices: 7.75 us -> 23.3 us  [the longest x1 15.6 us: expert_routed(): lax.all_to_all(pair_sum, 'req', split_axis=0, concat_axis=0, tiled=True)]
    reshape x3 -> x1, local copies, waits for them, and re-layouts: 13.9 us -> 6.77 us  [expert_routed(): pair_sum = pair_sum.reshape(nreq, 16, slots * half // 16)]
    slice x2 -> x0, local copies, waits for them, and re-layouts: 6.82 us -> none  [the longest x1 4.02 us: expert_routed(): collected = both[:, :piece_rows]]
    concatenate x1 -> x0, other arithmetic: 4.43 us -> none  [expert_routed(): jnp.concatenate([extra, pair_sum], axis=1)]
    ppermute x1, waiting for transfers between devices: 0.01 us -> 3.78 us  [expert_routed(): got = lax.ppermute(send, 'tp', CORE_PAIRS)]
  transfers between devices with their start and end apart: 5 -> 6, of which waited for: 2 -> 4; matrix products, arithmetic and copies ran while one was open for 15% -> 23% of each run, Pallas kernels for 0% -> 0%
where the time goes in v11:
time: 313 us; the launch traced here: 310 us
  waiting for transfers between devices  90.6 us (29%)
  local copies, waits for them, and re-layouts  76.9 us (25%)
  blocking collectives  74.3 us (24%)
  starting transfers between devices  39.9 us (13%)
  other arithmetic  15.8 us (5%)
  matrix products  11.2 us (4%)
    all_to_all x1, blocking collectives, expert_routed(): lax.all_to_all(outgoing, 'req', split_axis=0, concat_axis=0, tiled=True)  74.3 us
    all_to_all x1, waiting for transfers between devices, expert_routed(): lax.all_to_all(pair_sum, 'req', split_axis=0, concat_axis=0, tiled=True)  53.7 us
    ppermute x1, waiting for transfers between devices, expert_routed(): total = mine + lax.ppermute(away, 'tp', Z_PAIRS)  25.5 us
    all_to_all x1, starting transfers between devices, expert_routed(): lax.all_to_all(pair_sum, 'req', split_axis=0, concat_axis=0, tiled=True)  15.6 us
    all_to_all x1, waiting for transfers between devices, expert_routed(): lax.all_to_all(spread[needed], 'req', split_axis=0, concat_axis=0, tiled=...  7.71 us
    all_to_all x1, starting transfers between devices, expert_routed(): lax.all_to_all(spread[needed], 'req', split_axis=0, concat_axis=0, tiled=...  7.7 us
    reshape x1, local copies, waits for them, and re-layouts, expert_routed(): returned = returned.reshape(nreq * slots, 2, quarter)  7.39 us
    reshape x1, local copies, waits for them, and re-layouts, expert_routed(): pair_sum = pair_sum.reshape(nreq, 16, slots * half // 16)  6.77 us
  transfers between devices with their start and end apart: 6, of which 4 were waited for; matrix products, arithmetic and copies ran while one was open for 23% of the time, Pallas kernels for 0%

profile of v11, /device:TPU:1, one launch (start us, length us, event | category | flops | bytes accessed | tf_op | source)
XLA Modules:
  0.0 309.8 jit_solution(11161807563814294372)
XLA Ops:
  7.6 1.9 convolution_convert_fusion.1
  9.5 6.0 %reshape.266 = bf16[128,16,432]{2,1,0:T(8,128)(2,1)S(1)} reshape(bf16[768,1152]{1,0:T(8,128)(2,1)} %convolution_convert_fusion.1) | data formatting | bytes 3538944 | tf_op jit(solution)/shard_map/reshape | solution.py:102
  15.6 74.3 %all_to_all.20 = bf16[128,16,432]{2,1,0:T(8,128)(2,1)} all-to-all(bf16[128,16,432]{2,1,0:T(8,128)(2,1)S(1)} %reshape.266), channel_id=1, replica_groups=mesh['req'=128,'tp'=4] {'req'}, dimensions={0} | all-to-all | bytes 3538944 | tf_op jit(solution)/shard_map/all_to_all | solution.py:103
  89.9 4.6 %copy.35 = bf16[128,16,432]{0,2,1:T(8,128)(2,1)} copy(bf16[128,16,432]{2,1,0:T(8,128)(2,1)} %all_to_all.20) | data formatting | bytes 3538944 | tf_op jit(solution)/shard_map/all_to_all | solution.py:103
  94.5 4.5 %collective-permute-start = (bf16[128,6,1152]{0,2,1:T(8,128)(2,1)}, bf16[128,6,1152]{0,2,1:T(8,128)(2,1)}, u32[]{:S(2)}, u32[]{:S(2)}) collective-permute-start(bf16[128,6,1152]{0,2,1:T(8,128)(2,1)} %bitcast.12), channel_id=1, source_target_pairs={{0,1},{1,0},{2,3},{3,2},{4,5},{5,4},{6,7},{7,6},{8,9},{9,8},{10,11... | collective-permute-start | bytes 5308424 | tf_op jit(solution)/shard_map/ppermute | solution.py:105
  99.0 5.9 %reshape.271 = bf16[128,16,486]{2,1,0:T(8,128)(2,1)} reshape(bf16[1,432,2304]{2,1,0:T(8,128)(2,1)S(1)} %bitcast.69) | data formatting | bytes 3981312 | tf_op jit(solution)/shard_map/reshape | solution.py:149
  104.9 6.4 %all-to-all-start.2 = ((bf16[128,16,486]{2,1,0:T(8,128)(2,1)}), bf16[128,16,486]{2,1,0:T(8,128)(2,1)S(1)}, u32[]{:S(2)}, u32[]{:S(2)}) async-start(bf16[128,16,486]{2,1,0:T(8,128)(2,1)} %reshape.271), calls=%async_computation.2 | async-start | bytes 4194304 | tf_op jit(solution)/shard_map/all_to_all | solution.py:150
  111.3 2.2 broadcast_select_fusion.1
  113.6 2.0 pad_maximum_fusion
  115.6 6.7 %copy.36 = bf16[128,6,2304]{2,1,0:T(8,128)(2,1)} copy(bf16[128,6,2304]{0,2,1:T(8,128)(2,1)} %pad_maximum_fusion) | data formatting | bytes 7077888 | tf_op jit(solution)/shard_map/concatenate | solution.py:108
  122.3 6.6 %reshape.268 = bf16[768,2304]{1,0:T(8,128)(2,1)} reshape(bf16[128,6,2304]{2,1,0:T(8,128)(2,1)} %copy.36) | data formatting | bytes 7077888 | tf_op jit(solution)/shard_map/reshape | solution.py:108
  128.9 3.6 %fusion.1 = f32[768,288]{0,1:T(8,128)S(1)} fusion(bf16[768,2304]{1,0:T(8,128)(2,1)} %reshape.268, bf16[2304,432]{0,1:T(8,128)(2,1)} %bitcast.67), kind=kOutput, calls=%fused_computation.10 | convolution fusion | flops 1019215872 | bytes 5750784 | tf_op jit(solution)/shard_map/dot_general | solution.py:109
  132.5 4.1 %convolution_convert_fusion = bf16[768,2304]{1,0:T(8,128)(2,1)} fusion(bf16[2304,432]{0,1:T(8,128)(2,1)} %bitcast.68, f32[768,288]{0,1:T(8,128)S(1)} %fusion.1), kind=kOutput, calls=%fused_computation.2 | convolution fusion | flops 512040960 | bytes 5087232 | tf_op jit(solution)/shard_map/dot_general | solution.py:113
  136.6 5.7 %copy.37 = bf16[768,2304]{0,1:T(8,128)(2,1)} copy(bf16[768,2304]{1,0:T(8,128)(2,1)} %convolution_convert_fusion) | data formatting | bytes 7077888 | tf_op jit(solution)/shard_map/convert_element_type | solution.py:118
  142.3 2.8 dynamic-slice_bitcast_fusion
  145.1 2.1 collective-permute-start.1
  147.3 3.8 %collective-permute-done.1 = bf16[768,2,576]{0,2,1:T(8,128)(2,1)} collective-permute-done((bf16[768,2,576]{0,2,1:T(8,128)(2,1)}, bf16[768,2,576]{0,2,1:T(8,128)(2,1)}, u32[]{:S(2)}, u32[]{:S(2)}) %collective-permute-start.1) | collective-permute-done | bytes 1769504 | tf_op jit(solution)/shard_map/ppermute | solution.py:122
  151.0 3.7 %fusion = bf16[768,2,576]{0,2,1:T(8,128)(2,1)} fusion(bf16[768,2,576]{0,2,1:T(8,128)(2,1)} %collective-permute-done.1, bf16[768,2,2,576]{0,3,2,1:T(8,128)(2,1)} %bitcast.66, s32[]{:T(128)S(6)} %select_n.110), kind=kLoop, calls=%fused_computation.5 | loop fusion | flops 3538944 | bytes 5308420 | tf_op jit(solution)/shard_map/convert_element_type | solution.py:123
  154.7 6.5 %copy.38 = bf16[768,2,576]{2,1,0:T(2,128)(2,1)} copy(bf16[768,2,576]{0,2,1:T(8,128)(2,1)} %fusion) | data formatting | bytes 3538944 | tf_op jit(solution)/shard_map/convert_element_type | solution.py:123
  161.3 6.8 %reshape.270 = bf16[128,16,432]{2,1,0:T(8,128)(2,1)} reshape(bf16[768,2,576]{2,1,0:T(2,128)(2,1)} %copy.38) | data formatting | bytes 3538944 | tf_op jit(solution)/shard_map/reshape | solution.py:125
  168.1 1.3 copy-done.2
  169.4 15.6 %all-to-all-start.1 = ((bf16[128,16,432]{2,1,0:T(8,128)(2,1)}), bf16[128,16,432]{2,1,0:T(8,128)(2,1)S(1)}, u32[]{:S(2)}, u32[]{:S(2)}) async-start(bf16[128,16,432]{2,1,0:T(8,128)(2,1)} %reshape.270), calls=%async_computation.1 | async-start | bytes 4194304 | tf_op jit(solution)/shard_map/all_to_all | solution.py:126
  185.1 53.7 %all-to-all-done.1 = bf16[128,16,432]{2,1,0:T(8,128)(2,1)S(1)} async-done(((bf16[128,16,432]{2,1,0:T(8,128)(2,1)}), bf16[128,16,432]{2,1,0:T(8,128)(2,1)S(1)}, u32[]{:S(2)}, u32[]{:S(2)}) %all-to-all-start.1) | async-done | bytes 1769504 | tf_op jit(solution)/shard_map/all_to_all | solution.py:126
  238.8 4.4 %gather_fusion.1 = bf16[128,16,486]{2,1,0:T(8,128)(2,1)} fusion(bf16[128,16,486]{2,1,0:T(8,128)(2,1)} %copy-done.2, s32[1024]{0:T(1024)S(1)} %pad_clamp_fusion), kind=kCustom, calls=%fused_computation.1 | custom fusion | bytes 3981824 | tf_op jit(solution)/shard_map/gather | solution.py:128
  243.2 7.7 %all-to-all-start.3 = ((bf16[128,16,486]{2,1,0:T(8,128)(2,1)}), bf16[128,16,486]{2,1,0:T(8,128)(2,1)S(1)}, u32[]{:S(2)}, u32[]{:S(2)}) async-start(bf16[128,16,486]{2,1,0:T(8,128)(2,1)} %gather_fusion.1), calls=%async_computation.3 | async-start | bytes 4194304 | tf_op jit(solution)/shard_map/all_to_all | solution.py:128
  252.4 7.4 %reshape.272 = bf16[768,2,576]{2,1,0:T(2,128)(2,1)} reshape(bf16[128,16,432]{2,1,0:T(8,128)(2,1)} %copy-done.1) | data formatting | bytes 3538944 | tf_op jit(solution)/shard_map/reshape | solution.py:129
  259.8 3.6 %gather_fusion = bf16[256,2,576]{2,1,0:T(2,128)(2,1)S(1)} fusion(bf16[768,2,576]{2,1,0:T(2,128)(2,1)} %reshape.272, s32[1024]{0:T(1024)S(1)} %pad_clamp_fusion.1), kind=kCustom, calls=%fused_computation | custom fusion | bytes 1180672 | tf_op jit(solution)/shard_map/gather | solution.py:131
  264.3 3.6 %collective-permute-start.2 = (f32[16,576]{1,0:T(8,128)S(1)}, f32[16,576]{1,0:T(8,128)S(1)}, u32[]{:S(2)}, u32[]{:S(2)}) collective-permute-start(f32[16,576]{1,0:T(8,128)S(1)} %dynamic-slice_bitcast_fusion.1), channel_id=1, source_target_pairs={{0,2},{2,0},{1,3},{3,1},{4,6},{6,4},{5,7},{7,5},{8,10},{10,8},{9,1... | collective-permute-start | bytes 110600 | tf_op jit(solution)/shard_map/ppermute | solution.py:139
  267.9 1.2 fusion.6
  269.9 25.5 %collective-permute-done.2 = f32[16,576]{1,0:T(8,128)S(1)} collective-permute-done((f32[16,576]{1,0:T(8,128)S(1)}, f32[16,576]{1,0:T(8,128)S(1)}, u32[]{:S(2)}, u32[]{:S(2)}) %collective-permute-start.2) | collective-permute-done | bytes 36896 | tf_op jit(solution)/shard_map/ppermute | solution.py:139
  296.1 7.7 %all-to-all-done.3 = bf16[128,16,486]{2,1,0:T(8,128)(2,1)S(1)} async-done(((bf16[128,16,486]{2,1,0:T(8,128)(2,1)}), bf16[128,16,486]{2,1,0:T(8,128)(2,1)S(1)}, u32[]{:S(2)}, u32[]{:S(2)}) %all-to-all-start.3) | async-done | bytes 1990688 | tf_op jit(solution)/shard_map/all_to_all | solution.py:128
  303.8 6.0 %reshape.275 = bf16[1,432,2304]{2,1,0:T(8,128)(2,1)} reshape(bf16[128,16,486]{2,1,0:T(8,128)(2,1)S(1)} %all-to-all-done.3) | data formatting | bytes 3981312 | tf_op jit(solution)/shard_map/reshape | solution.py:182
  (70 shorter events, 10.7 us)
Async XLA Ops:
  0.6 251.2 %copy-start = (bf16[256,576]{0,1:T(8,128)(2,1)S(1)}, bf16[256,576]{0,1:T(8,128)(2,1)}, u32[]{:S(2)}) copy-start(bf16[256,576]{0,1:T(8,128)(2,1)} %param.16) | copy-start | bytes 884740
  89.9 9.2 %copy-start.3 = (bf16[1,2304,432]{1,2,0:T(8,128)(2,1)S(1)}, bf16[1,2304,432]{1,2,0:T(8,128)(2,1)}, u32[]{:S(2)}) copy-start(bf16[1,2304,432]{1,2,0:T(8,128)(2,1)} %param.25) | copy-start | bytes 5971972
  94.5 16.8 %collective-permute-start = (bf16[128,6,1152]{0,2,1:T(8,128)(2,1)}, bf16[128,6,1152]{0,2,1:T(8,128)(2,1)}, u32[]{:S(2)}, u32[]{:S(2)}) collective-permute-start(bf16[128,6,1152]{0,2,1:T(8,128)(2,1)} %bitcast.12), channel_id=1, source_target_pairs={{0,1},{1,0},{2,3},{3,2},{4,5},{5,4},{6,7},{7,6},{8,9},{9,8},{10,11... | collective-permute-start | bytes 5308424 | tf_op jit(solution)/shard_map/ppermute | solution.py:105
  104.9 63.1 %all-to-all-start.2 = ((bf16[128,16,486]{2,1,0:T(8,128)(2,1)}), bf16[128,16,486]{2,1,0:T(8,128)(2,1)S(1)}, u32[]{:S(2)}, u32[]{:S(2)}) async-start(bf16[128,16,486]{2,1,0:T(8,128)(2,1)} %reshape.271), calls=%async_computation.2 | async-start | bytes 4194304 | tf_op jit(solution)/shard_map/all_to_all | solution.py:150
  145.1 5.9 %collective-permute-start.1 = (bf16[768,2,576]{0,2,1:T(8,128)(2,1)}, bf16[768,2,576]{0,2,1:T(8,128)(2,1)}, u32[]{:S(2)}, u32[]{:S(2)}) collective-permute-start(bf16[768,2,576]{0,2,1:T(8,128)(2,1)} %dynamic-slice_bitcast_fusion), channel_id=1, source_target_pairs={{0,1},{1,0},{2,3},{3,2},{4,5},{5,4},{6,7},{7,6},{8,9},{9,8},{10,11... | collective-permute-start | bytes 5308424 | tf_op jit(solution)/shard_map/ppermute | solution.py:122
  168.0 17.0 %copy-start.10 = (s32[128]{0:T(128)S(1)}, s32[128]{0:T(128)}, u32[]{:S(2)}) copy-start(s32[128]{0:T(128)} %param.24) | copy-start | bytes 1540
  168.0 1.4 copy-start.2
  169.4 69.4 %all-to-all-start.1 = ((bf16[128,16,432]{2,1,0:T(8,128)(2,1)}), bf16[128,16,432]{2,1,0:T(8,128)(2,1)S(1)}, u32[]{:S(2)}, u32[]{:S(2)}) async-start(bf16[128,16,432]{2,1,0:T(8,128)(2,1)} %reshape.270), calls=%async_computation.1 | async-start | bytes 4194304 | tf_op jit(solution)/shard_map/all_to_all | solution.py:126
  238.8 4.4 %copy-start.1 = (bf16[128,16,432]{2,1,0:T(8,128)(2,1)}, bf16[128,16,432]{2,1,0:T(8,128)(2,1)S(1)}, u32[]{:S(2)}) copy-start(bf16[128,16,432]{2,1,0:T(8,128)(2,1)S(1)} %all-to-all-done.1) | copy-start | bytes 5308420
  243.2 7.8 %copy-start.8 = (f32[2,8,2]{1,2,0:T(2,128)S(1)}, f32[2,8,2]{1,2,0:T(2,128)}, u32[]{:S(2)}) copy-start(f32[2,8,2]{1,2,0:T(2,128)} %param.22) | copy-start | bytes 388
  243.2 7.9 %copy-start.9 = (s32[1,16]{1,0:T(1,128)S(1)}, s32[1,16]{1,0:T(1,128)}, u32[]{:S(2)}) copy-start(s32[1,16]{1,0:T(1,128)} %param.18) | copy-start | bytes 196
  243.2 8.2 %copy-start.6 = (bf16[2,8,576]{2,1,0:T(8,128)(2,1)S(1)}, bf16[2,8,576]{2,1,0:T(8,128)(2,1)}, u32[]{:S(2)}) copy-start(bf16[2,8,576]{2,1,0:T(8,128)(2,1)} %param.13) | copy-start | bytes 55300
  243.2 8.3 %copy-start.7 = (bf16[2,8,576]{2,1,0:T(8,128)(2,1)S(1)}, bf16[2,8,576]{2,1,0:T(8,128)(2,1)}, u32[]{:S(2)}) copy-start(bf16[2,8,576]{2,1,0:T(8,128)(2,1)} %param.14) | copy-start | bytes 55300
  243.2 8.9 %copy-start.5 = (bf16[2,8,576]{2,1,0:T(8,128)(2,1)S(1)}, bf16[2,8,576]{2,1,0:T(8,128)(2,1)}, u32[]{:S(2)}) copy-start(bf16[2,8,576]{2,1,0:T(8,128)(2,1)} %param.15) | copy-start | bytes 55300
  243.2 60.6 %all-to-all-start.3 = ((bf16[128,16,486]{2,1,0:T(8,128)(2,1)}), bf16[128,16,486]{2,1,0:T(8,128)(2,1)S(1)}, u32[]{:S(2)}, u32[]{:S(2)}) async-start(bf16[128,16,486]{2,1,0:T(8,128)(2,1)} %gather_fusion.1), calls=%async_computation.3 | async-start | bytes 4194304 | tf_op jit(solution)/shard_map/all_to_all | solution.py:128
  259.8 9.3 %copy-start.4 = (bf16[2,8,2304]{2,1,0:T(8,128)(2,1)S(1)}, bf16[2,8,2304]{2,1,0:T(8,128)(2,1)}, u32[]{:S(2)}) copy-start(bf16[2,8,2304]{2,1,0:T(8,128)(2,1)} %param.19) | copy-start | bytes 221188
  264.3 31.1 %collective-permute-start.2 = (f32[16,576]{1,0:T(8,128)S(1)}, f32[16,576]{1,0:T(8,128)S(1)}, u32[]{:S(2)}, u32[]{:S(2)}) collective-permute-start(f32[16,576]{1,0:T(8,128)S(1)} %dynamic-slice_bitcast_fusion.1), channel_id=1, source_target_pairs={{0,2},{2,0},{1,3},{3,1},{4,6},{6,4},{5,7},{7,5},{8,10},{10,8},{9,1... | collective-permute-start | bytes 110600 | tf_op jit(solution)/shard_map/ppermute | solution.py:139

commit v12 on v11

--- a/solution.py
+++ b/solution.py
@@ -122,7 +122,7 @@
     got = lax.ppermute(send, "tp", CORE_PAIRS)
     pair_sum = (keep.astype(jnp.float32) + got.astype(jnp.float32)).astype(jnp.bfloat16)
     spread, needed = extra
-    pair_sum = pair_sum.reshape(nreq, 16, slots * half // 16)
+    pair_sum = pair_sum.reshape(nreq, slots, half)
     returned = lax.all_to_all(pair_sum, "req", split_axis=0, concat_axis=0, tiled=True)
     returned, spread = lax.optimization_barrier((returned, spread))
     collected = lax.all_to_all(spread[needed], "req", split_axis=0, concat_axis=0, tiled=True)

time: 313 us -> 318 us (1.016)
  waiting for transfers between devices: 90.6 us -> 100 us
  local copies, waits for them, and re-layouts: 76.9 us -> 71.9 us
    all_to_all x1, waiting for transfers between devices: 53.7 us -> 59.1 us  [expert_routed(): lax.all_to_all(pair_sum, 'req', split_axis=0, concat_axis=0, tiled=True)]
    ppermute x1, waiting for transfers between devices: 25.5 us -> 29.8 us  [expert_routed(): total = mine + lax.ppermute(away, 'tp', Z_PAIRS)]
    reshape x1, local copies, waits for them, and re-layouts: 7.39 us -> 3.19 us  [expert_routed(): returned = returned.reshape(nreq * slots, 2, quarter)]
  transfers between devices with their start and end apart: 6 -> 6, of which waited for: 4 -> 4; matrix products, arithmetic and copies ran while one was open for 23% -> 21% of each run, Pallas kernels for 0% -> 0%
where the time goes in v12:
time: 318 us; the launch traced here: 314 us
  waiting for transfers between devices  100 us (31%)
  blocking collectives  74.3 us (23%)
  local copies, waits for them, and re-layouts  71.9 us (23%)
  starting transfers between devices  40.5 us (13%)
  other arithmetic  15.8 us (5%)
  matrix products  10.3 us (3%)
    all_to_all x1, blocking collectives, expert_routed(): lax.all_to_all(outgoing, 'req', split_axis=0, concat_axis=0, tiled=True)  74.3 us
    all_to_all x1, waiting for transfers between devices, expert_routed(): lax.all_to_all(pair_sum, 'req', split_axis=0, concat_axis=0, tiled=True)  59.1 us
    ppermute x1, waiting for transfers between devices, expert_routed(): total = mine + lax.ppermute(away, 'tp', Z_PAIRS)  29.8 us
    all_to_all x1, starting transfers between devices, expert_routed(): lax.all_to_all(pair_sum, 'req', split_axis=0, concat_axis=0, tiled=True)  15.6 us
    all_to_all x1, starting transfers between devices, expert_routed(): lax.all_to_all(spread[needed], 'req', split_axis=0, concat_axis=0, tiled=...  8.44 us
    all_to_all x1, waiting for transfers between devices, expert_routed(): lax.all_to_all(spread[needed], 'req', split_axis=0, concat_axis=0, tiled=...  7.77 us
    reshape x1, local copies, waits for them, and re-layouts, on_device(): moved = collected.reshape(1, old_weights.shape[2], old_weights.shape[1])  7.09 us
    concatenate x1, local copies, waits for them, and re-layouts, expert_routed(): jnp.concatenate([low, high], axis=-1).reshape(nreq * slots, width)  6.73 us
  transfers between devices with their start and end apart: 6, of which 4 were waited for; matrix products, arithmetic and copies ran while one was open for 21% of the time, Pallas kernels for 0%

profile of v12, /device:TPU:1, one launch (start us, length us, event | category | flops | bytes accessed | tf_op | source)
XLA Modules:
  0.0 314.3 jit_solution(12502029482726857590)
XLA Ops:
  5.5 1.0 multiply_reduce_fusion
  7.6 1.9 convolution_convert_fusion.1
  9.5 6.0 %reshape.266 = bf16[128,16,432]{2,1,0:T(8,128)(2,1)S(1)} reshape(bf16[768,1152]{1,0:T(8,128)(2,1)} %convolution_convert_fusion.1) | data formatting | bytes 3538944 | tf_op jit(solution)/shard_map/reshape | solution.py:102
  15.6 74.3 %all_to_all.20 = bf16[128,16,432]{2,1,0:T(8,128)(2,1)} all-to-all(bf16[128,16,432]{2,1,0:T(8,128)(2,1)S(1)} %reshape.266), channel_id=1, replica_groups=mesh['req'=128,'tp'=4] {'req'}, dimensions={0} | all-to-all | bytes 3538944 | tf_op jit(solution)/shard_map/all_to_all | solution.py:103
  89.9 4.6 %copy.35 = bf16[128,16,432]{0,2,1:T(8,128)(2,1)} copy(bf16[128,16,432]{2,1,0:T(8,128)(2,1)} %all_to_all.20) | data formatting | bytes 3538944 | tf_op jit(solution)/shard_map/all_to_all | solution.py:103
  94.5 4.5 %collective-permute-start = (bf16[128,6,1152]{0,2,1:T(8,128)(2,1)}, bf16[128,6,1152]{0,2,1:T(8,128)(2,1)}, u32[]{:S(2)}, u32[]{:S(2)}) collective-permute-start(bf16[128,6,1152]{0,2,1:T(8,128)(2,1)} %bitcast.12), channel_id=1, source_target_pairs={{0,1},{1,0},{2,3},{3,2},{4,5},{5,4},{6,7},{7,6},{8,9},{9,8},{10,11... | collective-permute-start | bytes 5308424 | tf_op jit(solution)/shard_map/ppermute | solution.py:105
  99.0 5.9 %reshape.271 = bf16[128,16,486]{2,1,0:T(8,128)(2,1)} reshape(bf16[1,432,2304]{2,1,0:T(8,128)(2,1)S(1)} %bitcast.69) | data formatting | bytes 3981312 | tf_op jit(solution)/shard_map/reshape | solution.py:149
  104.9 6.4 %all-to-all-start.2 = ((bf16[128,16,486]{2,1,0:T(8,128)(2,1)}), bf16[128,16,486]{2,1,0:T(8,128)(2,1)S(1)}, u32[]{:S(2)}, u32[]{:S(2)}) async-start(bf16[128,16,486]{2,1,0:T(8,128)(2,1)} %reshape.271), calls=%async_computation.2 | async-start | bytes 4194304 | tf_op jit(solution)/shard_map/all_to_all | solution.py:150
  111.3 2.2 broadcast_select_fusion.1
  113.6 2.0 pad_maximum_fusion
  115.6 6.7 %copy.36 = bf16[128,6,2304]{2,1,0:T(8,128)(2,1)} copy(bf16[128,6,2304]{0,2,1:T(8,128)(2,1)} %pad_maximum_fusion) | data formatting | bytes 7077888 | tf_op jit(solution)/shard_map/concatenate | solution.py:108
  122.3 6.6 %reshape.268 = bf16[768,2304]{1,0:T(8,128)(2,1)} reshape(bf16[128,6,2304]{2,1,0:T(8,128)(2,1)} %copy.36) | data formatting | bytes 7077888 | tf_op jit(solution)/shard_map/reshape | solution.py:108
  128.9 3.6 %fusion.1 = f32[768,288]{0,1:T(8,128)S(1)} fusion(bf16[768,2304]{1,0:T(8,128)(2,1)} %reshape.268, bf16[2304,432]{0,1:T(8,128)(2,1)} %bitcast.67), kind=kOutput, calls=%fused_computation.10 | convolution fusion | flops 1019215872 | bytes 5750784 | tf_op jit(solution)/shard_map/dot_general | solution.py:109
  132.5 4.1 %convolution_convert_fusion = bf16[768,2304]{1,0:T(8,128)(2,1)} fusion(bf16[2304,432]{0,1:T(8,128)(2,1)} %bitcast.68, f32[768,288]{0,1:T(8,128)S(1)} %fusion.1), kind=kOutput, calls=%fused_computation.2 | convolution fusion | flops 512040960 | bytes 5087232 | tf_op jit(solution)/shard_map/dot_general | solution.py:113
  136.6 5.7 %copy.37 = bf16[768,2304]{0,1:T(8,128)(2,1)} copy(bf16[768,2304]{1,0:T(8,128)(2,1)} %convolution_convert_fusion) | data formatting | bytes 7077888 | tf_op jit(solution)/shard_map/convert_element_type | solution.py:118
  142.3 2.8 dynamic-slice_bitcast_fusion
  145.1 2.1 collective-permute-start.1
  147.3 3.8 %collective-permute-done.1 = bf16[768,2,576]{0,2,1:T(8,128)(2,1)} collective-permute-done((bf16[768,2,576]{0,2,1:T(8,128)(2,1)}, bf16[768,2,576]{0,2,1:T(8,128)(2,1)}, u32[]{:S(2)}, u32[]{:S(2)}) %collective-permute-start.1) | collective-permute-done | bytes 1769504 | tf_op jit(solution)/shard_map/ppermute | solution.py:122
  151.0 3.7 %fusion = bf16[768,2,576]{0,2,1:T(8,128)(2,1)} fusion(bf16[768,2,576]{0,2,1:T(8,128)(2,1)} %collective-permute-done.1, bf16[768,2,2,576]{0,3,2,1:T(8,128)(2,1)} %bitcast.66, s32[]{:T(128)S(6)} %select_n.110), kind=kLoop, calls=%fused_computation.5 | loop fusion | flops 3538944 | bytes 5308420 | tf_op jit(solution)/shard_map/convert_element_type | solution.py:123
  154.7 6.5 %copy.38 = bf16[768,2,576]{2,1,0:T(2,128)(2,1)} copy(bf16[768,2,576]{0,2,1:T(8,128)(2,1)} %fusion) | data formatting | bytes 3538944 | tf_op jit(solution)/shard_map/convert_element_type | solution.py:123
  161.3 5.7 %reshape.270 = bf16[128,6,1152]{2,1,0:T(8,128)(2,1)} reshape(bf16[768,2,576]{2,1,0:T(2,128)(2,1)} %copy.38) | data formatting | bytes 3538944 | tf_op jit(solution)/shard_map/reshape | solution.py:125
  167.0 1.3 copy-done.1
  168.3 15.6 %all-to-all-start.1 = ((bf16[128,6,1152]{2,1,0:T(8,128)(2,1)}), bf16[128,6,1152]{2,1,0:T(8,128)(2,1)S(1)}, u32[]{:S(2)}, u32[]{:S(2)}) async-start(bf16[128,6,1152]{2,1,0:T(8,128)(2,1)} %reshape.270), calls=%async_computation.1 | async-start | bytes 4718592 | tf_op jit(solution)/shard_map/all_to_all | solution.py:126
  184.0 59.1 %all-to-all-done.1 = bf16[128,6,1152]{2,1,0:T(8,128)(2,1)S(1)} async-done(((bf16[128,6,1152]{2,1,0:T(8,128)(2,1)}), bf16[128,6,1152]{2,1,0:T(8,128)(2,1)S(1)}, u32[]{:S(2)}, u32[]{:S(2)}) %all-to-all-start.1) | async-done | bytes 1769504 | tf_op jit(solution)/shard_map/all_to_all | solution.py:126
  243.1 3.6 %gather_fusion.1 = bf16[128,16,486]{2,1,0:T(8,128)(2,1)} fusion(bf16[128,16,486]{2,1,0:T(8,128)(2,1)} %copy-done.1, s32[1024]{0:T(1024)S(1)} %pad_clamp_fusion), kind=kCustom, calls=%fused_computation.1 | custom fusion | bytes 3981824 | tf_op jit(solution)/shard_map/gather | solution.py:128
  246.8 8.4 %all-to-all-start.3 = ((bf16[128,16,486]{2,1,0:T(8,128)(2,1)}), bf16[128,16,486]{2,1,0:T(8,128)(2,1)}, u32[]{:S(2)}, u32[]{:S(2)}) async-start(bf16[128,16,486]{2,1,0:T(8,128)(2,1)} %gather_fusion.1), calls=%async_computation.3 | async-start | bytes 4194304 | tf_op jit(solution)/shard_map/all_to_all | solution.py:128
  256.8 3.2 %reshape.272 = bf16[768,2,576]{2,1,0:T(2,128)(2,1)} reshape(bf16[128,6,1152]{2,1,0:T(8,128)(2,1)S(1)} %all-to-all-done.1) | data formatting | bytes 3538944 | tf_op jit(solution)/shard_map/reshape | solution.py:129
  260.0 3.6 %gather_fusion = bf16[256,2,576]{2,1,0:T(2,128)(2,1)S(1)} fusion(bf16[768,2,576]{2,1,0:T(2,128)(2,1)} %reshape.272, s32[1024]{0:T(1024)S(1)} %pad_clamp_fusion.1), kind=kCustom, calls=%fused_computation | custom fusion | bytes 1180672 | tf_op jit(solution)/shard_map/gather | solution.py:131
  264.5 3.4 %collective-permute-start.2 = (f32[16,576]{1,0:T(8,128)S(1)}, f32[16,576]{1,0:T(8,128)S(1)}, u32[]{:S(2)}, u32[]{:S(2)}) collective-permute-start(f32[16,576]{1,0:T(8,128)S(1)} %dynamic-slice_bitcast_fusion.1), channel_id=1, source_target_pairs={{0,2},{2,0},{1,3},{3,1},{4,6},{6,4},{5,7},{7,5},{8,10},{10,8},{9,1... | collective-permute-start | bytes 110600 | tf_op jit(solution)/shard_map/ppermute | solution.py:139
  268.9 29.8 %collective-permute-done.2 = f32[16,576]{1,0:T(8,128)S(1)} collective-permute-done((f32[16,576]{1,0:T(8,128)S(1)}, f32[16,576]{1,0:T(8,128)S(1)}, u32[]{:S(2)}, u32[]{:S(2)}) %collective-permute-start.2) | collective-permute-done | bytes 36896 | tf_op jit(solution)/shard_map/ppermute | solution.py:139
  299.4 7.8 %all-to-all-done.3 = bf16[128,16,486]{2,1,0:T(8,128)(2,1)} async-done(((bf16[128,16,486]{2,1,0:T(8,128)(2,1)}), bf16[128,16,486]{2,1,0:T(8,128)(2,1)}, u32[]{:S(2)}, u32[]{:S(2)}) %all-to-all-start.3) | async-done | bytes 1990688 | tf_op jit(solution)/shard_map/all_to_all | solution.py:128
  307.2 7.1 %reshape.275 = bf16[1,432,2304]{2,1,0:T(8,128)(2,1)} reshape(bf16[128,16,486]{2,1,0:T(8,128)(2,1)} %all-to-all-done.3) | data formatting | bytes 3981312 | tf_op jit(solution)/shard_map/reshape | solution.py:182
  (70 shorter events, 10.0 us)
Async XLA Ops:
  0.6 255.6 %copy-start = (bf16[256,576]{0,1:T(8,128)(2,1)S(1)}, bf16[256,576]{0,1:T(8,128)(2,1)}, u32[]{:S(2)}) copy-start(bf16[256,576]{0,1:T(8,128)(2,1)} %param.16) | copy-start | bytes 884740
  89.9 9.2 %copy-start.2 = (bf16[1,2304,432]{1,2,0:T(8,128)(2,1)S(1)}, bf16[1,2304,432]{1,2,0:T(8,128)(2,1)}, u32[]{:S(2)}) copy-start(bf16[1,2304,432]{1,2,0:T(8,128)(2,1)} %param.25) | copy-start | bytes 5971972
  94.5 16.8 %collective-permute-start = (bf16[128,6,1152]{0,2,1:T(8,128)(2,1)}, bf16[128,6,1152]{0,2,1:T(8,128)(2,1)}, u32[]{:S(2)}, u32[]{:S(2)}) collective-permute-start(bf16[128,6,1152]{0,2,1:T(8,128)(2,1)} %bitcast.12), channel_id=1, source_target_pairs={{0,1},{1,0},{2,3},{3,2},{4,5},{5,4},{6,7},{7,6},{8,9},{9,8},{10,11... | collective-permute-start | bytes 5308424 | tf_op jit(solution)/shard_map/ppermute | solution.py:105
  104.9 62.1 %all-to-all-start.2 = ((bf16[128,16,486]{2,1,0:T(8,128)(2,1)}), bf16[128,16,486]{2,1,0:T(8,128)(2,1)S(1)}, u32[]{:S(2)}, u32[]{:S(2)}) async-start(bf16[128,16,486]{2,1,0:T(8,128)(2,1)} %reshape.271), calls=%async_computation.2 | async-start | bytes 4194304 | tf_op jit(solution)/shard_map/all_to_all | solution.py:150
  145.1 5.9 %collective-permute-start.1 = (bf16[768,2,576]{0,2,1:T(8,128)(2,1)}, bf16[768,2,576]{0,2,1:T(8,128)(2,1)}, u32[]{:S(2)}, u32[]{:S(2)}) collective-permute-start(bf16[768,2,576]{0,2,1:T(8,128)(2,1)} %dynamic-slice_bitcast_fusion), channel_id=1, source_target_pairs={{0,1},{1,0},{2,3},{3,2},{4,5},{5,4},{6,7},{7,6},{8,9},{9,8},{10,11... | collective-permute-start | bytes 5308424 | tf_op jit(solution)/shard_map/ppermute | solution.py:122
  167.0 16.9 %copy-start.10 = (s32[128]{0:T(128)S(1)}, s32[128]{0:T(128)}, u32[]{:S(2)}) copy-start(s32[128]{0:T(128)} %param.24) | copy-start | bytes 1540
  167.0 1.3 copy-start.1
  168.3 74.9 %all-to-all-start.1 = ((bf16[128,6,1152]{2,1,0:T(8,128)(2,1)}), bf16[128,6,1152]{2,1,0:T(8,128)(2,1)S(1)}, u32[]{:S(2)}, u32[]{:S(2)}) async-start(bf16[128,6,1152]{2,1,0:T(8,128)(2,1)} %reshape.270), calls=%async_computation.1 | async-start | bytes 4718592 | tf_op jit(solution)/shard_map/all_to_all | solution.py:126
  246.8 8.6 %copy-start.7 = (f32[2,8,2]{1,2,0:T(2,128)S(1)}, f32[2,8,2]{1,2,0:T(2,128)}, u32[]{:S(2)}) copy-start(f32[2,8,2]{1,2,0:T(2,128)} %param.22) | copy-start | bytes 388
  246.8 8.7 %copy-start.8 = (s32[1,16]{1,0:T(1,128)S(1)}, s32[1,16]{1,0:T(1,128)}, u32[]{:S(2)}) copy-start(s32[1,16]{1,0:T(1,128)} %param.18) | copy-start | bytes 196
  246.8 8.9 %copy-start.5 = (bf16[2,8,576]{2,1,0:T(8,128)(2,1)S(1)}, bf16[2,8,576]{2,1,0:T(8,128)(2,1)}, u32[]{:S(2)}) copy-start(bf16[2,8,576]{2,1,0:T(8,128)(2,1)} %param.13) | copy-start | bytes 55300
  246.8 9.0 %copy-start.6 = (bf16[2,8,576]{2,1,0:T(8,128)(2,1)S(1)}, bf16[2,8,576]{2,1,0:T(8,128)(2,1)}, u32[]{:S(2)}) copy-start(bf16[2,8,576]{2,1,0:T(8,128)(2,1)} %param.14) | copy-start | bytes 55300
  246.8 9.7 %copy-start.4 = (bf16[2,8,576]{2,1,0:T(8,128)(2,1)S(1)}, bf16[2,8,576]{2,1,0:T(8,128)(2,1)}, u32[]{:S(2)}) copy-start(bf16[2,8,576]{2,1,0:T(8,128)(2,1)} %param.15) | copy-start | bytes 55300
  246.8 60.4 %all-to-all-start.3 = ((bf16[128,16,486]{2,1,0:T(8,128)(2,1)}), bf16[128,16,486]{2,1,0:T(8,128)(2,1)}, u32[]{:S(2)}, u32[]{:S(2)}) async-start(bf16[128,16,486]{2,1,0:T(8,128)(2,1)} %gather_fusion.1), calls=%async_computation.3 | async-start | bytes 4194304 | tf_op jit(solution)/shard_map/all_to_all | solution.py:128
  260.0 7.9 %copy-start.9 = (bf16[256,576]{0,1:T(8,128)(2,1)S(1)}, bf16[256,576]{0,1:T(8,128)(2,1)}, u32[]{:S(2)}) copy-start(bf16[256,576]{0,1:T(8,128)(2,1)} %param.17) | copy-start | bytes 884740
  260.0 8.2 %copy-start.3 = (bf16[2,8,2304]{2,1,0:T(8,128)(2,1)S(1)}, bf16[2,8,2304]{2,1,0:T(8,128)(2,1)}, u32[]{:S(2)}) copy-start(bf16[2,8,2304]{2,1,0:T(8,128)(2,1)} %param.19) | copy-start | bytes 221188
  264.5 34.2 %collective-permute-start.2 = (f32[16,576]{1,0:T(8,128)S(1)}, f32[16,576]{1,0:T(8,128)S(1)}, u32[]{:S(2)}, u32[]{:S(2)}) collective-permute-start(f32[16,576]{1,0:T(8,128)S(1)} %dynamic-slice_bitcast_fusion.1), channel_id=1, source_target_pairs={{0,2},{2,0},{1,3},{3,1},{4,6},{6,4},{5,7},{7,5},{8,10},{10,8},{9,1... | collective-permute-start | bytes 110600 | tf_op jit(solution)/shard_map/ppermute | solution.py:139
